TPU v7x, 32 devices: a whole 2x2x4 slice. The times are simulated.
32 devices in a mesh: gx: 4 (over y, x), gy: 4 (over z), gz: 2 (over core).
Axes of the slice: x: 2, y: 2, z: 4, core: 2. Of those that a mesh axis runs over, the one named last changes fastest.
Arguments:
- right_side: float32 [16, 256, 512], P('gz', 'gx', 'gy'), may hold values from -6 to 6
- permeability: float32 [16, 256, 512], P('gz', 'gx', 'gy'), may hold values from 0.05 to 50
- storage: float32 [16, 256, 512], P('gz', 'gx', 'gy'), may hold values from 0.05 to 0.5
- deflation: float32 [8, 16, 256, 512], P(None, 'gz', 'gx', 'gy'), may hold values from -0.0234375 to 0.0234375
- coarse_inverse: float32 [256, 256], P('gx'), as said below
- owners: int32 [2, 4, 4, 8], P('gz', 'gx', 'gy'), may hold values from 0 to 255, as said below
- margin: int32 [2, 4, 4, 6], P('gz', 'gx', 'gy'), may hold values from 0 to 1
Outputs:
- solution: float32 [16, 256, 512], P('gz', 'gx', 'gy')
- residual: float32 [16, 256, 512], P('gz', 'gx', 'gy')
Inputs may be any that keep to these rules, and one draw needn't show every extreme that they name: `coarse_inverse`: symmetric and positive definite. `owners`: every coarse index appears exactly once.
All inputs are finite; a program needn't handle non-finite values.
Results may differ from a plain program's by a relative error of at most 0.0003.
Values sent between devices are 32-bit elements; how exact they have to be, the bound alone decides.
No kernel may reach another device: no remote copies, remote signals or barrier semaphores. Data moves between devices by JAX's collectives and lax.ppermute only.
A program may use at most 128 MiB of HBM per device.

v0:
```python
import jax
import jax.numpy as jnp
from jax import lax
from jax.sharding import PartitionSpec as P

ITERS = 4


RELAXATION = 0.7
PRECISE = lax.Precision.HIGHEST


def padded_2(cells, sides, width):
    for axis, dim in sides:
        count = lax.axis_size(axis)
        ends = count - 1
        head = lax.slice_in_dim(cells, 0, width, axis=dim)
        tail = lax.slice_in_dim(cells, cells.shape[dim] - width, cells.shape[dim], axis=dim)
        cells = jnp.concatenate(
            [
                lax.ppermute(tail, axis, [(i, (i + 1) % count) for i in range(ends)]),
                cells,
                lax.ppermute(head, axis, [((i + 1) % count, i) for i in range(ends)]),
            ],
            axis=dim,
        )
    return cells


def conduct(first_perm, second_perm):
    return 2.0 * first_perm * second_perm / jnp.maximum(first_perm + second_perm, 0.05)


def neighbour(padded, dimension, offset):
    starts = [1, 1, 1]
    starts[dimension] = 1 + offset
    limits = [
        starts[0] + padded.shape[0] - 2,
        starts[1] + padded.shape[1] - 2,
        starts[2] + padded.shape[2] - 2,
    ]
    return lax.slice(padded, starts, limits)


def diagonal_of(perm_pad, storage_in):
    perm_center = neighbour(perm_pad, 0, 0)
    diagonal = storage_in
    for dimension in range(3):
        for offset in (-1, 1):
            diagonal = diagonal + conduct(perm_center, neighbour(perm_pad, dimension, offset))
    return diagonal


def stencil(padded, perm_pad, storage_in):
    center = neighbour(padded, 0, 0)
    perm_center = neighbour(perm_pad, 0, 0)
    applied = storage_in * center
    for dimension in range(3):
        for offset in (-1, 1):
            transmit = conduct(perm_center, neighbour(perm_pad, dimension, offset))
            applied = applied + transmit * (center - neighbour(padded, dimension, offset))
    return applied


def line_mask(length, low_side, high_side, position, blocks):
    places = jnp.arange(length + 2, dtype=jnp.int32)
    inside = (places >= 1 - low_side) & (places <= length + high_side)
    ingrid = ((places >= 1) | (position > 0)) & ((places <= length) | (position < blocks - 1))
    return (inside & ingrid).astype(jnp.float32)


def local_solve(residual_ext, perm_pad, storage_ext, keep_mask, inverse):
    source = keep_mask * residual_ext
    solved = RELAXATION * inverse * source
    applied = stencil(jnp.pad(solved, 1), perm_pad, storage_ext)
    solved = solved + RELAXATION * inverse * (source - applied)
    return solved[1:-1, 1:-1, 1:-1]


def local(right_side, permeability, storage, deflation, coarse_inverse, owners, margin):
    widened = padded_2(jnp.stack((permeability, storage)), (("gx", 2), ("gy", 3), ("gz", 1)), 2)
    perm_wide = widened[0]
    perm_near = perm_wide[1:-1, 1:-1, 1:-1]
    storage_ext = widened[1][1:-1, 1:-1, 1:-1]
    local_z, local_x, local_y = right_side.shape
    depths = margin.reshape(6)
    keep_mask = (
        line_mask(local_z, depths[0], depths[1], lax.axis_index("gz"), lax.axis_size("gz"))[
            :, None, None
        ]
        * line_mask(local_x, depths[2], depths[3], lax.axis_index("gx"), lax.axis_size("gx"))[
            None, :, None
        ]
        * line_mask(local_y, depths[4], depths[5], lax.axis_index("gy"), lax.axis_size("gy"))[
            None, None, :
        ]
    )
    diagonal = diagonal_of(perm_wide, storage_ext)
    inverse = keep_mask / jnp.where(keep_mask > 0, diagonal, 1.0)
    flat_vectors = deflation.reshape(deflation.shape[0], -1)
    order_total = coarse_inverse.shape[1]
    owner_list = owners.reshape(-1)
    picker = (owner_list[:, None] == jnp.arange(order_total, dtype=jnp.int32)[None, :]).astype(
        jnp.float32
    )

    def coarse_terms(field):
        coefficients = jnp.dot(flat_vectors, field.reshape(-1), precision=PRECISE)
        return jnp.dot(coefficients, picker, precision=PRECISE)

    def coarse_field(vector):
        solved_part = jnp.dot(coarse_inverse, vector, precision=PRECISE)
        solved = lax.all_gather(solved_part, "gx", axis=0, tiled=True)
        picked = jnp.dot(picker, solved, precision=PRECISE)
        return jnp.dot(picked, flat_vectors, precision=PRECISE).reshape(right_side.shape)

    def residual_rim(residual):
        return padded_2(residual, (("gx", 1), ("gy", 2), ("gz", 0)), 1)

    def precondition(residual_ext, vector):
        return local_solve(residual_ext, perm_wide, storage_ext, keep_mask, inverse) + coarse_field(
            vector
        )

    def inner_of(residual, precond):
        return lax.psum(jnp.sum(residual * precond), ("gx", "gy", "gz"))

    solution = jnp.zeros(right_side.shape, jnp.float32)
    residual = right_side
    residual_ext = residual_rim(residual)
    vector = lax.psum(coarse_terms(residual), ("gx", "gy", "gz"))
    precond = precondition(residual_ext, vector)
    inner_prod = inner_of(residual, precond)
    direction = precond
    for iteration in range(ITERS):
        padded = padded_2(direction, (("gx", 1), ("gy", 2), ("gz", 0)), 1)
        applied = stencil(padded, perm_near, storage)
        curvature, coarse_image = lax.psum(
            (jnp.sum(direction * applied), coarse_terms(applied)), ("gx", "gy", "gz")
        )
        step_size = inner_prod / curvature
        solution = solution + step_size * direction
        residual = residual - step_size * applied
        if iteration + 1 < ITERS:
            residual_ext = residual_rim(residual)
            vector = vector - step_size * coarse_image
            precond = precondition(residual_ext, vector)
            fresh_prod = inner_of(residual, precond)
            direction = precond + fresh_prod / inner_prod * direction
            inner_prod = fresh_prod
    return (solution, residual)


def solution(mesh):
    in_specs = (
        P("gz", "gx", "gy"),
        P("gz", "gx", "gy"),
        P("gz", "gx", "gy"),
        P(None, "gz", "gx", "gy"),
        P("gx", None),
        P("gz", "gx", "gy", None),
        P("gz", "gx", "gy", None),
    )
    out_specs = (P("gz", "gx", "gy"), P("gz", "gx", "gy"))
    return jax.shard_map(local, mesh=mesh, in_specs=in_specs, out_specs=out_specs, check_vma=False)
```

profile of v0, /device:TPU:0, one launch (start us, length us, event | category | flops | bytes accessed | tf_op | source)
XLA Modules:
  0.0 727.6 jit_solution(15111064473556556727)
XLA Ops:
  2.1 4.9 collective-permute-start
  8.3 4.5 collective-permute-start.6
  16.8 6.5 fusion.8
  23.5 42.0 %psum.84 = f32[256]{0:T(256)S(1)} all-reduce(f32[256]{0:T(256)S(1)} %bitcast.151), channel_id=1, replica_groups=mesh['gx'=4,'gy'=4,'gz'=2] {'gx','gy','gz'}, use_global_device_ids=true, to_apply=%region_0.1 | all-reduce | flops 256 | bytes 2048 | tf_op jit(solution)/shard_map/psum | solution.py:131
  67.2 11.1 %all-reduce.4 = f32[256]{0:T(256)S(1)} all-reduce(f32[256]{0:T(256)S(1)} %dynamic-update-slice), channel_id=1, replica_groups=mesh['gx'=4,'gy'=4,'gz'=2] {'gx'}, use_global_device_ids=true, to_apply=%add.4 | all-reduce | flops 256 | bytes 2048
  95.5 5.1 collective-permute-start.2
  123.9 6.1 fusion.144
  130.0 8.2 %multiply_add_fusion.3 = (f32[10,66,130]{2,0,1:T(8,128)}, f32[10,66,130]{2,0,1:T(8,128)}, f32[10,66,130]{2,0,1:T(8,128)}, f32[10,66,130]{2,0,1:T(8,128)}) fusion(f32[10,66,130]{2,0,1:T(8,128)} %get-tuple-element.38, f32[10,66,130]{2,0,1:T(8,128)} %get-tuple-element.34, f32[10,66,130]{2,0,1:T(8,128)} %get-tuple-element.37, ...), kind=kLoop, calls=%fused_computation.57 | loop fusion | flops 1115400 | bytes 3432000 | tf_op jit(solution)/shard_map/add | solution.py:61
  138.2 4.5 fusion.125
  145.4 4.8 collective-permute-done.13
  150.4 4.6 collective-permute-start.14
  156.2 4.7 collective-permute-done.14
  173.1 5.2 fusion.11
  178.5 39.4 %all-reduce.10 = (f32[]{:T(128)}, f32[]{:T(128)}, f32[256]{0:T(256)}) all-reduce(f32[]{:T(128)} %get-tuple-element.7, f32[]{:T(128)} %get-tuple-element.6, f32[256]{0:T(256)S(1)} %bitcast.150), channel_id=1, replica_groups=mesh['gx'=4,'gy'=4,'gz'=2] {'gx','gy','gz'}, use_global_device_ids=true, to_apply=%region_2.3 | all-reduce | flops 258 | bytes 2064 | tf_op jit(solution)/shard_map/psum | solution.py:126
  230.0 12.2 %all-reduce.5 = f32[256]{0:T(256)} all-reduce(f32[256]{0:T(256)} %dynamic-update-slice.1), channel_id=1, replica_groups=mesh['gx'=4,'gy'=4,'gz'=2] {'gx'}, use_global_device_ids=true, to_apply=%add.5 | all-reduce | flops 256 | bytes 2048
  261.4 7.9 %multiply_add_fusion.2 = (f32[10,66,130]{2,0,1:T(8,128)}, f32[10,66,130]{2,0,1:T(8,128)}, f32[10,66,130]{2,0,1:T(8,128)}, f32[10,66,130]{2,0,1:T(8,128)}) fusion(f32[10,66,130]{2,0,1:T(8,128)} %get-tuple-element.38, f32[10,66,130]{2,0,1:T(8,128)} %get-tuple-element.67, f32[10,66,130]{2,0,1:T(8,128)S(1)} %copy-done.8, f32[10,66,130]{2,0,1:T(8,128)S(1)} %copy-done.5, ...), kind=kLoop, calls=%fused_computation.49 | loop fusion | flops 1115400 | bytes 3432000 | tf_op jit(solution)/shard_map/add | solution.py:61
  269.3 5.9 multiply_reduce_fusion.5
  275.1 38.5 %psum.88 = f32[]{:T(128)} all-reduce(f32[]{:T(128)} %get-tuple-element.25), channel_id=1, replica_groups=mesh['gx'=4,'gy'=4,'gz'=2] {'gx','gy','gz'}, use_global_device_ids=true, to_apply=%region_7.8 | all-reduce | flops 1 | bytes 8 | tf_op jit(solution)/shard_map/psum | solution.py:126
  344.3 5.2 fusion.14
  350.3 39.3 %all-reduce.9 = (f32[]{:T(128)}, f32[256]{0:T(256)}) all-reduce(f32[]{:T(128)} %get-tuple-element.23, f32[256]{0:T(256)} %bitcast.161), channel_id=1, replica_groups=mesh['gx'=4,'gy'=4,'gz'=2] {'gx','gy','gz'}, use_global_device_ids=true, to_apply=%region_9.10 | all-reduce | flops 257 | bytes 2056 | tf_op jit(solution)/shard_map/psum | solution.py:138
  401.9 11.7 %all-reduce.6 = f32[256]{0:T(256)S(1)} all-reduce(f32[256]{0:T(256)} %dynamic-update-slice.2), channel_id=1, replica_groups=mesh['gx'=4,'gy'=4,'gz'=2] {'gx'}, use_global_device_ids=true, to_apply=%add.6 | all-reduce | flops 256 | bytes 2048
  434.4 7.9 %multiply_add_fusion.1 = (f32[10,66,130]{2,0,1:T(8,128)}, f32[10,66,130]{2,0,1:T(8,128)}, f32[10,66,130]{2,0,1:T(8,128)}, f32[10,66,130]{2,0,1:T(8,128)}) fusion(f32[10,66,130]{2,0,1:T(8,128)} %get-tuple-element.38, f32[10,66,130]{2,0,1:T(8,128)} %get-tuple-element.65, f32[10,66,130]{2,0,1:T(8,128)S(1)} %copy-done.9, f32[10,66,130]{2,0,1:T(8,128)S(1)} %copy-done.6, ...), kind=kLoop, calls=%fused_computation.41 | loop fusion | flops 1115400 | bytes 3432000 | tf_op jit(solution)/shard_map/add | solution.py:61
  442.3 5.9 multiply_reduce_fusion.3
  448.1 38.5 %psum.91 = f32[]{:T(128)} all-reduce(f32[]{:T(128)} %get-tuple-element.21), channel_id=1, replica_groups=mesh['gx'=4,'gy'=4,'gz'=2] {'gx','gy','gz'}, use_global_device_ids=true, to_apply=%region_12.13 | all-reduce | flops 1 | bytes 8 | tf_op jit(solution)/shard_map/psum | solution.py:126
  517.2 5.2 fusion.17
  523.2 39.3 %all-reduce.8 = (f32[]{:T(128)}, f32[256]{0:T(256)}) all-reduce(f32[]{:T(128)} %get-tuple-element.19, f32[256]{0:T(256)} %bitcast.162), channel_id=1, replica_groups=mesh['gx'=4,'gy'=4,'gz'=2] {'gx','gy','gz'}, use_global_device_ids=true, to_apply=%region_14.15 | all-reduce | flops 257 | bytes 2056 | tf_op jit(solution)/shard_map/psum | solution.py:138
  574.3 11.7 %all-reduce.7 = f32[256]{0:T(256)S(1)} all-reduce(f32[256]{0:T(256)} %dynamic-update-slice.3), channel_id=1, replica_groups=mesh['gx'=4,'gy'=4,'gz'=2] {'gx'}, use_global_device_ids=true, to_apply=%add.7 | all-reduce | flops 256 | bytes 2048
  607.1 4.5 multiply_add_fusion
  611.7 4.7 multiply_reduce_fusion.1
  616.4 38.4 %psum.94 = f32[]{:T(128)} all-reduce(f32[]{:T(128)} %get-tuple-element.17), channel_id=1, replica_groups=mesh['gx'=4,'gy'=4,'gz'=2] {'gx','gy','gz'}, use_global_device_ids=true, to_apply=%region_17.18 | all-reduce | flops 1 | bytes 8 | tf_op jit(solution)/shard_map/psum | solution.py:126
  673.5 4.4 collective-permute-done.51
  685.0 39.2 %psum.95 = f32[]{:T(128)} all-reduce(f32[]{:T(128)} %get-tuple-element.15), channel_id=1, replica_groups=mesh['gx'=4,'gy'=4,'gz'=2] {'gx','gy','gz'}, use_global_device_ids=true, to_apply=%region_19.20 | all-reduce | flops 1 | bytes 8 | tf_op jit(solution)/shard_map/psum | solution.py:138
  (340 shorter events, 239.3 us)
Async XLA Ops:
  2.1 91.0 %collective-permute-start = (f32[2,8,2,128]{3,1,2,0:T(8,128)S(1)}, f32[2,8,2,128]{3,1,2,0:T(8,128)S(1)}, u32[]{:S(2)}, u32[]{:S(2)}) collective-permute-start(f32[2,8,2,128]{3,1,2,0:T(8,128)S(1)} %get-tuple-element.86), channel_id=1, source_target_pairs={{0,8},{8,16},{16,24},{1,9},{9,17},{17,25},{2,10},{10,18},{18,26},{... | collective-permute-start | bytes 49160 | tf_op jit(solution)/shard_map/ppermute | solution.py:21
  6.9 86.1 %collective-permute-start.1 = (f32[2,8,2,128]{3,1,2,0:T(8,128)S(1)}, f32[2,8,2,128]{3,1,2,0:T(8,128)S(1)}, u32[]{:S(2)}, u32[]{:S(2)}) collective-permute-start(f32[2,8,2,128]{3,1,2,0:T(8,128)S(1)} %get-tuple-element.87), channel_id=1, source_target_pairs={{8,0},{16,8},{24,16},{9,1},{17,9},{25,17},{10,2},{18,10},{26,18},{... | collective-permute-start | bytes 49160 | tf_op jit(solution)/shard_map/ppermute | solution.py:23
  8.3 78.2 %collective-permute-start.6 = (f32[8,1,128]{2,0,1:T(8,128)S(1)}, f32[8,1,128]{2,0,1:T(8,128)S(1)}, u32[]{:S(2)}, u32[]{:S(2)}) collective-permute-start(f32[8,1,128]{2,0,1:T(8,128)S(1)} %copy.93), channel_id=1, source_target_pairs={{0,8},{8,16},{16,24},{1,9},{9,17},{17,25},{2,10},{10,18},{18,26},{... | collective-permute-start | bytes 12296 | tf_op jit(solution)/shard_map/ppermute | solution.py:21
  12.8 73.8 %collective-permute-start.7 = (f32[8,1,128]{2,0,1:T(8,128)S(1)}, f32[8,1,128]{2,0,1:T(8,128)S(1)}, u32[]{:S(2)}, u32[]{:S(2)}) collective-permute-start(f32[8,1,128]{2,0,1:T(8,128)S(1)} %copy.94), channel_id=1, source_target_pairs={{8,0},{16,8},{24,16},{9,1},{17,9},{25,17},{10,2},{18,10},{26,18},{... | collective-permute-start | bytes 12296 | tf_op jit(solution)/shard_map/ppermute | solution.py:23
  87.6 16.3 %collective-permute-start.8 = (f32[8,66,1]{2,0,1:T(8,128)}, f32[8,66,1]{2,0,1:T(8,128)}, u32[]{:S(2)}, u32[]{:S(2)}) collective-permute-start(f32[8,66,1]{2,0,1:T(8,128)} %get-tuple-element.102), channel_id=1, source_target_pairs={{0,2},{2,4},{4,6},{1,3},{3,5},{5,7},{8,10},{10,12},{12,14},{9,11},... | collective-permute-start | bytes 6344 | tf_op jit(solution)/shard_map/ppermute | solution.py:21
  91.7 12.2 %collective-permute-start.9 = (f32[8,66,1]{2,0,1:T(8,128)}, f32[8,66,1]{2,0,1:T(8,128)}, u32[]{:S(2)}, u32[]{:S(2)}) collective-permute-start(f32[8,66,1]{2,0,1:T(8,128)} %get-tuple-element.103), channel_id=1, source_target_pairs={{2,0},{4,2},{6,4},{3,1},{5,3},{7,5},{10,8},{12,10},{14,12},{11,9},... | collective-permute-start | bytes 6344 | tf_op jit(solution)/shard_map/ppermute | solution.py:23
  95.5 13.9 %collective-permute-start.2 = (f32[2,8,68,2]{2,1,3,0:T(8,128)S(1)}, f32[2,8,68,2]{2,1,3,0:T(8,128)}, u32[]{:S(2)}, u32[]{:S(2)}) collective-permute-start(f32[2,8,68,2]{2,1,3,0:T(8,128)S(1)} %copy.24), channel_id=1, source_target_pairs={{0,2},{2,4},{4,6},{1,3},{3,5},{5,7},{8,10},{10,12},{12,14},{9,11},... | collective-permute-start | bytes 26120 | tf_op jit(solution)/shard_map/ppermute | solution.py:21
  102.6 7.9 %collective-permute-start.3 = (f32[2,8,68,2]{2,1,3,0:T(8,128)}, f32[2,8,68,2]{2,1,3,0:T(8,128)}, u32[]{:S(2)}, u32[]{:S(2)}) collective-permute-start(f32[2,8,68,2]{2,1,3,0:T(8,128)} %copy.25), channel_id=1, source_target_pairs={{2,0},{4,2},{6,4},{3,1},{5,3},{7,5},{10,8},{12,10},{14,12},{11,9},... | collective-permute-start | bytes 26120 | tf_op jit(solution)/shard_map/ppermute | solution.py:23
  106.3 13.6 %collective-permute-start.10 = (f32[1,66,130]{2,0,1:T(1,128)}, f32[1,66,130]{2,0,1:T(1,128)}, u32[]{:S(2)}, u32[]{:S(2)}) collective-permute-start(f32[1,66,130]{2,0,1:T(1,128)} %get-tuple-element.82), channel_id=1, source_target_pairs={{0,1},{2,3},{4,5},{6,7},{8,9},{10,11},{12,13},{14,15},{16,17},{18,... | collective-permute-start | bytes 102968 | tf_op jit(solution)/shard_map/ppermute | solution.py:21
  108.2 11.7 %collective-permute-start.11 = (f32[1,66,130]{2,0,1:T(1,128)}, f32[1,66,130]{2,0,1:T(1,128)}, u32[]{:S(2)}, u32[]{:S(2)}) collective-permute-start(f32[1,66,130]{2,0,1:T(1,128)} %get-tuple-element.83), channel_id=1, source_target_pairs={{1,0},{3,2},{5,4},{7,6},{9,8},{11,10},{13,12},{15,14},{17,16},{19,... | collective-permute-start | bytes 102968 | tf_op jit(solution)/shard_map/ppermute | solution.py:23
  114.5 8.1 %collective-permute-start.4 = (f32[2,2,68,132]{3,1,2,0:T(2,128)S(1)}, f32[2,2,68,132]{3,1,2,0:T(2,128)S(1)}, u32[]{:S(2)}, u32[]{:S(2)}) collective-permute-start(f32[2,2,68,132]{3,1,2,0:T(2,128)S(1)} %get-tuple-element.44), channel_id=1, source_target_pairs={{0,1},{2,3},{4,5},{6,7},{8,9},{10,11},{12,13},{14,15},{16,17},{18,... | collective-permute-start | bytes 430856 | tf_op jit(solution)/shard_map/ppermute | solution.py:21
  144.0 6.1 collective-permute-start.13
  150.4 10.6 %collective-permute-start.14 = (f32[8,66,1]{2,0,1:T(8,128)S(1)}, f32[8,66,1]{2,0,1:T(8,128)S(1)}, u32[]{:S(2)}, u32[]{:S(2)}) collective-permute-start(f32[8,66,1]{2,0,1:T(8,128)S(1)} %get-tuple-element.100), channel_id=1, source_target_pairs={{0,2},{2,4},{4,6},{1,3},{3,5},{5,7},{8,10},{10,12},{12,14},{9,11},... | collective-permute-start | bytes 6344 | tf_op jit(solution)/shard_map/ppermute | solution.py:21
  154.9 10.1 %collective-permute-start.15 = (f32[8,66,1]{2,0,1:T(8,128)S(1)}, f32[8,66,1]{2,0,1:T(8,128)S(1)}, u32[]{:S(2)}, u32[]{:S(2)}) collective-permute-start(f32[8,66,1]{2,0,1:T(8,128)S(1)} %get-tuple-element.101), channel_id=1, source_target_pairs={{2,0},{4,2},{6,4},{3,1},{5,3},{7,5},{10,8},{12,10},{14,12},{11,9},... | collective-permute-start | bytes 6344 | tf_op jit(solution)/shard_map/ppermute | solution.py:23
  221.1 21.0 %collective-permute-start.18 = (f32[8,1,128]{2,0,1:T(8,128)}, f32[8,1,128]{2,0,1:T(8,128)S(1)}, u32[]{:S(2)}, u32[]{:S(2)}) collective-permute-start(f32[8,1,128]{2,0,1:T(8,128)} %get-tuple-element.114), channel_id=1, source_target_pairs={{0,8},{8,16},{16,24},{1,9},{9,17},{17,25},{2,10},{10,18},{18,26},{... | collective-permute-start | bytes 12296 | tf_op jit(solution)/shard_map/ppermute | solution.py:21
  225.3 16.8 %collective-permute-start.19 = (f32[8,1,128]{2,0,1:T(8,128)}, f32[8,1,128]{2,0,1:T(8,128)S(1)}, u32[]{:S(2)}, u32[]{:S(2)}) collective-permute-start(f32[8,1,128]{2,0,1:T(8,128)} %get-tuple-element.115), channel_id=1, source_target_pairs={{8,0},{16,8},{24,16},{9,1},{17,9},{25,17},{10,2},{18,10},{26,18},{... | collective-permute-start | bytes 12296 | tf_op jit(solution)/shard_map/ppermute | solution.py:23
  242.3 7.5 %collective-permute-start.20 = (f32[8,66,1]{2,0,1:T(8,128)S(1)}, f32[8,66,1]{2,0,1:T(8,128)S(1)}, u32[]{:S(2)}, u32[]{:S(2)}) collective-permute-start(f32[8,66,1]{2,0,1:T(8,128)S(1)} %get-tuple-element.98), channel_id=1, source_target_pairs={{0,2},{2,4},{4,6},{1,3},{3,5},{5,7},{8,10},{10,12},{12,14},{9,11},... | collective-permute-start | bytes 6344 | tf_op jit(solution)/shard_map/ppermute | solution.py:21
  245.9 8.4 %collective-permute-start.21 = (f32[8,66,1]{2,0,1:T(8,128)S(1)}, f32[8,66,1]{2,0,1:T(8,128)S(1)}, u32[]{:S(2)}, u32[]{:S(2)}) collective-permute-start(f32[8,66,1]{2,0,1:T(8,128)S(1)} %get-tuple-element.99), channel_id=1, source_target_pairs={{2,0},{4,2},{6,4},{3,1},{5,3},{7,5},{10,8},{12,10},{14,12},{11,9},... | collective-permute-start | bytes 6344 | tf_op jit(solution)/shard_map/ppermute | solution.py:23
  326.0 7.4 %collective-permute-start.26 = (f32[8,66,1]{2,0,1:T(8,128)S(1)}, f32[8,66,1]{2,0,1:T(8,128)S(1)}, u32[]{:S(2)}, u32[]{:S(2)}) collective-permute-start(f32[8,66,1]{2,0,1:T(8,128)S(1)} %get-tuple-element.96), channel_id=1, source_target_pairs={{0,2},{2,4},{4,6},{1,3},{3,5},{5,7},{8,10},{10,12},{12,14},{9,11},... | collective-permute-start | bytes 6344 | tf_op jit(solution)/shard_map/ppermute | solution.py:21
  329.4 8.4 %collective-permute-start.27 = (f32[8,66,1]{2,0,1:T(8,128)S(1)}, f32[8,66,1]{2,0,1:T(8,128)S(1)}, u32[]{:S(2)}, u32[]{:S(2)}) collective-permute-start(f32[8,66,1]{2,0,1:T(8,128)S(1)} %get-tuple-element.97), channel_id=1, source_target_pairs={{2,0},{4,2},{6,4},{3,1},{5,3},{7,5},{10,8},{12,10},{14,12},{11,9},... | collective-permute-start | bytes 6344 | tf_op jit(solution)/shard_map/ppermute | solution.py:23
  393.3 20.4 %collective-permute-start.30 = (f32[8,1,128]{2,0,1:T(8,128)}, f32[8,1,128]{2,0,1:T(8,128)S(1)}, u32[]{:S(2)}, u32[]{:S(2)}) collective-permute-start(f32[8,1,128]{2,0,1:T(8,128)} %get-tuple-element.110), channel_id=1, source_target_pairs={{0,8},{8,16},{16,24},{1,9},{9,17},{17,25},{2,10},{10,18},{18,26},{... | collective-permute-start | bytes 12296 | tf_op jit(solution)/shard_map/ppermute | solution.py:21
  397.4 16.3 %collective-permute-start.31 = (f32[8,1,128]{2,0,1:T(8,128)}, f32[8,1,128]{2,0,1:T(8,128)S(1)}, u32[]{:S(2)}, u32[]{:S(2)}) collective-permute-start(f32[8,1,128]{2,0,1:T(8,128)} %get-tuple-element.111), channel_id=1, source_target_pairs={{8,0},{16,8},{24,16},{9,1},{17,9},{25,17},{10,2},{18,10},{26,18},{... | collective-permute-start | bytes 12296 | tf_op jit(solution)/shard_map/ppermute | solution.py:23
  414.9 7.3 collective-permute-start.32
  418.2 8.4 %collective-permute-start.33 = (f32[8,66,1]{2,0,1:T(8,128)S(1)}, f32[8,66,1]{2,0,1:T(8,128)S(1)}, u32[]{:S(2)}, u32[]{:S(2)}) collective-permute-start(f32[8,66,1]{2,0,1:T(8,128)S(1)} %get-tuple-element.95), channel_id=1, source_target_pairs={{2,0},{4,2},{6,4},{3,1},{5,3},{7,5},{10,8},{12,10},{14,12},{11,9},... | collective-permute-start | bytes 6344 | tf_op jit(solution)/shard_map/ppermute | solution.py:23
  499.0 7.4 %collective-permute-start.38 = (f32[8,66,1]{2,0,1:T(8,128)S(1)}, f32[8,66,1]{2,0,1:T(8,128)S(1)}, u32[]{:S(2)}, u32[]{:S(2)}) collective-permute-start(f32[8,66,1]{2,0,1:T(8,128)S(1)} %get-tuple-element.92), channel_id=1, source_target_pairs={{0,2},{2,4},{4,6},{1,3},{3,5},{5,7},{8,10},{10,12},{12,14},{9,11},... | collective-permute-start | bytes 6344 | tf_op jit(solution)/shard_map/ppermute | solution.py:21
  502.4 8.4 %collective-permute-start.39 = (f32[8,66,1]{2,0,1:T(8,128)S(1)}, f32[8,66,1]{2,0,1:T(8,128)S(1)}, u32[]{:S(2)}, u32[]{:S(2)}) collective-permute-start(f32[8,66,1]{2,0,1:T(8,128)S(1)} %get-tuple-element.93), channel_id=1, source_target_pairs={{2,0},{4,2},{6,4},{3,1},{5,3},{7,5},{10,8},{12,10},{14,12},{11,9},... | collective-permute-start | bytes 6344 | tf_op jit(solution)/shard_map/ppermute | solution.py:23
  566.1 19.9 %collective-permute-start.42 = (f32[8,1,128]{2,0,1:T(8,128)}, f32[8,1,128]{2,0,1:T(8,128)S(1)}, u32[]{:S(2)}, u32[]{:S(2)}) collective-permute-start(f32[8,1,128]{2,0,1:T(8,128)} %get-tuple-element.106), channel_id=1, source_target_pairs={{0,8},{8,16},{16,24},{1,9},{9,17},{17,25},{2,10},{10,18},{18,26},{... | collective-permute-start | bytes 12296 | tf_op jit(solution)/shard_map/ppermute | solution.py:21
  570.2 15.8 %collective-permute-start.43 = (f32[8,1,128]{2,0,1:T(8,128)}, f32[8,1,128]{2,0,1:T(8,128)S(1)}, u32[]{:S(2)}, u32[]{:S(2)}) collective-permute-start(f32[8,1,128]{2,0,1:T(8,128)} %get-tuple-element.107), channel_id=1, source_target_pairs={{8,0},{16,8},{24,16},{9,1},{17,9},{25,17},{10,2},{18,10},{26,18},{... | collective-permute-start | bytes 12296 | tf_op jit(solution)/shard_map/ppermute | solution.py:23
  587.2 7.3 collective-permute-start.44
  590.5 8.4 %collective-permute-start.45 = (f32[8,66,1]{2,0,1:T(8,128)S(1)}, f32[8,66,1]{2,0,1:T(8,128)S(1)}, u32[]{:S(2)}, u32[]{:S(2)}) collective-permute-start(f32[8,66,1]{2,0,1:T(8,128)S(1)} %get-tuple-element.91), channel_id=1, source_target_pairs={{2,0},{4,2},{6,4},{3,1},{5,3},{7,5},{10,8},{12,10},{14,12},{11,9},... | collective-permute-start | bytes 6344 | tf_op jit(solution)/shard_map/ppermute | solution.py:23
  666.2 7.4 %collective-permute-start.50 = (f32[8,66,1]{2,0,1:T(8,128)S(1)}, f32[8,66,1]{2,0,1:T(8,128)S(1)}, u32[]{:S(2)}, u32[]{:S(2)}) collective-permute-start(f32[8,66,1]{2,0,1:T(8,128)S(1)} %get-tuple-element.88), channel_id=1, source_target_pairs={{0,2},{2,4},{4,6},{1,3},{3,5},{5,7},{8,10},{10,12},{12,14},{9,11},... | collective-permute-start | bytes 6344 | tf_op jit(solution)/shard_map/ppermute | solution.py:21
  669.6 8.4 %collective-permute-start.51 = (f32[8,66,1]{2,0,1:T(8,128)S(1)}, f32[8,66,1]{2,0,1:T(8,128)S(1)}, u32[]{:S(2)}, u32[]{:S(2)}) collective-permute-start(f32[8,66,1]{2,0,1:T(8,128)S(1)} %get-tuple-element.89), channel_id=1, source_target_pairs={{2,0},{4,2},{6,4},{3,1},{5,3},{7,5},{10,8},{12,10},{14,12},{11,9},... | collective-permute-start | bytes 6344 | tf_op jit(solution)/shard_map/ppermute | solution.py:23
  (92 other events, 1092.2 us)
where the time goes:
time: 739 us; the launch traced here: 728 us
  blocking collectives  361 us (49%)
  starting transfers between devices  121 us (16%)
  other arithmetic  90.9 us (12%)
  waiting for transfers between devices  73.3 us (10%)
  matrix products  37.2 us (5%)
  local copies, waits for them, and re-layouts  27.4 us (4%)
  between operations  16.1 us (2%)
    psum x4, blocking collectives, inner_of(): return lax.psum(jnp.sum(residual * precond), ('gx', 'gy', 'gz'))  155 us
    psum x3, blocking collectives, local(): lax.psum((jnp.sum(direction * applied), coarse_terms(applied)), ('gx', 'g...  118 us
    ppermute x27, starting transfers between devices, padded_2(): lax.ppermute(tail, axis, [(i, (i + 1) % count) for i in range(ends)])  85 us
    ppermute x27, waiting for transfers between devices, padded_2(): lax.ppermute(head, axis, [((i + 1) % count, i) for i in range(ends)])  55.2 us
    unnamed x4, blocking collectives  46.7 us
    psum x1, blocking collectives, local(): vector = lax.psum(coarse_terms(residual), ('gx', 'gy', 'gz'))  42 us
    ppermute x27, starting transfers between devices, padded_2(): lax.ppermute(head, axis, [((i + 1) % count, i) for i in range(ends)])  36.3 us
    add x4, other arithmetic, stencil(): applied + transmit * (center - neighbour(padded, dimension, offset))  28.6 us
  transfers between devices with their start and end apart: 54, of which 22 were waited for; matrix products, arithmetic and copies ran while one was open for 7% of the time, Pallas kernels for 0%

commit v1 on v0

v1 whole, which is shorter than its diff:
```python
import jax
import jax.numpy as jnp
from jax import lax
from jax.sharding import PartitionSpec as P

ITERS = 4
RELAXATION = 0.7
PRECISE = lax.Precision.HIGHEST
AXES = ("gx", "gy", "gz")
SIDES = (("gz", 0), ("gx", 1), ("gy", 2))


def conduct(first_perm, second_perm):
    return 2.0 * first_perm * second_perm / jnp.maximum(first_perm + second_perm, 0.05)


def faces(cells):
    out = []
    for axis, dim in SIDES:
        count = lax.axis_size(axis)
        head = lax.slice_in_dim(cells, 0, 1, axis=dim)
        tail = lax.slice_in_dim(cells, cells.shape[dim] - 1, cells.shape[dim], axis=dim)
        low = lax.ppermute(tail, axis, [(i, i + 1) for i in range(count - 1)])
        high = lax.ppermute(head, axis, [(i + 1, i) for i in range(count - 1)])
        out.append((low, high))
    return out


def extended(cells, halo, dim):
    return jnp.concatenate([halo[0], cells, halo[1]], axis=dim)


def couplings(cells, halos, transmit, scale=None):
    total = 0.0
    for dim in range(3):
        low, high = halos[dim]
        if scale is not None:
            low, high = low * scale[2 * dim], high * scale[2 * dim + 1]
        size = cells.shape[dim]
        padded = extended(cells, (low, high), dim)
        before = lax.slice_in_dim(padded, 0, size, axis=dim)
        after = lax.slice_in_dim(padded, 2, size + 2, axis=dim)
        t = transmit[dim]
        total = total + lax.slice_in_dim(t, 0, size, axis=dim) * before
        total = total + lax.slice_in_dim(t, 1, size + 1, axis=dim) * after
    return total


def everyone(row):
    count = 1
    for axis in AXES:
        count *= lax.axis_size(axis)
    copies = jnp.broadcast_to(row[None], (count,) + row.shape)
    return lax.all_to_all(copies, AXES, 0, 0, tiled=True)


def local(right_side, permeability, storage, deflation, coarse_inverse, owners, margin):
    vectors = deflation.shape[0]
    order = coarse_inverse.shape[1]
    depths = margin.reshape(6).astype(jnp.float32)
    sizes = [lax.axis_size(a) for a in AXES]
    me = (lax.axis_index("gx") * sizes[1] + lax.axis_index("gy")) * sizes[2] + lax.axis_index("gz")

    def coefficients(field):
        return jnp.sum(deflation * field[None], axis=(1, 2, 3))

    perm_faces = faces(permeability)
    transmit, diagonal = [], storage
    for dim in range(3):
        size = permeability.shape[dim]
        padded = extended(permeability, perm_faces[dim], dim)
        t = conduct(
            lax.slice_in_dim(padded, 0, size + 1, axis=dim),
            lax.slice_in_dim(padded, 1, size + 2, axis=dim),
        )
        transmit.append(t)
        diagonal = diagonal + lax.slice_in_dim(t, 0, size, axis=dim)
        diagonal = diagonal + lax.slice_in_dim(t, 1, size + 1, axis=dim)
    relax = RELAXATION / diagonal

    first = jnp.concatenate([coefficients(right_side), owners.reshape(-1).astype(jnp.float32)])
    table = everyone(first)
    known = table[:, :vectors].reshape(-1)
    owner_all = table[:, vectors:].reshape(-1)
    picker = (owner_all[:, None] == jnp.arange(order, dtype=jnp.float32)[None, :]).astype(jnp.float32)
    whole = lax.all_gather(coarse_inverse, "gx", axis=0, tiled=True)
    whole = jnp.dot(jnp.dot(picker, whole, precision=PRECISE), picker.T, precision=PRECISE)

    def precondition(residual, vector):
        scaled = relax * residual
        smooth = (2.0 - RELAXATION) * scaled + relax * couplings(scaled, faces(scaled), transmit, depths)
        solved = jnp.dot(whole, vector, precision=PRECISE)
        mine = lax.dynamic_slice(solved, (me * vectors,), (vectors,))
        return smooth + jnp.sum(deflation * mine[:, None, None, None], axis=0)

    def operate(field):
        return diagonal * field - couplings(field, faces(field), transmit)

    solution = jnp.zeros(right_side.shape, jnp.float32)
    residual = right_side
    direction = image = solution
    image_known = jnp.zeros_like(known)
    old_inner = jnp.float32(1.0)
    curvature = jnp.float32(0.0)
    for iteration in range(ITERS):
        precond = precondition(residual, known)
        applied = operate(precond)
        scalars = jnp.stack(
            [jnp.sum(residual * precond), jnp.sum(precond * applied), jnp.sum(precond * image)]
        )
        parts = everyone(jnp.concatenate([scalars, coefficients(applied)]))
        sums = jnp.sum(parts[:, :3], axis=0)
        inner = sums[0]
        ratio = inner / old_inner if iteration else jnp.float32(0.0)
        curvature = sums[1] + ratio * (2.0 * sums[2] + ratio * curvature)
        step = inner / curvature
        direction = precond + ratio * direction
        image = applied + ratio * image
        image_known = parts[:, 3:].reshape(-1) + ratio * image_known
        solution = solution + step * direction
        residual = residual - step * image
        known = known - step * image_known
        old_inner = inner
    return (solution, residual)


def solution(mesh):
    in_specs = (
        P("gz", "gx", "gy"),
        P("gz", "gx", "gy"),
        P("gz", "gx", "gy"),
        P(None, "gz", "gx", "gy"),
        P("gx", None),
        P("gz", "gx", "gy", None),
        P("gz", "gx", "gy", None),
    )
    out_specs = (P("gz", "gx", "gy"), P("gz", "gx", "gy"))
    return jax.shard_map(local, mesh=mesh, in_specs=in_specs, out_specs=out_specs, check_vma=False)
```

time: 739 us -> 314 us (0.42); the launches traced: 728 us -> 312 us
  blocking collectives: 361 us -> 44.6 us
  other arithmetic: 90.9 us -> 47.8 us
  waiting for transfers between devices: 73.3 us -> 31.7 us
  matrix products: 37.2 us -> 4.76 us
  starting transfers between devices: 121 us -> 150 us
  local copies, waits for them, and re-layouts: 27.4 us -> 18.7 us
    psum x8 -> x0, blocking collectives: 315 us -> none  [the longest x4 155 us: inner_of(): return lax.psum(jnp.sum(residual * precond), ('gx', 'gy', 'gz'))]
    ppermute x54, waiting for transfers between devices: 73.3 us -> 24.6 us  [the longest x27 17.5 us: faces(): low = lax.ppermute(tail, axis, [(i, i + 1) for i in range(count - 1)])]
    unnamed x4 -> x0, blocking collectives: 46.7 us -> none
    all_to_all x0 -> x3, blocking collectives: none -> 34.6 us  [everyone(): return lax.all_to_all(copies, AXES, 0, 0, tiled=True)]
    add x9 -> x4, other arithmetic: 35.2 us -> 1.63 us  [precondition(): return smooth + jnp.sum(deflation * mine[:, None, None, None], axis=0)]
    dot_general x20 -> x6, matrix products: 37.2 us -> 4.76 us  [the longest x4 4.03 us: precondition(): solved = jnp.dot(whole, vector, precision=PRECISE)]
    ppermute x54, starting transfers between devices: 121 us -> 138 us  [the longest x27 103 us: faces(): low = lax.ppermute(tail, axis, [(i, i + 1) for i in range(count - 1)])]
    reduce_sum x7 -> x17, other arithmetic: 23.8 us -> 9.68 us  [the longest x4 4.48 us: local(): jnp.sum(residual * precond)]
  transfers between devices with their start and end apart: 54 -> 56, of which waited for: 22 -> 8; matrix products, arithmetic and copies ran while one was open for 7% -> 7% of each run, Pallas kernels for 0% -> 0%
where the time goes in v1:
time: 314 us; the launch traced here: 312 us
  starting transfers between devices  150 us (48%)
  other arithmetic  47.8 us (15%)
  blocking collectives  44.6 us (14%)
  waiting for transfers between devices  31.7 us (10%)
  local copies, waits for them, and re-layouts  18.7 us (6%)
  between operations  13.8 us (4%)
  matrix products  4.76 us (2%)
    ppermute x27, starting transfers between devices, faces(): low = lax.ppermute(tail, axis, [(i, i + 1) for i in range(count - 1)])  103 us
    ppermute x27, starting transfers between devices, faces(): high = lax.ppermute(head, axis, [(i + 1, i) for i in range(count - 1)])  34.8 us
    all_to_all x3, blocking collectives, everyone(): return lax.all_to_all(copies, AXES, 0, 0, tiled=True)  34.6 us
    ppermute x27, waiting for transfers between devices, faces(): low = lax.ppermute(tail, axis, [(i, i + 1) for i in range(count - 1)])  17.5 us
    mul x24, other arithmetic, couplings(): low, high = (low * scale[2 * dim], high * scale[2 * dim + 1])  15.8 us
    all_to_all x2, starting transfers between devices, everyone(): return lax.all_to_all(copies, AXES, 0, 0, tiled=True)  12.1 us
    all_gather x1, blocking collectives, local(): whole = lax.all_gather(coarse_inverse, 'gx', axis=0, tiled=True)  10 us
    concatenate x4, other arithmetic, local(): parts = everyone(jnp.concatenate([scalars, coefficients(applied)]))  7.84 us
  transfers between devices with their start and end apart: 56, of which 8 were waited for; matrix products, arithmetic and copies ran while one was open for 7% of the time, Pallas kernels for 0%

profile of v1, /device:TPU:0, one launch (start us, length us, event | category | flops | bytes accessed | tf_op | source)
XLA Modules:
  0.0 311.6 jit_solution(13758603884640357724)
XLA Ops:
  3.9 7.3 %all-to-all-start = ((f32[32,1,16]{2,1,0:T(1,128)}), f32[32,1,16]{2,1,0:T(1,128)S(1)}, u32[]{:S(2)}, u32[]{:S(2)}) async-start(f32[32,1,16]{2,1,0:T(1,128)} %broadcast_in_dim.12), calls=%async_computation | async-start | bytes 32768 | tf_op jit(solution)/shard_map/all_to_all | solution.py:54
  15.7 5.3 %collective-permute-start.4 = (f32[8,64,1]{2,1,0:T(8,128)}, f32[8,64,1]{2,1,0:T(8,128)}, u32[]{:S(2)}, u32[]{:S(2)}) collective-permute-start(f32[8,64,1]{2,1,0:T(8,128)} %get-tuple-element.83), channel_id=1, source_target_pairs={{0,2},{2,4},{4,6},{1,3},{3,5},{5,7},{8,10},{10,12},{12,14},{9,11},... | collective-permute-start | bytes 6152 | tf_op jit(solution)/shard_map/ppermute | solution.py:23
  22.2 4.5 %collective-permute-start.2 = (f32[8,1,128]{2,1,0:T(1,128)S(1)}, f32[8,1,128]{2,1,0:T(1,128)S(1)}, u32[]{:S(2)}, u32[]{:S(2)}) collective-permute-start(f32[8,1,128]{2,1,0:T(1,128)S(1)} %get-tuple-element.81), channel_id=1, source_target_pairs={{0,8},{8,16},{16,24},{1,9},{9,17},{17,25},{2,10},{10,18},{18,26},{... | collective-permute-start | bytes 12296 | tf_op jit(solution)/shard_map/ppermute | solution.py:23
  27.5 10.0 %all_gather.3 = f32[256,256]{1,0:T(8,128)S(1)} all-gather(f32[64,256]{1,0:T(8,128)S(1)} %copy-done.37), channel_id=1, replica_groups=mesh['gx'=4,'gy'=4,'gz'=2] {'gx'}, dimensions={0}, use_global_device_ids=true | all-gather | bytes 327680 | tf_op jit(solution)/shard_map/all_gather | solution.py:86
  49.4 4.6 %collective-permute-start.10 = (f32[8,64,1]{2,1,0:T(8,128)S(1)}, f32[8,64,1]{2,1,0:T(8,128)S(1)}, u32[]{:S(2)}, u32[]{:S(2)}) collective-permute-start(f32[8,64,1]{2,1,0:T(8,128)S(1)} %get-tuple-element.73), channel_id=1, source_target_pairs={{0,2},{2,4},{4,6},{1,3},{3,5},{5,7},{8,10},{10,12},{12,14},{9,11},... | collective-permute-start | bytes 6152 | tf_op jit(solution)/shard_map/ppermute | solution.py:23
  55.3 4.5 %collective-permute-start.8 = (f32[8,1,128]{2,1,0:T(1,128)S(1)}, f32[8,1,128]{2,1,0:T(1,128)S(1)}, u32[]{:S(2)}, u32[]{:S(2)}) collective-permute-start(f32[8,1,128]{2,1,0:T(1,128)S(1)} %get-tuple-element.71), channel_id=1, source_target_pairs={{0,8},{8,16},{16,24},{1,9},{9,17},{17,25},{2,10},{10,18},{18,26},{... | collective-permute-start | bytes 12296 | tf_op jit(solution)/shard_map/ppermute | solution.py:23
  61.1 3.0 collective-permute-start.6
  75.8 4.5 %collective-permute-start.14 = (f32[8,1,128]{2,1,0:T(1,128)S(1)}, f32[8,1,128]{2,1,0:T(1,128)S(1)}, u32[]{:S(2)}, u32[]{:S(2)}) collective-permute-start(f32[8,1,128]{2,1,0:T(1,128)S(1)} %get-tuple-element.65), channel_id=1, source_target_pairs={{0,8},{8,16},{16,24},{1,9},{9,17},{17,25},{2,10},{10,18},{18,26},{... | collective-permute-start | bytes 12296 | tf_op jit(solution)/shard_map/ppermute | solution.py:23
  82.7 3.1 collective-permute-start.16
  85.8 4.5 %collective-permute-done.16 = f32[8,64,1]{2,1,0:T(8,128)S(1)} collective-permute-done((f32[8,64,1]{2,1,0:T(8,128)S(1)}, f32[8,64,1]{2,1,0:T(8,128)S(1)}, u32[]{:S(2)}, u32[]{:S(2)}) %collective-permute-start.16) | collective-permute-done | bytes 2080 | tf_op jit(solution)/shard_map/ppermute | solution.py:23
  95.1 4.8 %all-to-all-start.1 = ((f32[32,1,11]{2,1,0:T(1,128)}), f32[32,1,11]{2,1,0:T(1,128)S(1)}, u32[]{:S(2)}, u32[]{:S(2)}) async-start(f32[32,1,11]{2,1,0:T(1,128)} %broadcast_in_dim.14), calls=%async_computation.1 | async-start | bytes 32768 | tf_op jit(solution)/shard_map/all_to_all | solution.py:54
  99.9 7.1 %all-to-all-done.1 = f32[32,1,11]{2,1,0:T(1,128)S(1)} async-done(((f32[32,1,11]{2,1,0:T(1,128)}), f32[32,1,11]{2,1,0:T(1,128)S(1)}, u32[]{:S(2)}, u32[]{:S(2)}) %all-to-all-start.1) | async-done | bytes 1440 | tf_op jit(solution)/shard_map/all_to_all | solution.py:54
  116.0 4.6 %collective-permute-start.22 = (f32[8,64,1]{2,1,0:T(8,128)S(1)}, f32[8,64,1]{2,1,0:T(8,128)S(1)}, u32[]{:S(2)}, u32[]{:S(2)}) collective-permute-start(f32[8,64,1]{2,1,0:T(8,128)S(1)} %copy-done.35), channel_id=1, source_target_pairs={{0,2},{2,4},{4,6},{1,3},{3,5},{5,7},{8,10},{10,12},{12,14},{9,11},... | collective-permute-start | bytes 6152 | tf_op jit(solution)/shard_map/ppermute | solution.py:23
  121.9 4.5 %collective-permute-start.20 = (f32[8,1,128]{2,1,0:T(1,128)S(1)}, f32[8,1,128]{2,1,0:T(1,128)S(1)}, u32[]{:S(2)}, u32[]{:S(2)}) collective-permute-start(f32[8,1,128]{2,1,0:T(1,128)S(1)} %get-tuple-element.59), channel_id=1, source_target_pairs={{0,8},{8,16},{16,24},{1,9},{9,17},{17,25},{2,10},{10,18},{18,26},{... | collective-permute-start | bytes 12296 | tf_op jit(solution)/shard_map/ppermute | solution.py:23
  138.1 3.0 collective-permute-start.24
  142.4 4.5 %collective-permute-start.26 = (f32[8,1,128]{2,1,0:T(1,128)S(1)}, f32[8,1,128]{2,1,0:T(1,128)S(1)}, u32[]{:S(2)}, u32[]{:S(2)}) collective-permute-start(f32[8,1,128]{2,1,0:T(1,128)S(1)} %get-tuple-element.53), channel_id=1, source_target_pairs={{0,8},{8,16},{16,24},{1,9},{9,17},{17,25},{2,10},{10,18},{18,26},{... | collective-permute-start | bytes 12296 | tf_op jit(solution)/shard_map/ppermute | solution.py:23
  147.0 4.6 %collective-permute-start.28 = (f32[8,64,1]{2,1,0:T(8,128)S(1)}, f32[8,64,1]{2,1,0:T(8,128)S(1)}, u32[]{:S(2)}, u32[]{:S(2)}) collective-permute-start(f32[8,64,1]{2,1,0:T(8,128)S(1)} %get-tuple-element.55), channel_id=1, source_target_pairs={{0,2},{2,4},{4,6},{1,3},{3,5},{5,7},{8,10},{10,12},{12,14},{9,11},... | collective-permute-start | bytes 6152 | tf_op jit(solution)/shard_map/ppermute | solution.py:23
  151.6 4.5 %collective-permute-done.28 = f32[8,64,1]{2,1,0:T(8,128)S(1)} collective-permute-done((f32[8,64,1]{2,1,0:T(8,128)S(1)}, f32[8,64,1]{2,1,0:T(8,128)S(1)}, u32[]{:S(2)}, u32[]{:S(2)}) %collective-permute-start.28) | collective-permute-done | bytes 2080 | tf_op jit(solution)/shard_map/ppermute | solution.py:23
  160.3 11.6 %all_to_all.45 = f32[32,1,11]{2,1,0:T(1,128)S(1)} all-to-all(f32[32,1,11]{2,1,0:T(1,128)S(1)} %broadcast_in_dim.15), channel_id=1, replica_groups=mesh['gx'=4,'gy'=4,'gz'=2] {'gx','gy','gz'}, dimensions={0} | all-to-all | bytes 2816 | tf_op jit(solution)/shard_map/all_to_all | solution.py:54
  184.4 4.6 %collective-permute-start.34 = (f32[8,64,1]{2,1,0:T(8,128)S(1)}, f32[8,64,1]{2,1,0:T(8,128)S(1)}, u32[]{:S(2)}, u32[]{:S(2)}) collective-permute-start(f32[8,64,1]{2,1,0:T(8,128)S(1)} %copy-done.36), channel_id=1, source_target_pairs={{0,2},{2,4},{4,6},{1,3},{3,5},{5,7},{8,10},{10,12},{12,14},{9,11},... | collective-permute-start | bytes 6152 | tf_op jit(solution)/shard_map/ppermute | solution.py:23
  190.3 4.5 %collective-permute-start.32 = (f32[8,1,128]{2,1,0:T(1,128)S(1)}, f32[8,1,128]{2,1,0:T(1,128)S(1)}, u32[]{:S(2)}, u32[]{:S(2)}) collective-permute-start(f32[8,1,128]{2,1,0:T(1,128)S(1)} %copy-done.44), channel_id=1, source_target_pairs={{0,8},{8,16},{16,24},{1,9},{9,17},{17,25},{2,10},{10,18},{18,26},{... | collective-permute-start | bytes 12296 | tf_op jit(solution)/shard_map/ppermute | solution.py:23
  196.1 3.0 collective-permute-start.30
  205.1 3.0 collective-permute-start.36
  210.8 4.5 %collective-permute-start.38 = (f32[8,1,128]{2,1,0:T(1,128)S(1)}, f32[8,1,128]{2,1,0:T(1,128)S(1)}, u32[]{:S(2)}, u32[]{:S(2)}) collective-permute-start(f32[8,1,128]{2,1,0:T(1,128)S(1)} %get-tuple-element.41), channel_id=1, source_target_pairs={{0,8},{8,16},{16,24},{1,9},{9,17},{17,25},{2,10},{10,18},{18,26},{... | collective-permute-start | bytes 12296 | tf_op jit(solution)/shard_map/ppermute | solution.py:23
  220.1 4.2 %collective-permute-done.40 = f32[8,64,1]{2,1,0:T(8,128)S(1)} collective-permute-done((f32[8,64,1]{2,1,0:T(8,128)S(1)}, f32[8,64,1]{2,1,0:T(8,128)S(1)}, u32[]{:S(2)}, u32[]{:S(2)}) %collective-permute-start.40) | collective-permute-done | bytes 2080 | tf_op jit(solution)/shard_map/ppermute | solution.py:23
  228.6 11.5 %all_to_all.46 = f32[32,1,11]{2,1,0:T(1,128)S(1)} all-to-all(f32[32,1,11]{2,1,0:T(1,128)S(1)} %broadcast_in_dim.16), channel_id=1, replica_groups=mesh['gx'=4,'gy'=4,'gz'=2] {'gx','gy','gz'}, dimensions={0} | all-to-all | bytes 2816 | tf_op jit(solution)/shard_map/all_to_all | solution.py:54
  250.5 4.6 %collective-permute-start.46 = (f32[8,64,1]{2,1,0:T(8,128)S(1)}, f32[8,64,1]{2,1,0:T(8,128)S(1)}, u32[]{:S(2)}, u32[]{:S(2)}) collective-permute-start(f32[8,64,1]{2,1,0:T(8,128)S(1)} %copy-done.34), channel_id=1, source_target_pairs={{0,2},{2,4},{4,6},{1,3},{3,5},{5,7},{8,10},{10,12},{12,14},{9,11},... | collective-permute-start | bytes 6152 | tf_op jit(solution)/shard_map/ppermute | solution.py:23
  256.4 4.5 %collective-permute-start.44 = (f32[8,1,128]{2,1,0:T(1,128)S(1)}, f32[8,1,128]{2,1,0:T(1,128)S(1)}, u32[]{:S(2)}, u32[]{:S(2)}) collective-permute-start(f32[8,1,128]{2,1,0:T(1,128)S(1)} %get-tuple-element.35), channel_id=1, source_target_pairs={{0,8},{8,16},{16,24},{1,9},{9,17},{17,25},{2,10},{10,18},{18,26},{... | collective-permute-start | bytes 12296 | tf_op jit(solution)/shard_map/ppermute | solution.py:23
  262.2 3.0 collective-permute-start.42
  276.9 4.5 %collective-permute-start.50 = (f32[8,1,128]{2,1,0:T(1,128)S(1)}, f32[8,1,128]{2,1,0:T(1,128)S(1)}, u32[]{:S(2)}, u32[]{:S(2)}) collective-permute-start(f32[8,1,128]{2,1,0:T(1,128)S(1)} %get-tuple-element.29), channel_id=1, source_target_pairs={{0,8},{8,16},{16,24},{1,9},{9,17},{17,25},{2,10},{10,18},{18,26},{... | collective-permute-start | bytes 12296 | tf_op jit(solution)/shard_map/ppermute | solution.py:23
  286.2 4.2 %collective-permute-done.52 = f32[8,64,1]{2,1,0:T(8,128)S(1)} collective-permute-done((f32[8,64,1]{2,1,0:T(8,128)S(1)}, f32[8,64,1]{2,1,0:T(8,128)S(1)}, u32[]{:S(2)}, u32[]{:S(2)}) %collective-permute-start.52) | collective-permute-done | bytes 2080 | tf_op jit(solution)/shard_map/ppermute | solution.py:23
  294.3 11.5 %all_to_all.47 = f32[32,1,11]{2,1,0:T(1,128)S(1)} all-to-all(f32[32,1,11]{2,1,0:T(1,128)S(1)} %broadcast_in_dim.17), channel_id=1, replica_groups=mesh['gx'=4,'gy'=4,'gz'=2] {'gx','gy','gz'}, dimensions={0} | all-to-all | bytes 2816 | tf_op jit(solution)/shard_map/all_to_all | solution.py:54
  (303 shorter events, 129.4 us)
Async XLA Ops:
  3.9 33.5 %all-to-all-start = ((f32[32,1,16]{2,1,0:T(1,128)}), f32[32,1,16]{2,1,0:T(1,128)S(1)}, u32[]{:S(2)}, u32[]{:S(2)}) async-start(f32[32,1,16]{2,1,0:T(1,128)} %broadcast_in_dim.12), calls=%async_computation | async-start | bytes 32768 | tf_op jit(solution)/shard_map/all_to_all | solution.py:54
  11.3 28.6 %collective-permute-start = (f32[1,64,128]{2,1,0:T(8,128)S(1)}, f32[1,64,128]{2,1,0:T(8,128)S(1)}, u32[]{:S(2)}, u32[]{:S(2)}) collective-permute-start(f32[1,64,128]{2,1,0:T(8,128)S(1)} %get-tuple-element.76), channel_id=1, source_target_pairs={{0,1},{2,3},{4,5},{6,7},{8,9},{10,11},{12,13},{14,15},{16,17},{18,... | collective-permute-start | bytes 98312 | tf_op jit(solution)/shard_map/ppermute | solution.py:23
  14.4 27.6 %collective-permute-start.5 = (f32[8,64,1]{2,1,0:T(8,128)}, f32[8,64,1]{2,1,0:T(8,128)}, u32[]{:S(2)}, u32[]{:S(2)}) collective-permute-start(f32[8,64,1]{2,1,0:T(8,128)} %get-tuple-element.84), channel_id=1, source_target_pairs={{2,0},{4,2},{6,4},{3,1},{5,3},{7,5},{10,8},{12,10},{14,12},{11,9},... | collective-permute-start | bytes 6152 | tf_op jit(solution)/shard_map/ppermute | solution.py:24
  15.7 27.3 %collective-permute-start.4 = (f32[8,64,1]{2,1,0:T(8,128)}, f32[8,64,1]{2,1,0:T(8,128)}, u32[]{:S(2)}, u32[]{:S(2)}) collective-permute-start(f32[8,64,1]{2,1,0:T(8,128)} %get-tuple-element.83), channel_id=1, source_target_pairs={{0,2},{2,4},{4,6},{1,3},{3,5},{5,7},{8,10},{10,12},{12,14},{9,11},... | collective-permute-start | bytes 6152 | tf_op jit(solution)/shard_map/ppermute | solution.py:23
  20.9 23.3 %collective-permute-start.3 = (f32[8,1,128]{2,1,0:T(1,128)S(1)}, f32[8,1,128]{2,1,0:T(1,128)S(1)}, u32[]{:S(2)}, u32[]{:S(2)}) collective-permute-start(f32[8,1,128]{2,1,0:T(1,128)S(1)} %get-tuple-element.82), channel_id=1, source_target_pairs={{8,0},{16,8},{24,16},{9,1},{17,9},{25,17},{10,2},{18,10},{26,18},{... | collective-permute-start | bytes 12296 | tf_op jit(solution)/shard_map/ppermute | solution.py:24
  22.2 23.4 %collective-permute-start.2 = (f32[8,1,128]{2,1,0:T(1,128)S(1)}, f32[8,1,128]{2,1,0:T(1,128)S(1)}, u32[]{:S(2)}, u32[]{:S(2)}) collective-permute-start(f32[8,1,128]{2,1,0:T(1,128)S(1)} %get-tuple-element.81), channel_id=1, source_target_pairs={{0,8},{8,16},{16,24},{1,9},{9,17},{17,25},{2,10},{10,18},{18,26},{... | collective-permute-start | bytes 12296 | tf_op jit(solution)/shard_map/ppermute | solution.py:23
  48.1 13.0 %collective-permute-start.11 = (f32[8,64,1]{2,1,0:T(8,128)S(1)}, f32[8,64,1]{2,1,0:T(8,128)S(1)}, u32[]{:S(2)}, u32[]{:S(2)}) collective-permute-start(f32[8,64,1]{2,1,0:T(8,128)S(1)} %get-tuple-element.74), channel_id=1, source_target_pairs={{2,0},{4,2},{6,4},{3,1},{5,3},{7,5},{10,8},{12,10},{14,12},{11,9},... | collective-permute-start | bytes 6152 | tf_op jit(solution)/shard_map/ppermute | solution.py:24
  49.4 15.5 %collective-permute-start.10 = (f32[8,64,1]{2,1,0:T(8,128)S(1)}, f32[8,64,1]{2,1,0:T(8,128)S(1)}, u32[]{:S(2)}, u32[]{:S(2)}) collective-permute-start(f32[8,64,1]{2,1,0:T(8,128)S(1)} %get-tuple-element.73), channel_id=1, source_target_pairs={{0,2},{2,4},{4,6},{1,3},{3,5},{5,7},{8,10},{10,12},{12,14},{9,11},... | collective-permute-start | bytes 6152 | tf_op jit(solution)/shard_map/ppermute | solution.py:23
  68.8 21.5 %collective-permute-start.13 = (f32[1,64,128]{2,1,0:T(8,128)S(1)}, f32[1,64,128]{2,1,0:T(8,128)S(1)}, u32[]{:S(2)}, u32[]{:S(2)}) collective-permute-start(f32[1,64,128]{2,1,0:T(8,128)S(1)} %get-tuple-element.64), channel_id=1, source_target_pairs={{1,0},{3,2},{5,4},{7,6},{9,8},{11,10},{13,12},{15,14},{17,16},{19,... | collective-permute-start | bytes 98312 | tf_op jit(solution)/shard_map/ppermute | solution.py:24
  70.1 20.2 %collective-permute-start.12 = (f32[1,64,128]{2,1,0:T(8,128)S(1)}, f32[1,64,128]{2,1,0:T(8,128)S(1)}, u32[]{:S(2)}, u32[]{:S(2)}) collective-permute-start(f32[1,64,128]{2,1,0:T(8,128)S(1)} %get-tuple-element.63), channel_id=1, source_target_pairs={{0,1},{2,3},{4,5},{6,7},{8,9},{10,11},{12,13},{14,15},{16,17},{18,... | collective-permute-start | bytes 98312 | tf_op jit(solution)/shard_map/ppermute | solution.py:23
  74.5 15.8 %collective-permute-start.15 = (f32[8,1,128]{2,1,0:T(1,128)S(1)}, f32[8,1,128]{2,1,0:T(1,128)S(1)}, u32[]{:S(2)}, u32[]{:S(2)}) collective-permute-start(f32[8,1,128]{2,1,0:T(1,128)S(1)} %get-tuple-element.66), channel_id=1, source_target_pairs={{8,0},{16,8},{24,16},{9,1},{17,9},{25,17},{10,2},{18,10},{26,18},{... | collective-permute-start | bytes 12296 | tf_op jit(solution)/shard_map/ppermute | solution.py:24
  75.8 14.5 %collective-permute-start.14 = (f32[8,1,128]{2,1,0:T(1,128)S(1)}, f32[8,1,128]{2,1,0:T(1,128)S(1)}, u32[]{:S(2)}, u32[]{:S(2)}) collective-permute-start(f32[8,1,128]{2,1,0:T(1,128)S(1)} %get-tuple-element.65), channel_id=1, source_target_pairs={{0,8},{8,16},{16,24},{1,9},{9,17},{17,25},{2,10},{10,18},{18,26},{... | collective-permute-start | bytes 12296 | tf_op jit(solution)/shard_map/ppermute | solution.py:23
  95.1 12.0 %all-to-all-start.1 = ((f32[32,1,11]{2,1,0:T(1,128)}), f32[32,1,11]{2,1,0:T(1,128)S(1)}, u32[]{:S(2)}, u32[]{:S(2)}) async-start(f32[32,1,11]{2,1,0:T(1,128)} %broadcast_in_dim.14), calls=%async_computation.1 | async-start | bytes 32768 | tf_op jit(solution)/shard_map/all_to_all | solution.py:54
  114.4 13.3 %collective-permute-start.23 = (f32[8,64,1]{2,1,0:T(8,128)}, f32[8,64,1]{2,1,0:T(8,128)S(1)}, u32[]{:S(2)}, u32[]{:S(2)}) collective-permute-start(f32[8,64,1]{2,1,0:T(8,128)} %get-tuple-element.62), channel_id=1, source_target_pairs={{2,0},{4,2},{6,4},{3,1},{5,3},{7,5},{10,8},{12,10},{14,12},{11,9},... | collective-permute-start | bytes 6152 | tf_op jit(solution)/shard_map/ppermute | solution.py:24
  116.0 15.5 %collective-permute-start.22 = (f32[8,64,1]{2,1,0:T(8,128)S(1)}, f32[8,64,1]{2,1,0:T(8,128)S(1)}, u32[]{:S(2)}, u32[]{:S(2)}) collective-permute-start(f32[8,64,1]{2,1,0:T(8,128)S(1)} %copy-done.35), channel_id=1, source_target_pairs={{0,2},{2,4},{4,6},{1,3},{3,5},{5,7},{8,10},{10,12},{12,14},{9,11},... | collective-permute-start | bytes 6152 | tf_op jit(solution)/shard_map/ppermute | solution.py:23
  136.8 19.3 %collective-permute-start.25 = (f32[1,64,128]{2,1,0:T(8,128)S(1)}, f32[1,64,128]{2,1,0:T(8,128)S(1)}, u32[]{:S(2)}, u32[]{:S(2)}) collective-permute-start(f32[1,64,128]{2,1,0:T(8,128)S(1)} %get-tuple-element.52), channel_id=1, source_target_pairs={{1,0},{3,2},{5,4},{7,6},{9,8},{11,10},{13,12},{15,14},{17,16},{19,... | collective-permute-start | bytes 98312 | tf_op jit(solution)/shard_map/ppermute | solution.py:24
  138.1 18.0 %collective-permute-start.24 = (f32[1,64,128]{2,1,0:T(8,128)S(1)}, f32[1,64,128]{2,1,0:T(8,128)S(1)}, u32[]{:S(2)}, u32[]{:S(2)}) collective-permute-start(f32[1,64,128]{2,1,0:T(8,128)S(1)} %get-tuple-element.51), channel_id=1, source_target_pairs={{0,1},{2,3},{4,5},{6,7},{8,9},{10,11},{12,13},{14,15},{16,17},{18,... | collective-permute-start | bytes 98312 | tf_op jit(solution)/shard_map/ppermute | solution.py:23
  141.1 15.0 %collective-permute-start.27 = (f32[8,1,128]{2,1,0:T(1,128)S(1)}, f32[8,1,128]{2,1,0:T(1,128)S(1)}, u32[]{:S(2)}, u32[]{:S(2)}) collective-permute-start(f32[8,1,128]{2,1,0:T(1,128)S(1)} %get-tuple-element.54), channel_id=1, source_target_pairs={{8,0},{16,8},{24,16},{9,1},{17,9},{25,17},{10,2},{18,10},{26,18},{... | collective-permute-start | bytes 12296 | tf_op jit(solution)/shard_map/ppermute | solution.py:24
  142.4 13.7 %collective-permute-start.26 = (f32[8,1,128]{2,1,0:T(1,128)S(1)}, f32[8,1,128]{2,1,0:T(1,128)S(1)}, u32[]{:S(2)}, u32[]{:S(2)}) collective-permute-start(f32[8,1,128]{2,1,0:T(1,128)S(1)} %get-tuple-element.53), channel_id=1, source_target_pairs={{0,8},{8,16},{16,24},{1,9},{9,17},{17,25},{2,10},{10,18},{18,26},{... | collective-permute-start | bytes 12296 | tf_op jit(solution)/shard_map/ppermute | solution.py:23
  182.8 13.4 %collective-permute-start.35 = (f32[8,64,1]{2,1,0:T(8,128)}, f32[8,64,1]{2,1,0:T(8,128)S(1)}, u32[]{:S(2)}, u32[]{:S(2)}) collective-permute-start(f32[8,64,1]{2,1,0:T(8,128)} %get-tuple-element.50), channel_id=1, source_target_pairs={{2,0},{4,2},{6,4},{3,1},{5,3},{7,5},{10,8},{12,10},{14,12},{11,9},... | collective-permute-start | bytes 6152 | tf_op jit(solution)/shard_map/ppermute | solution.py:24
  184.4 15.5 %collective-permute-start.34 = (f32[8,64,1]{2,1,0:T(8,128)S(1)}, f32[8,64,1]{2,1,0:T(8,128)S(1)}, u32[]{:S(2)}, u32[]{:S(2)}) collective-permute-start(f32[8,64,1]{2,1,0:T(8,128)S(1)} %copy-done.36), channel_id=1, source_target_pairs={{0,2},{2,4},{4,6},{1,3},{3,5},{5,7},{8,10},{10,12},{12,14},{9,11},... | collective-permute-start | bytes 6152 | tf_op jit(solution)/shard_map/ppermute | solution.py:23
  188.9 11.7 %collective-permute-start.33 = (f32[8,1,128]{2,1,0:T(1,128)S(1)}, f32[8,1,128]{2,1,0:T(1,128)S(1)}, u32[]{:S(2)}, u32[]{:S(2)}) collective-permute-start(f32[8,1,128]{2,1,0:T(1,128)S(1)} %copy-done.45), channel_id=1, source_target_pairs={{8,0},{16,8},{24,16},{9,1},{17,9},{25,17},{10,2},{18,10},{26,18},{... | collective-permute-start | bytes 12296 | tf_op jit(solution)/shard_map/ppermute | solution.py:24
  203.8 20.5 %collective-permute-start.37 = (f32[1,64,128]{2,1,0:T(8,128)S(1)}, f32[1,64,128]{2,1,0:T(8,128)S(1)}, u32[]{:S(2)}, u32[]{:S(2)}) collective-permute-start(f32[1,64,128]{2,1,0:T(8,128)S(1)} %get-tuple-element.40), channel_id=1, source_target_pairs={{1,0},{3,2},{5,4},{7,6},{9,8},{11,10},{13,12},{15,14},{17,16},{19,... | collective-permute-start | bytes 98312 | tf_op jit(solution)/shard_map/ppermute | solution.py:24
  205.1 19.2 %collective-permute-start.36 = (f32[1,64,128]{2,1,0:T(8,128)S(1)}, f32[1,64,128]{2,1,0:T(8,128)S(1)}, u32[]{:S(2)}, u32[]{:S(2)}) collective-permute-start(f32[1,64,128]{2,1,0:T(8,128)S(1)} %get-tuple-element.39), channel_id=1, source_target_pairs={{0,1},{2,3},{4,5},{6,7},{8,9},{10,11},{12,13},{14,15},{16,17},{18,... | collective-permute-start | bytes 98312 | tf_op jit(solution)/shard_map/ppermute | solution.py:23
  209.5 14.9 %collective-permute-start.39 = (f32[8,1,128]{2,1,0:T(1,128)S(1)}, f32[8,1,128]{2,1,0:T(1,128)S(1)}, u32[]{:S(2)}, u32[]{:S(2)}) collective-permute-start(f32[8,1,128]{2,1,0:T(1,128)S(1)} %get-tuple-element.42), channel_id=1, source_target_pairs={{8,0},{16,8},{24,16},{9,1},{17,9},{25,17},{10,2},{18,10},{26,18},{... | collective-permute-start | bytes 12296 | tf_op jit(solution)/shard_map/ppermute | solution.py:24
  210.8 13.6 %collective-permute-start.38 = (f32[8,1,128]{2,1,0:T(1,128)S(1)}, f32[8,1,128]{2,1,0:T(1,128)S(1)}, u32[]{:S(2)}, u32[]{:S(2)}) collective-permute-start(f32[8,1,128]{2,1,0:T(1,128)S(1)} %get-tuple-element.41), channel_id=1, source_target_pairs={{0,8},{8,16},{16,24},{1,9},{9,17},{17,25},{2,10},{10,18},{18,26},{... | collective-permute-start | bytes 12296 | tf_op jit(solution)/shard_map/ppermute | solution.py:23
  248.9 13.3 %collective-permute-start.47 = (f32[8,64,1]{2,1,0:T(8,128)}, f32[8,64,1]{2,1,0:T(8,128)S(1)}, u32[]{:S(2)}, u32[]{:S(2)}) collective-permute-start(f32[8,64,1]{2,1,0:T(8,128)} %get-tuple-element.38), channel_id=1, source_target_pairs={{2,0},{4,2},{6,4},{3,1},{5,3},{7,5},{10,8},{12,10},{14,12},{11,9},... | collective-permute-start | bytes 6152 | tf_op jit(solution)/shard_map/ppermute | solution.py:24
  250.5 15.5 %collective-permute-start.46 = (f32[8,64,1]{2,1,0:T(8,128)S(1)}, f32[8,64,1]{2,1,0:T(8,128)S(1)}, u32[]{:S(2)}, u32[]{:S(2)}) collective-permute-start(f32[8,64,1]{2,1,0:T(8,128)S(1)} %copy-done.34), channel_id=1, source_target_pairs={{0,2},{2,4},{4,6},{1,3},{3,5},{5,7},{8,10},{10,12},{12,14},{9,11},... | collective-permute-start | bytes 6152 | tf_op jit(solution)/shard_map/ppermute | solution.py:23
  270.0 20.5 %collective-permute-start.49 = (f32[1,64,128]{2,1,0:T(8,128)S(1)}, f32[1,64,128]{2,1,0:T(8,128)S(1)}, u32[]{:S(2)}, u32[]{:S(2)}) collective-permute-start(f32[1,64,128]{2,1,0:T(8,128)S(1)} %get-tuple-element.28), channel_id=1, source_target_pairs={{1,0},{3,2},{5,4},{7,6},{9,8},{11,10},{13,12},{15,14},{17,16},{19,... | collective-permute-start | bytes 98312 | tf_op jit(solution)/shard_map/ppermute | solution.py:24
  271.3 19.2 %collective-permute-start.48 = (f32[1,64,128]{2,1,0:T(8,128)S(1)}, f32[1,64,128]{2,1,0:T(8,128)S(1)}, u32[]{:S(2)}, u32[]{:S(2)}) collective-permute-start(f32[1,64,128]{2,1,0:T(8,128)S(1)} %get-tuple-element.27), channel_id=1, source_target_pairs={{0,1},{2,3},{4,5},{6,7},{8,9},{10,11},{12,13},{14,15},{16,17},{18,... | collective-permute-start | bytes 98312 | tf_op jit(solution)/shard_map/ppermute | solution.py:23
  275.6 14.9 %collective-permute-start.51 = (f32[8,1,128]{2,1,0:T(1,128)S(1)}, f32[8,1,128]{2,1,0:T(1,128)S(1)}, u32[]{:S(2)}, u32[]{:S(2)}) collective-permute-start(f32[8,1,128]{2,1,0:T(1,128)S(1)} %get-tuple-element.30), channel_id=1, source_target_pairs={{8,0},{16,8},{24,16},{9,1},{17,9},{25,17},{10,2},{18,10},{26,18},{... | collective-permute-start | bytes 12296 | tf_op jit(solution)/shard_map/ppermute | solution.py:24
  276.9 13.6 %collective-permute-start.50 = (f32[8,1,128]{2,1,0:T(1,128)S(1)}, f32[8,1,128]{2,1,0:T(1,128)S(1)}, u32[]{:S(2)}, u32[]{:S(2)}) collective-permute-start(f32[8,1,128]{2,1,0:T(1,128)S(1)} %get-tuple-element.29), channel_id=1, source_target_pairs={{0,8},{8,16},{16,24},{1,9},{9,17},{17,25},{2,10},{10,18},{18,26},{... | collective-permute-start | bytes 12296 | tf_op jit(solution)/shard_map/ppermute | solution.py:23
  (71 other events, 945.2 us)

commit v2 on v1

v2 whole, which is shorter than its diff:
```python
import jax
import jax.numpy as jnp
from jax import lax
from jax.experimental import pallas as pl
from jax.experimental.pallas import tpu as pltpu
from jax.sharding import PartitionSpec as P

ITERS = 4
RELAXATION = 0.7
PRECISE = lax.Precision.HIGHEST
LANES = 128
STRIDE = 8
PERIOD = 32
ROW = 32
SLOT = 40


def conduct(first_perm, second_perm):
    return 2.0 * first_perm * second_perm / jnp.maximum(first_perm + second_perm, 0.05)


def turn(values, shift, axis):
    size = values.shape[axis]
    if isinstance(shift, int):
        shift = shift % size
        if shift == 0:
            return values
    return pltpu.roll(values, shift, axis)


def x_next(v):
    return turn(v, -1, 0)


def x_prev(v):
    return turn(v, 1, 0)


def y_next(v):
    return turn(v, -1, 1)


def y_prev(v):
    return turn(v, 1, 1)


def iota(shape, dim):
    return lax.broadcasted_iota(jnp.int32, shape, dim)


def place(shape):
    lane = iota(shape, 1)
    return lane >> 3, lane & 7


def eights(values):
    out = values[0:8]
    for t in range(1, values.shape[0] // 8):
        out = out + values[8 * t : 8 * t + 8]
    return out


def pack_kernel(zdim, xdim, *refs):
    (own, other) = (refs[0:3], refs[3:6])
    (hi_own, lo_own, hi_other, lo_other, d_own, d_other) = refs[6:12]
    main, strip_hi, strip_lo = refs[12:15]
    rows = xdim + 8
    shape = (rows, LANES)
    plane_of, slot_of = place(shape)
    for f in range(3):
        acc = jnp.zeros(shape, jnp.float32)
        for p in range(2 * zdim):
            pz = p % zdim
            src = own if p < zdim else other
            hi = hi_own if p < zdim else hi_other
            lo = lo_own if p < zdim else lo_other
            at = (f * zdim + pz) * 3
            tile = jnp.concatenate(
                [hi[at : at + 3, :], jnp.zeros((2, LANES), jnp.float32), lo[at : at + 3, :]], axis=0
            )
            plane = jnp.concatenate([src[f][pz], tile], axis=0)
            main[f, p] = plane
            moved = turn(plane, STRIDE * p + 3, 1)
            acc = jnp.where((plane_of == p) & (slot_of < 6), moved, acc)
        strip_hi[f * rows : (f + 1) * rows, :] = acc
        strip_lo[f * rows : (f + 1) * rows, :] = acc
    lane = iota((xdim, LANES), 1)
    vectors = d_own.shape[0]
    hi_acc = jnp.zeros((xdim, LANES), jnp.float32)
    lo_acc = hi_acc
    for b, d_ref in ((0, d_own), (1, d_other)):
        for k in range(vectors):

            def body(pz, carry, k=k, b=b, d_ref=d_ref):
                one, two = carry
                at = STRIDE * (b * zdim + pz) + k
                moved = pltpu.roll(d_ref[k, pz], at + 1, 1)
                one = jnp.where(lane == at, moved, one)
                two = jnp.where(lane == ((at + 1) & (LANES - 1)), moved, two)
                return one, two

            hi_acc, lo_acc = lax.fori_loop(0, zdim, body, (hi_acc, lo_acc))
    strip_hi[3 * rows : 3 * rows + xdim, :] = hi_acc
    strip_lo[3 * rows : 3 * rows + xdim, :] = turn(lo_acc, -1, 1)


def solve_coarse(known, select_ref, yb_ref):
    total = 0.0
    for t, row in enumerate(known):
        total = total + select_ref[:, LANES * t : LANES * (t + 1)] * row
    column = jnp.sum(total, axis=1, keepdims=True)
    yb_ref[...] = jnp.broadcast_to(column, yb_ref.shape)


def finish(c, scaled, strip_q, r_ref, z_ref, send_ref, w_ref, zown_ref, sw_ref, img_ref, ids, last):
    zdim, xdim = c["d_own"].shape[1], c["d_own"].shape[2]
    planes, rows = 2 * zdim, xdim + 8
    vectors = c["d_own"].shape[0]
    strips = c["strips"]
    yb = c["yb"]
    plane_of, slot_of = place((rows, LANES))

    te, cxp, cxm, cin, cout, czp, czm, ss = (strips[i] for i in range(8))
    smooth = (
        cxp * x_next(strip_q)
        + cxm * x_prev(strip_q)
        + cin * turn(strip_q, 4, 1)
        + cout * turn(strip_q, 2, 1)
        + czp * turn(strip_q, -STRIDE, 1)
        + czm * turn(strip_q, STRIDE, 1)
    )
    strip_z = (2.0 - RELAXATION) * strip_q + ss * smooth
    lane16 = iota((2 * vectors, LANES), 1)
    row16 = iota((2 * vectors, LANES), 0)
    wanted = row16 == (lane16 >> 6) * vectors + (lane16 & 7)
    for side, d_strip in ((0, c["dy_hi"]), (1, c["dy_lo"])):
        at = 6 * vectors + side * 2 * vectors
        coeff = jnp.sum(jnp.where(wanted, yb[at : at + 2 * vectors, :], 0.0), axis=0, keepdims=True)
        t = d_strip[...] * coeff
        t = t + turn(t, -1, 1)
        t = t + turn(t, -2, 1)
        t = t + turn(t, -4, 1)
        t = jnp.where(slot_of[:xdim] == 5 + side, turn(t, 5 + side, 1), 0.0)
        t = jnp.concatenate([t, jnp.zeros((8, LANES), jnp.float32)], axis=0)
        strip_z = strip_z + t
    edge_q = te * strip_q
    edge_z = te * strip_z

    row8 = iota((8, LANES), 0)
    for b in range(2):
        d_ref = c["d_own"] if b == 0 else c["d_other"]
        x_rows = []
        for side in range(2):
            dx = c["dx"][2 * b + side]
            acc = 0.0
            for k in range(vectors):
                at = (3 * b + 1 + side) * vectors + k
                acc = acc + dx[k * zdim : (k + 1) * zdim, :] * yb[at : at + 1, :]
            x_rows.append(acc)
        c["bx"][0] = x_rows[0]
        c["bx"][1] = x_rows[1]
        mxp, mxm, my = c["mxp"][b], c["mxm"][b], c["my"][b]

        def body(pz, carry, b=b, d_ref=d_ref, mxp=mxp, mxm=mxm, my=my):
            p = b * zdim + pz
            q = scaled[p]
            tx, ty = c["tx"][p], c["ty"][p]
            acc = tx * mxp * x_next(q) + mxm * x_prev(tx * q)
            acc = acc + ty * y_next(q) + y_prev(ty * q)
            acc = acc + my * pltpu.roll(edge_q, LANES - 6 - STRIDE * p, 1)
            acc = acc + c["tzlp"][p] * scaled[lax.rem(p + 1, planes)]
            acc = acc + c["tzlm"][p] * scaled[lax.rem(p + planes - 1, planes)]
            z = (2.0 - RELAXATION) * q + c["s"][p] * acc
            field = 0.0
            for k in range(vectors):
                at = 3 * b * vectors + k
                field = field + d_ref[k, pz] * yb[at : at + 1, :]
            tile = jnp.where(row8 == 0, c["bx"][0, pl.ds(pz, 1), :], 0.0)
            tile = jnp.where(row8 == 7, c["bx"][1, pl.ds(pz, 1), :], tile)
            z = z + jnp.concatenate([field, tile], axis=0)
            z_ref[p] = z
            if b == 0:
                zown_ref[pz] = z[:xdim]
            return carry

        lax.fori_loop(0, zdim, body, 0)

    lane = iota((rows, LANES), 1)
    edge = jnp.where((lane == 0) | (lane == LANES - 1), 1.0, 0.0)
    plane64, slot64 = plane_of[:xdim], slot_of[:xdim]
    zero = jnp.zeros((8, LANES), jnp.float32)
    scal = (zero, zero, zero)
    coeffs = []
    packed = jnp.zeros((xdim, LANES), jnp.float32)
    for b in range(2):
        d_ref = c["d_own"] if b == 0 else c["d_other"]

        def body(pz, carry, b=b, d_ref=d_ref):
            scal, sums, packed = carry
            p = b * zdim + pz
            z = z_ref[p]
            tx, ty = c["tx"][p], c["ty"][p]
            before = lax.rem(p + planes - 1, planes)
            acc = tx * x_next(z) + x_prev(tx * z)
            acc = acc + ty * y_next(z) + y_prev(ty * z)
            acc = acc + edge * pltpu.roll(edge_z, LANES - 6 - STRIDE * p, 1)
            acc = acc + c["tz"][p] * z_ref[lax.rem(p + 1, planes)]
            acc = acc + c["tz"][before] * z_ref[before]
            w = (c["diag"][p] * z - acc)[:xdim]
            z = z[:xdim]
            w_ref[p] = w
            rz, zw, zi = scal
            rz = rz + eights(r_ref[p][:xdim] * z)
            zw = zw + eights(w * z)
            if img_ref is not None:
                zi = zi + eights(img_ref[p][:xdim] * z)
            sums = tuple(sums[k] + eights(d_ref[k, pz] * w) for k in range(vectors))
            moved = pltpu.roll(w, lax.rem(STRIDE * p + 2, LANES), 1)
            packed = jnp.where((plane64 == p) & (slot64 < 4), moved, packed)
            return (rz, zw, zi), sums, packed

        scal, sums, packed = lax.fori_loop(0, zdim, body, (scal, (zero,) * vectors, packed))
        coeffs.extend(sums)

    acc_ref = c["acc"]
    acc_ref[...] = jnp.zeros(acc_ref.shape, jnp.float32)
    for j, value in enumerate(coeffs + list(scal)):
        acc_ref[j : j + 1, :] = jnp.sum(value, axis=0, keepdims=True)
    column = jnp.sum(acc_ref[...], axis=1, keepdims=True)
    spread = jnp.broadcast_to(column, (PERIOD, LANES))
    spread = jnp.where(iota((PERIOD, LANES), 0) == (iota((PERIOD, LANES), 1) & (PERIOD - 1)), spread, 0.0)
    row = jnp.sum(spread, axis=0, keepdims=True)
    peers = send_ref.shape[0]
    if last:
        for p in range(peers):
            send_ref[p] = row
        return
    for p in range(peers):
        send_ref[p, ROW : ROW + 1, :] = row
    sw_ref[...] = packed
    for p in range(planes):
        send_ref[ids[1], 2 * p : 2 * p + 2, :] = w_ref[p, xdim - 2 : xdim, :]
        send_ref[ids[2], 2 * p : 2 * p + 2, :] = w_ref[p, 0:2, :]
    part = xdim // 4
    pair = (iota((part, LANES), 1) & 7) >> 1
    to_hi = jnp.zeros((part, LANES), jnp.float32)
    to_lo = to_hi
    for g in range(4):
        rows_g = packed[g * part : (g + 1) * part]
        to_hi = jnp.where(pair == g, turn(rows_g, 2 * g, 1), to_hi)
        to_lo = jnp.where(pair == g, turn(rows_g, 2 * g - 2, 1), to_lo)
    send_ref[ids[3], 0:part, :] = to_hi
    send_ref[ids[4], 0:part, :] = to_lo
    for i in (5, 6):
        send_ref[ids[i], 0:1, :] = packed[xdim - 1 : xdim, :]
    for i in (7, 8):
        send_ref[ids[i], 0:1, :] = packed[0:1, :]


def first_kernel(zdim, xdim, *refs):
    (ids, mt, f, s_own, s_hi, s_lo, d_own, d_other) = refs[0:8]
    dx = refs[8:12]
    (select, known_ref) = refs[12:14]
    (send, w_ref, zown, sw, strips, tx, ty, tz, tzlp, tzlm, s_ref, diag_ref, mxp, mxm, my, rs_ref) = refs[14:30]
    (scaled, z_ref, yb, acc, bx) = refs[30:35]
    planes, rows = 2 * zdim, xdim + 8
    shape = (rows, LANES)
    row, lane = iota(shape, 0), iota(shape, 1)
    plane_of, slot_of = place(shape)
    zb = ids[9]
    cut = jnp.where(zb == 0, planes - 1, zdim - 1)

    def mg(col, b, d):
        return mt[(col * 2 + b) * 6 + d]

    def by_row(b, d):
        return jnp.where(row < xdim, mg(0, b, d), jnp.where(row < xdim + 4, mg(1, b, d), mg(2, b, d)))

    for b in range(2):
        mxp[b] = jnp.where(row == xdim - 1, mg(0, b, 3), jnp.where(row == rows - 1, mg(2, b, 3), 1.0))
        mxm[b] = jnp.where(row == 0, mg(0, b, 2), jnp.where(row == xdim, mg(1, b, 2), 1.0))
        my[b] = jnp.where(lane == LANES - 1, by_row(b, 5), jnp.where(lane == 0, by_row(b, 4), 0.0))

    def strip(i):
        at = slice(i * rows, (i + 1) * rows)
        own, hi, lo = s_own[at, :], s_hi[at, :], s_lo[at, :]
        out = jnp.where((slot_of == 1) | (slot_of == 2), turn(own, -1, 1), 0.0)
        out = jnp.where(slot_of == 5, turn(hi, 2, 1), out)
        out = jnp.where(slot_of == 3, turn(hi, -1, 1), out)
        out = jnp.where(slot_of == 0, turn(hi, -5, 1), out)
        out = jnp.where(slot_of == 6, turn(lo, 4, 1), out)
        out = jnp.where(slot_of == 4, turn(lo, 3, 1), out)
        return jnp.where(slot_of == 7, turn(lo, 7, 1), out)

    ps, st, rs = strip(0), strip(1), strip(2)
    rs_ref[...] = rs
    face = (slot_of == 5) | (slot_of == 6)
    t_x = conduct(ps, x_next(ps))
    t_z = jnp.where(plane_of == cut, 0.0, conduct(ps, turn(ps, -STRIDE, 1)))
    t_in = jnp.where(face, conduct(ps, turn(ps, 4, 1)), 0.0)
    t_out = jnp.where(face, conduct(ps, turn(ps, 2, 1)), 0.0)
    t_far = jnp.where(
        slot_of == 3,
        conduct(ps, turn(ps, 3, 1)),
        jnp.where(slot_of == 4, conduct(ps, turn(ps, -3, 1)), 0.0),
    )
    diag_s = st + t_x + x_prev(t_x) + t_z + turn(t_z, STRIDE, 1)
    diag_s = diag_s + t_in + t_out + turn(t_out, -2, 1) + t_far
    ss = jnp.where(diag_s > 0.0, RELAXATION / jnp.where(diag_s > 0.0, diag_s, 1.0), 0.0)

    def by_side(b, d_hi, d_lo):
        return jnp.where(slot_of == 5, mg(3, b, d_hi), mg(4, b, d_lo))

    def by_brick(d_hi, d_lo):
        return jnp.where(plane_of < zdim, by_side(0, d_hi, d_lo), by_side(1, d_hi, d_lo))

    def only(values):
        return jnp.where(face, values, 0.0)

    strips[0] = t_in
    strips[1] = only(t_x * jnp.where(row == xdim - 1, by_brick(3, 3), 1.0))
    strips[2] = only(x_prev(t_x) * jnp.where(row == 0, by_brick(2, 2), 1.0))
    strips[3] = t_in * by_brick(4, 5)
    strips[4] = t_out
    high = (plane_of == zdim - 1) | (plane_of == planes - 1)
    low = (plane_of == 0) | (plane_of == zdim)
    strips[5] = only(t_z * jnp.where(high, by_brick(1, 1), 1.0))
    strips[6] = only(turn(t_z, STRIDE, 1) * jnp.where(low, by_brick(0, 0), 1.0))

    inside = lane < LANES - 1

    def transmit(p, carry):
        here = f[0, p]
        after = f[0, lax.rem(p + 1, planes)]
        tx[p] = conduct(here, x_next(here))
        ty[p] = jnp.where(inside, conduct(here, y_next(here)), 0.0)
        tz[p] = conduct(here, after) * jnp.where(p == cut, 0.0, 1.0)
        return carry

    lax.fori_loop(0, planes, transmit, 0)
    edge = (lane == 0) | (lane == LANES - 1)
    inner = jnp.zeros(shape, jnp.float32)
    for b in range(2):
        m_hi, m_lo = by_row(b, 1), by_row(b, 0)

        def diagonal(pz, inner, b=b, m_hi=m_hi, m_lo=m_lo):
            p = b * zdim + pz
            t_x, t_y, t_z = tx[p], ty[p], tz[p]
            t_b = tz[lax.rem(p + planes - 1, planes)]
            total = f[1, p] + t_x + x_prev(t_x) + t_y + y_prev(t_y) + t_z + t_b
            total = total + jnp.where(edge, pltpu.roll(t_in, LANES - 6 - STRIDE * p, 1), 0.0)
            relax = jnp.where(total > 0.0, RELAXATION / jnp.where(total > 0.0, total, 1.0), 0.0)
            diag_ref[p] = total
            s_ref[p] = relax
            tzlp[p] = t_z * jnp.where(pz == zdim - 1, m_hi, 1.0)
            tzlm[p] = t_b * jnp.where(pz == 0, m_lo, 1.0)
            scaled[p] = relax * f[2, p]
            moved = pltpu.roll(relax, lax.rem(STRIDE * p + 2, LANES), 1)
            return jnp.where((plane_of == p) & ((slot_of == 1) | (slot_of == 2)), moved, inner)

        inner = lax.fori_loop(0, zdim, diagonal, inner)
    ss = jnp.where((slot_of == 1) | (slot_of == 2), inner, ss)
    strips[7] = ss

    known = [known_ref[t : t + 1, :] for t in range(known_ref.shape[0])]
    solve_coarse(known, select, yb)
    c = dict(
        tx=tx, ty=ty, tz=tz, tzlp=tzlp, tzlm=tzlm, s=s_ref, diag=diag_ref, mxp=mxp, mxm=mxm, my=my,
        strips=strips, d_own=d_own, d_other=d_other, dx=dx, dy_hi=s_hi.at[3 * rows : 3 * rows + xdim, :],
        dy_lo=s_lo.at[3 * rows : 3 * rows + xdim, :], yb=yb, acc=acc, bx=bx,
    )
    finish(c, scaled, ss * rs, f.at[2], z_ref, send, w_ref, zown, sw, None, ids, False)


def totals(rows):
    lane = iota((1, LANES), 1)
    group = lane >> 5
    tiles = []
    for t in range(len(rows) // 4):
        tile = 0.0
        for i in range(4):
            tile = tile + jnp.where(group == i, rows[4 * t + i], 0.0)
        tiles.append(tile)
    total = tiles[0]
    for tile in tiles[1:]:
        total = total + tile
    index = lane & (PERIOD - 1)
    sums = [
        jnp.sum(jnp.where(index == 16 + j, total, 0.0), axis=1, keepdims=True) for j in range(3)
    ]
    return tiles, sums


def scalars(sums, scal_ref, first):
    inner = sums[0]
    if first:
        ratio = jnp.zeros_like(inner)
        curvature = sums[1]
    else:
        ratio = inner / scal_ref[0:1, 0:1]
        curvature = sums[1] + ratio * (2.0 * sums[2] + ratio * scal_ref[1:2, 0:1])
    return inner, ratio, curvature, inner / curvature


def next_kernel(zdim, xdim, first, last, *refs):
    refs = list(refs)

    def take(n):
        out, refs[:n] = refs[:n], []
        return out

    ids, got, d_own, d_other, *dx = take(8)
    s_hi, s_lo, select, strips, tx, ty, tz, tzlp, tzlm, s_ref, diag_ref, mxp, mxm, my = take(14)
    known_ref, w_in, z_in, sw_in, rs_in = take(5)
    if first:
        (f,) = take(1)
        r_in = f.at[2]
    else:
        r_in, img_in, dir_in, sol_in, is_in, kimg_ref, scal_ref = take(7)
    send, w_ref, zown, sw, rs_ref, r_ref, img_ref, dir_ref, sol_ref, is_ref, known_out, kimg_out, scal_out = take(13)
    scaled, z_ref, yb, acc, bx, tiles_ref = take(6)
    planes, rows = 2 * zdim, xdim + 8
    plane_of, slot_of = place((rows, LANES))

    peers = got.shape[0]
    tiles, sums = totals([got[p, ROW : ROW + 1, :] for p in range(peers)])
    inner, ratio, curvature, step = scalars(sums, None if first else scal_ref, first)
    scal_out[0:1, :] = jnp.broadcast_to(inner, (1, LANES))
    scal_out[1:2, :] = jnp.broadcast_to(curvature, (1, LANES))
    known = []
    for t, tile in enumerate(tiles):
        if not first:
            tile = tile + ratio * kimg_ref[t : t + 1, :]
        kimg_out[t : t + 1, :] = tile
        value = known_ref[t : t + 1, :] - step * tile
        known_out[t : t + 1, :] = value
        known.append(value)
    solve_coarse(known, select, yb)

    part = xdim // 4
    from_hi, from_lo = got[ids[3], 0:part, :], got[ids[4], 0:part, :]
    own = sw_in[...]
    slot_part = slot_of[:part]
    blocks = []
    for g in range(4):
        value = own[g * part : (g + 1) * part]
        value = jnp.where(slot_part == 5, turn(from_hi, 5 - 2 * g, 1), value)
        value = jnp.where(slot_part == 3, turn(from_hi, 2 - 2 * g, 1), value)
        value = jnp.where(slot_part == 4, turn(from_lo, 4 - 2 * g, 1), value)
        value = jnp.where(slot_part == 6, turn(from_lo, 5 - 2 * g, 1), value)
        blocks.append(value)
    slot8, row8 = slot_of[:8], iota((8, LANES), 0)
    tile = jnp.zeros((8, LANES), jnp.float32)
    for i, at, want, shift in ((5, 0, 5, 3), (6, 0, 6, 5), (7, 7, 5, 3), (8, 7, 6, 5)):
        value = turn(jnp.broadcast_to(got[ids[i], 0:1, :], (8, LANES)), shift, 1)
        tile = jnp.where((row8 == at) & (slot8 == want), value, tile)
    ws = jnp.concatenate(blocks + [tile], axis=0)
    ws = jnp.where((slot_of == 0) | (slot_of == 7), 0.0, ws)
    if not first:
        ws = ws + ratio * is_in[...]
    is_ref[...] = ws
    rs = rs_in[...] - step * ws
    rs_ref[...] = rs
    strip_q = strips[7] * rs

    tiles_ref[...] = jnp.zeros(tiles_ref.shape, jnp.float32)
    for p in range(planes):
        tiles_ref[p, 0:2, :] = got[ids[1], 2 * p : 2 * p + 2, :]
        tiles_ref[p, 6:8, :] = got[ids[2], 2 * p : 2 * p + 2, :]

    def update(p, carry):
        image = jnp.concatenate([w_in[p], tiles_ref[p]], axis=0)
        if not first:
            image = image + ratio * img_in[p]
        img_ref[p] = image
        r = r_in[p] - step * image
        r_ref[p] = r
        scaled[p] = s_ref[p] * r
        return carry

    lax.fori_loop(0, planes, update, 0)

    def advance(p, carry):
        d = z_in[p]
        if first:
            sol_ref[p] = step * d
        else:
            d = d + ratio * dir_in[p]
            sol_ref[p] = sol_in[p] + step * d
        dir_ref[p] = d
        return carry

    lax.fori_loop(0, zdim, advance, 0)
    c = dict(
        tx=tx, ty=ty, tz=tz, tzlp=tzlp, tzlm=tzlm, s=s_ref, diag=diag_ref, mxp=mxp, mxm=mxm, my=my,
        strips=strips, d_own=d_own, d_other=d_other, dx=dx, dy_hi=s_hi.at[3 * rows : 3 * rows + xdim, :],
        dy_lo=s_lo.at[3 * rows : 3 * rows + xdim, :], yb=yb, acc=acc, bx=bx,
    )
    finish(c, scaled, strip_q, r_ref, z_ref, send, w_ref, zown, sw, img_ref, ids, last)


def last_kernel(zdim, xdim, got, w_in, z_in, r_in, img_in, dir_in, sol_in, scal_ref, sol_ref, r_ref):
    peers = got.shape[0]
    _, sums = totals([got[p] for p in range(peers)])
    _, ratio, _, step = scalars(sums, scal_ref, False)

    def body(p, carry):
        image = w_in[p] + ratio * img_in[p][:xdim]
        r_ref[p] = r_in[p][:xdim] - step * image
        sol_ref[p] = sol_in[p] + step * (z_in[p] + ratio * dir_in[p])
        return carry

    lax.fori_loop(0, zdim, body, 0)


def call(kernel, name, args, outs, scratch=(), smem=0):
    specs = [pl.BlockSpec(memory_space=pltpu.SMEM)] * smem
    specs += [pl.BlockSpec(memory_space=pltpu.VMEM)] * (len(args) - smem)
    return pl.pallas_call(
        kernel,
        name=name,
        in_specs=specs,
        out_specs=[pl.BlockSpec(memory_space=pltpu.VMEM)] * len(outs),
        out_shape=[jax.ShapeDtypeStruct(o, jnp.float32) for o in outs],
        scratch_shapes=[pltpu.VMEM(s, jnp.float32) for s in scratch],
        compiler_params=pltpu.CompilerParams(vmem_limit_bytes=40 * 1024 * 1024),
    )(*args)


def local(right_side, permeability, storage, deflation, coarse_inverse, owners, margin):
    nx, ny, nz = (lax.axis_size(a) for a in ("gx", "gy", "gz"))
    vectors, zdim, xdim, ydim = deflation.shape
    order = coarse_inverse.shape[1]
    assert nz == 2 and ydim == LANES and 2 * zdim * STRIDE == LANES and vectors == 8
    gx, gy, gz = (lax.axis_index(a) for a in ("gx", "gy", "gz"))
    peers, planes, rows = nx * ny, 2 * zdim, xdim + 8
    me = gx * ny + gy
    off_x = jnp.array([0, 1, -1, 0, 0, 1, 1, -1, -1, 0], jnp.int32) + gx
    off_y = jnp.array([0, 0, 0, 1, -1, 1, -1, 1, -1, 0], jnp.int32) + gy
    there = (off_x >= 0) & (off_x < nx) & (off_y >= 0) & (off_y < ny)
    ids = jnp.where(there, off_x * ny + off_y, me)
    ids = jnp.where(jnp.arange(10) == 9, gz, ids)

    def swap(v):
        return lax.ppermute(v, "gz", [(0, 1), (1, 0)])

    def up(v, axis, count):
        return lax.ppermute(v, axis, [(i, i + 1) for i in range(count - 1)])

    def down(v, axis, count):
        return lax.ppermute(v, axis, [(i + 1, i) for i in range(count - 1)])

    fields = (permeability, storage, right_side)

    def edge_rows(lo, hi, at):
        parts = [v[:, lo:hi, :].reshape(-1, LANES) for v in fields]
        return jnp.concatenate(parts + [deflation[:, :, at, :].reshape(-1, LANES)], axis=0)

    x_lo = up(edge_rows(xdim - 3, xdim, xdim - 1), "gx", nx)
    x_hi = down(edge_rows(0, 3, 0), "gx", nx)
    others = [swap(v) for v in fields]
    d_other = swap(deflation)

    coeffs = jnp.sum(deflation * right_side[None], axis=(1, 2, 3))
    first_row = jnp.concatenate(
        [coeffs, owners.reshape(-1).astype(jnp.float32), margin.reshape(-1).astype(jnp.float32)]
    )
    first_row = jnp.pad(first_row, (0, LANES - first_row.shape[0]))
    table = lax.all_to_all(
        jnp.broadcast_to(first_row[None, None], (peers * nz, 1, LANES)),
        ("gx", "gy", "gz"), 0, 0, tiled=True,
    ).reshape(peers, nz, LANES)
    table = jnp.where(gz == 0, table, table[:, ::-1])
    hot = (ids[:5, None] == jnp.arange(peers)[None, :]).astype(jnp.float32)
    near = jnp.dot(hot, table.reshape(peers, nz * LANES), precision=PRECISE).reshape(5, nz, LANES)
    mt = near[:, :, 16:22].reshape(-1)
    near_owners = near[:, :, 8:16]
    wanted = jnp.concatenate(
        [near_owners[:3].transpose(1, 0, 2).reshape(-1), near_owners[3].reshape(-1), near_owners[4].reshape(-1)]
    )
    numbers = jnp.arange(order, dtype=jnp.float32)
    spare = PERIOD - 2 * vectors
    owner_all = jnp.pad(table[:, :, 8:16].reshape(peers, -1), ((0, 0), (0, spare)), constant_values=-1.0)
    known = jnp.pad(table[:, :, 0:8].reshape(peers, -1), ((0, 0), (0, spare))).reshape(-1, LANES)

    x_hi_other, x_lo_other = swap(x_hi), swap(x_lo)
    split = 3 * zdim * 3
    sides = [(v[:split], v[split:]) for v in (x_hi, x_lo, x_hi_other, x_lo_other)]
    strip_rows = 3 * rows + xdim
    main, strip_hi, strip_lo = call(
        lambda *refs: pack_kernel(zdim, xdim, *refs), "pack",
        [*fields, *others, *(v[0] for v in sides), deflation, d_other],
        [(3, planes, rows, LANES), (strip_rows, LANES), (strip_rows, LANES)],
    )
    dx = [v[1] for v in sides]
    s_lo = up(strip_hi, "gy", ny)
    s_hi = down(strip_lo, "gy", ny)
    whole = lax.all_gather(coarse_inverse, "gx", axis=0, tiled=True)
    select = jnp.dot((wanted[:, None] == numbers[None, :]).astype(jnp.float32), whole, precision=PRECISE)
    pick = (numbers[:, None] == owner_all.reshape(1, -1)).astype(jnp.float32)
    select = jnp.dot(select, pick, precision=PRECISE)

    tiles = known.shape[0]
    full, brick, one = (planes, rows, LANES), (planes, xdim, LANES), (rows, LANES)
    mine, slots = (zdim, xdim, LANES), (peers, SLOT, LANES)
    scratch = [full, full, (10 * vectors, LANES), (PERIOD, LANES), (2, zdim, LANES)]
    (send, w, z, sw, strips, *consts, rs) = call(
        lambda *refs: first_kernel(zdim, xdim, *refs), "first",
        [ids, mt, main, strip_hi, s_hi, s_lo, deflation, d_other, *dx, select, known],
        [slots, brick, mine, (xdim, LANES), (8, *one)] + [full] * 7 + [(2, *one)] * 3 + [one],
        scratch, smem=2,
    )
    state = [main]
    for iteration in range(ITERS - 1):
        first, last = iteration == 0, iteration == ITERS - 2
        got = lax.all_to_all(send, ("gx", "gy"), 0, 0, tiled=True)
        send, w, z, sw, rs, r, img, direct, sol, ist, known, kimg, scal = call(
            lambda *refs: next_kernel(zdim, xdim, first, last, *refs), f"step{iteration}",
            [ids, got, deflation, d_other, *dx, s_hi, s_lo, select, strips, *consts, known, w, z, sw, rs, *state],
            [(peers, 1, LANES) if last else slots, brick, mine, (xdim, LANES), one, full, full, mine, mine, one,
             (tiles, LANES), (tiles, LANES), (8, LANES)],
            scratch + [(planes, 8, LANES)], smem=1,
        )
        state = [r, img, direct, sol, ist, kimg, scal]
    got = lax.all_to_all(send, ("gx", "gy"), 0, 0, tiled=True)
    return tuple(call(
        lambda *refs: last_kernel(zdim, xdim, *refs), "last",
        [got, w, z, r, img, direct, sol, scal], [mine, mine],
    ))


def solution(mesh):
    in_specs = (
        P("gz", "gx", "gy"),
        P("gz", "gx", "gy"),
        P("gz", "gx", "gy"),
        P(None, "gz", "gx", "gy"),
        P("gx", None),
        P("gz", "gx", "gy", None),
        P("gz", "gx", "gy", None),
    )
    out_specs = (P("gz", "gx", "gy"), P("gz", "gx", "gy"))
    return jax.shard_map(local, mesh=mesh, in_specs=in_specs, out_specs=out_specs, check_vma=False)
```

time: 314 us -> 154 us (0.49)
  starting transfers between devices: 150 us -> 20.5 us
  Pallas kernels: 0 us -> 45.9 us
  other arithmetic: 47.8 us -> 6.11 us
  waiting for transfers between devices: 31.7 us -> 0.03 us
  blocking collectives: 44.6 us -> 66 us
  between operations: 13.8 us -> 0.91 us
  local copies, waits for them, and re-layouts: 18.7 us -> 11.6 us
    ppermute x54 -> x10, starting transfers between devices: 138 us -> 13.6 us  [the longest x2 9.09 us: up(): return lax.ppermute(v, axis, [(i, i + 1) for i in range(count - 1)])]
    pallas_call x0 -> x6, Pallas kernels: none -> 45.9 us  [call(): pl.pallas_call(kernel, name=name, in_specs=specs, out_specs=[pl.BlockSpec...]
    ppermute x54 -> x10, waiting for transfers between devices: 24.6 us -> 0.03 us  [the longest x6 0.02 us: swap(): return lax.ppermute(v, 'gz', [(0, 1), (1, 0)])]
    mul x31 -> x0, other arithmetic: 22.9 us -> none  [the longest x24 15.8 us: couplings(): low, high = (low * scale[2 * dim], high * scale[2 * dim + 1])]
    all_to_all x3 -> x4, blocking collectives: 34.6 us -> 55.3 us  [local(): got = lax.all_to_all(send, ('gx', 'gy'), 0, 0, tiled=True)]
    reduce_sum x17 -> x1, other arithmetic: 9.68 us -> 1.95 us  [local(): coeffs = jnp.sum(deflation * right_side[None], axis=(1, 2, 3))]
    all_to_all x2 -> x1, waiting for transfers between devices: 7.09 us -> 0.01 us  [local(): lax.all_to_all(jnp.broadcast_to(first_row[None, None], (peers * nz, 1, LA...]
    concatenate x5 -> x4, other arithmetic: 7.92 us -> 2.14 us  [the longest x2 1.98 us: edge_rows(): jnp.concatenate(parts + [deflation[:, :, at, :].reshape(-1, LANES)], axis=0)]
  transfers between devices with their start and end apart: 56 -> 11, of which waited for: 8 -> 0; matrix products, arithmetic and copies ran while one was open for 7% -> 12% of each run, Pallas kernels for 0% -> 0%
where the time goes in v2:
time: 154 us; the launch traced here: 153 us
  blocking collectives  66 us (43%)
  Pallas kernels  45.9 us (30%)
  starting transfers between devices  20.5 us (13%)
  local copies, waits for them, and re-layouts  11.6 us (8%)
  other arithmetic  6.11 us (4%)
  matrix products  1.72 us (1%)
    all_to_all x4, blocking collectives, local(): got = lax.all_to_all(send, ('gx', 'gy'), 0, 0, tiled=True)  55.3 us
    pallas_call x6, Pallas kernels, call(): pl.pallas_call(kernel, name=name, in_specs=specs, out_specs=[pl.BlockSpec...  45.9 us
    all_gather x1, blocking collectives, local(): whole = lax.all_gather(coarse_inverse, 'gx', axis=0, tiled=True)  10.8 us
    ppermute x2, starting transfers between devices, up(): return lax.ppermute(v, axis, [(i, i + 1) for i in range(count - 1)])  9.09 us
    all_to_all x1, starting transfers between devices, local(): lax.all_to_all(jnp.broadcast_to(first_row[None, None], (peers * nz, 1, LA...  6.96 us
    slice x4, local copies, waits for them, and re-layouts, local(): v[:split]  3.1 us
  transfers between devices with their start and end apart: 11, of which 0 were waited for; matrix products, arithmetic and copies ran while one was open for 12% of the time, Pallas kernels for 0%

profile of v2, /device:TPU:0, one launch (start us, length us, event | category | flops | bytes accessed | tf_op | source)
XLA Modules:
  0.0 152.7 jit_solution(4158672037796645582)
XLA Ops:
  1.2 0.7 convert_bitcast_fusion.1
  2.6 1.9 %multiply_reduce_fusion = f32[8]{0:T(128)S(1)} fusion(f32[8,8,64,128]{3,2,1,0:T(8,128)} %refs_2_.7, f32[8,64,128]{2,1,0:T(8,128)} %refs_2_.4), kind=kLoop, calls=%fused_computation | loop fusion | flops 1048568 | bytes 2359328 | tf_op jit(solution)/shard_map/reduce_sum | solution.py:564
  5.2 7.0 %all-to-all-start = ((f32[32,1,128]{2,1,0:T(1,128)}), f32[32,1,128]{2,1,0:T(1,128)S(1)}, u32[]{:S(2)}, u32[]{:S(2)}) async-start(f32[32,1,128]{2,1,0:T(1,128)} %broadcast_in_dim.12), calls=%async_computation | async-start | bytes 32768 | tf_op jit(solution)/shard_map/all_to_all | solution.py:569
  12.8 0.8 fusion.11
  13.5 0.8 fusion.12
  15.0 1.3 pad_maximum_fusion
  16.4 1.3 collective-permute-start.3
  18.4 4.5 %collective-permute-start.4 = (f32[136,128]{1,0:T(8,128)}, f32[136,128]{1,0:T(8,128)S(1)}, u32[]{:S(2)}, u32[]{:S(2)}) collective-permute-start(f32[136,128]{1,0:T(8,128)} %pad_maximum_fusion.1), channel_id=1, source_target_pairs={{0,8},{8,16},{16,24},{1,9},{9,17},{17,25},{2,10},{10,18},{18,26},{... | collective-permute-start | bytes 208904 | tf_op jit(solution)/shard_map/ppermute | solution.py:548
  22.9 0.7 compare_select_fusion.refs_0_
  23.6 10.8 %all_gather.3 = f32[256,256]{1,0:T(8,128)} all-gather(f32[64,256]{1,0:T(8,128)} %param.13), channel_id=1, replica_groups=mesh['gx'=4,'gy'=4,'gz'=2] {'gx'}, dimensions={0}, use_global_device_ids=true | all-gather | bytes 327680 | tf_op jit(solution)/shard_map/all_gather | solution.py:598
  36.3 1.2 fusion.2
  37.8 0.8 slice.96
  39.2 0.8 slice.97.refs_6_
  40.0 0.8 slice.98.refs_7_
  40.7 0.8 slice.99.refs_8_
  41.5 0.8 slice.100.refs_9_
  42.3 12.0 %pack.1 = (f32[3,16,72,128]{3,2,1,0:T(8,128)S(1)}, f32[280,128]{1,0:T(8,128)S(1)}, f32[280,128]{1,0:T(8,128)S(1)}) custom-call(f32[8,64,128]{2,1,0:T(8,128)S(1)} %copy-done.2, f32[8,64,128]{2,1,0:T(8,128)S(1)} %copy-done.3, f32[8,64,128]{2,1,0:T(8,128)S(1)} %copy-done.1, f32[8,64,128]{2,1,0:T(8,128)S(1)} %collective-permute-done.refs_3_, ...), custom_call_target="tpu_custom_call" | custom-call | tf_op jit(solution)/shard_map/pack/pallas_call | solution.py:519
  54.4 1.3 collective-permute-start.8
  55.7 4.6 %collective-permute-start.9 = (f32[280,128]{1,0:T(8,128)S(1)}, f32[280,128]{1,0:T(8,128)S(1)}, u32[]{:S(2)}, u32[]{:S(2)}) collective-permute-start(f32[280,128]{1,0:T(8,128)S(1)} %get-tuple-element.56.refs_3_), channel_id=1, source_target_pairs={{0,2},{2,4},{4,6},{1,3},{3,5},{5,7},{8,10},{10,12},{12,14},{9,11},... | collective-permute-start | bytes 430088 | tf_op jit(solution)/shard_map/ppermute | solution.py:548
  60.6 0.8 slice.101.refs_8_.refs_4_
  61.3 0.8 slice.102.refs_9_.refs_5_
  62.1 0.8 slice.103.refs_10_.refs_6_
  62.9 0.8 slice.104.refs_11_.refs_7_
  63.6 11.3 %first.1 = (f32[16,40,128]{2,1,0:T(8,128)S(1)}, f32[16,64,128]{2,1,0:T(8,128)S(1)}, f32[8,64,128]{2,1,0:T(8,128)S(1)}, f32[64,128]{1,0:T(8,128)S(1)}, f32[8,72,1...) custom-call(s32[10]{0:T(128)S(1)} %compare_select_fusion.refs_0_, ...), custom_call_target="tpu_custom_call" | custom-call | tf_op jit(solution)/shard_map/first/pallas_call | solution.py:519
  74.9 17.5 %all_to_all.25.refs_1_ = f32[16,40,128]{2,1,0:T(8,128)S(1)} all-to-all(f32[16,40,128]{2,1,0:T(8,128)S(1)} %get-tuple-element.58), channel_id=1, replica_groups=mesh['gx'=4,'gy'=4,'gz'=2] {'gx','gy'}, dimensions={0} | all-to-all | bytes 655360 | tf_op jit(solution)/shard_map/all_to_all | solution.py:616
  92.4 7.2 %step0.1 = (f32[16,40,128]{2,1,0:T(8,128)S(1)}, f32[16,64,128]{2,1,0:T(8,128)S(1)}, f32[8,64,128]{2,1,0:T(8,128)S(1)}, f32[64,128]{1,0:T(8,128)S(1)}, f32[72,128...) custom-call(s32[10]{0:T(128)S(1)} %compare_select_fusion.refs_0_, ...), custom_call_target="tpu_custom_call" | custom-call | tf_op jit(solution)/shard_map/step0/pallas_call | solution.py:519
  99.6 14.0 %all_to_all.26.refs_1_ = f32[16,40,128]{2,1,0:T(8,128)S(1)} all-to-all(f32[16,40,128]{2,1,0:T(8,128)S(1)} %get-tuple-element.74), channel_id=1, replica_groups=mesh['gx'=4,'gy'=4,'gz'=2] {'gx','gy'}, dimensions={0} | all-to-all | bytes 655360 | tf_op jit(solution)/shard_map/all_to_all | solution.py:616
  113.6 7.4 %step1.1 = (f32[16,40,128]{2,1,0:T(8,128)S(1)}, f32[16,64,128]{2,1,0:T(8,128)S(1)}, f32[8,64,128]{2,1,0:T(8,128)S(1)}, f32[64,128]{1,0:T(8,128)S(1)}, f32[72,128...) custom-call(s32[10]{0:T(128)S(1)} %compare_select_fusion.refs_0_, ...), custom_call_target="tpu_custom_call" | custom-call | tf_op jit(solution)/shard_map/step1/pallas_call | solution.py:519
  120.9 13.9 %all_to_all.27.refs_1_ = f32[16,40,128]{2,1,0:T(8,128)S(1)} all-to-all(f32[16,40,128]{2,1,0:T(8,128)S(1)} %get-tuple-element.87), channel_id=1, replica_groups=mesh['gx'=4,'gy'=4,'gz'=2] {'gx','gy'}, dimensions={0} | all-to-all | bytes 655360 | tf_op jit(solution)/shard_map/all_to_all | solution.py:616
  134.8 6.7 %step2.1 = (f32[16,1,128]{2,1,0:T(1,128)S(1)}, f32[16,64,128]{2,1,0:T(8,128)S(1)}, f32[8,64,128]{2,1,0:T(8,128)S(1)}, f32[64,128]{1,0:T(8,128)}, f32[72,128]{1,0...) custom-call(s32[10]{0:T(128)S(1)} %compare_select_fusion.refs_0_, ...), custom_call_target="tpu_custom_call" | custom-call | tf_op jit(solution)/shard_map/step2/pallas_call | solution.py:519
  141.5 10.0 %all_to_all.28.refs_0_ = f32[16,1,128]{2,1,0:T(1,128)S(1)} all-to-all(f32[16,1,128]{2,1,0:T(1,128)S(1)} %get-tuple-element.100), channel_id=1, replica_groups=mesh['gx'=4,'gy'=4,'gz'=2] {'gx','gy'}, dimensions={0} | all-to-all | bytes 16384 | tf_op jit(solution)/shard_map/all_to_all | solution.py:625
  151.5 1.2 last.1
  (66 shorter events, 7.0 us)
Async XLA Ops:
  0.6 22.3 %copy-start.7 = (s32[10]{0:T(128)S(1)}, s32[10]{0:T(128)}, u32[]{:S(2)}) copy-start(s32[10]{0:T(128)} %constant.29.clone) | copy-start | bytes 124
  0.6 14.4 %copy-start = (f32[8,8,64,128]{3,2,1,0:T(8,128)S(1)}, f32[8,8,64,128]{3,2,1,0:T(8,128)}, u32[]{:S(2)}) copy-start(f32[8,8,64,128]{3,2,1,0:T(8,128)} %refs_2_.7) | copy-start | bytes 6291460
  0.7 13.7 %copy-start.1 = (f32[8,64,128]{2,1,0:T(8,128)S(1)}, f32[8,64,128]{2,1,0:T(8,128)}, u32[]{:S(2)}) copy-start(f32[8,64,128]{2,1,0:T(8,128)} %refs_2_.4) | copy-start | bytes 786436
  0.7 41.6 %collective-permute-start.7 = (f32[8,8,64,128]{3,2,1,0:T(8,128)}, f32[8,8,64,128]{3,2,1,0:T(8,128)}, u32[]{:S(2)}, u32[]{:S(2)}) collective-permute-start(f32[8,8,64,128]{3,2,1,0:T(8,128)} %refs_2_.7), channel_id=1, source_target_pairs={{0,1},{1,0},{2,3},{3,2},{4,5},{5,4},{6,7},{7,6},{8,9},{9,8},{10,11... | collective-permute-start | bytes 6291464 | tf_op jit(solution)/shard_map/ppermute | solution.py:545
  2.6 39.7 %copy-start.2 = (f32[8,64,128]{2,1,0:T(8,128)S(1)}, f32[8,64,128]{2,1,0:T(8,128)}, u32[]{:S(2)}) copy-start(f32[8,64,128]{2,1,0:T(8,128)} %refs_0_.1) | copy-start | bytes 786436
  2.6 39.7 %copy-start.3 = (f32[8,64,128]{2,1,0:T(8,128)S(1)}, f32[8,64,128]{2,1,0:T(8,128)}, u32[]{:S(2)}) copy-start(f32[8,64,128]{2,1,0:T(8,128)} %refs_1_.1) | copy-start | bytes 786436
  5.2 29.1 %all-to-all-start = ((f32[32,1,128]{2,1,0:T(1,128)}), f32[32,1,128]{2,1,0:T(1,128)S(1)}, u32[]{:S(2)}, u32[]{:S(2)}) async-start(f32[32,1,128]{2,1,0:T(1,128)} %broadcast_in_dim.12), calls=%async_computation | async-start | bytes 32768 | tf_op jit(solution)/shard_map/all_to_all | solution.py:569
  12.2 30.1 %collective-permute-start = (f32[8,64,128]{2,1,0:T(8,128)}, f32[8,64,128]{2,1,0:T(8,128)S(1)}, u32[]{:S(2)}, u32[]{:S(2)}) collective-permute-start(f32[8,64,128]{2,1,0:T(8,128)} %refs_0_.1), channel_id=1, source_target_pairs={{0,1},{1,0},{2,3},{3,2},{4,5},{5,4},{6,7},{7,6},{8,9},{9,8},{10,11... | collective-permute-start | bytes 786440 | tf_op jit(solution)/shard_map/ppermute | solution.py:545
  12.5 29.8 %collective-permute-start.1 = (f32[8,64,128]{2,1,0:T(8,128)}, f32[8,64,128]{2,1,0:T(8,128)S(1)}, u32[]{:S(2)}, u32[]{:S(2)}) collective-permute-start(f32[8,64,128]{2,1,0:T(8,128)} %refs_1_.1), channel_id=1, source_target_pairs={{0,1},{1,0},{2,3},{3,2},{4,5},{5,4},{6,7},{7,6},{8,9},{9,8},{10,11... | collective-permute-start | bytes 786440 | tf_op jit(solution)/shard_map/ppermute | solution.py:545
  16.4 18.7 %collective-permute-start.3 = (f32[136,128]{1,0:T(8,128)}, f32[136,128]{1,0:T(8,128)}, u32[]{:S(2)}, u32[]{:S(2)}) collective-permute-start(f32[136,128]{1,0:T(8,128)} %pad_maximum_fusion), channel_id=1, source_target_pairs={{8,0},{16,8},{24,16},{9,1},{17,9},{25,17},{10,2},{18,10},{26,18},{... | collective-permute-start | bytes 208904 | tf_op jit(solution)/shard_map/ppermute | solution.py:551
  18.4 16.8 %collective-permute-start.4 = (f32[136,128]{1,0:T(8,128)}, f32[136,128]{1,0:T(8,128)S(1)}, u32[]{:S(2)}, u32[]{:S(2)}) collective-permute-start(f32[136,128]{1,0:T(8,128)} %pad_maximum_fusion.1), channel_id=1, source_target_pairs={{0,8},{8,16},{16,24},{1,9},{9,17},{17,25},{2,10},{10,18},{18,26},{... | collective-permute-start | bytes 208904 | tf_op jit(solution)/shard_map/ppermute | solution.py:548
  34.6 3.1 %copy-start.6 = (f32[5,2,128]{2,0,1:T(8,128)}, f32[5,2,128]{2,0,1:T(8,128)S(1)}, u32[]{:S(2)}) copy-start(f32[5,2,128]{2,0,1:T(8,128)S(1)} %fusion.4) | copy-start | bytes 15364
  35.1 7.2 %collective-permute-start.2 = (f32[8,64,128]{2,1,0:T(8,128)S(1)}, f32[8,64,128]{2,1,0:T(8,128)}, u32[]{:S(2)}, u32[]{:S(2)}) collective-permute-start(f32[8,64,128]{2,1,0:T(8,128)S(1)} %copy-done.1), channel_id=1, source_target_pairs={{0,1},{1,0},{2,3},{3,2},{4,5},{5,4},{6,7},{7,6},{8,9},{9,8},{10,11... | collective-permute-start | bytes 786440 | tf_op jit(solution)/shard_map/ppermute | solution.py:545
  35.1 0.6 copy-start.4
  35.8 1.7 %collective-permute-start.5 = (f32[136,128]{1,0:T(8,128)}, f32[136,128]{1,0:T(8,128)S(1)}, u32[]{:S(2)}, u32[]{:S(2)}) collective-permute-start(f32[136,128]{1,0:T(8,128)} %collective-permute-done.3), channel_id=1, source_target_pairs={{0,1},{1,0},{2,3},{3,2},{4,5},{5,4},{6,7},{7,6},{8,9},{9,8},{10,11... | collective-permute-start | bytes 208904 | tf_op jit(solution)/shard_map/ppermute | solution.py:545
  37.5 1.1 copy-start.5
  37.5 4.0 %collective-permute-start.6 = (f32[136,128]{1,0:T(8,128)}, f32[136,128]{1,0:T(8,128)}, u32[]{:S(2)}, u32[]{:S(2)}) collective-permute-start(f32[136,128]{1,0:T(8,128)} %copy-done.4), channel_id=1, source_target_pairs={{0,1},{1,0},{2,3},{3,2},{4,5},{5,4},{6,7},{7,6},{8,9},{9,8},{10,11... | collective-permute-start | bytes 208904 | tf_op jit(solution)/shard_map/ppermute | solution.py:545
  54.4 9.3 %collective-permute-start.8 = (f32[280,128]{1,0:T(8,128)S(1)}, f32[280,128]{1,0:T(8,128)S(1)}, u32[]{:S(2)}, u32[]{:S(2)}) collective-permute-start(f32[280,128]{1,0:T(8,128)S(1)} %get-tuple-element.57), channel_id=1, source_target_pairs={{2,0},{4,2},{6,4},{3,1},{5,3},{7,5},{10,8},{12,10},{14,12},{11,9},... | collective-permute-start | bytes 430088 | tf_op jit(solution)/shard_map/ppermute | solution.py:551
  55.7 8.0 %collective-permute-start.9 = (f32[280,128]{1,0:T(8,128)S(1)}, f32[280,128]{1,0:T(8,128)S(1)}, u32[]{:S(2)}, u32[]{:S(2)}) collective-permute-start(f32[280,128]{1,0:T(8,128)S(1)} %get-tuple-element.56.refs_3_), channel_id=1, source_target_pairs={{0,2},{2,4},{4,6},{1,3},{3,5},{5,7},{8,10},{10,12},{12,14},{9,11},... | collective-permute-start | bytes 430088 | tf_op jit(solution)/shard_map/ppermute | solution.py:548

commit v3 on v2

--- a/solution.py
+++ b/solution.py
@@ -11,8 +11,6 @@
 LANES = 128
 STRIDE = 8
 PERIOD = 32
-ROW = 32
-SLOT = 40
 
 
 def conduct(first_perm, second_perm):
@@ -28,6 +26,10 @@
     return pltpu.roll(values, shift, axis)
 
 
+def rem(a, b):
+    return a % b if isinstance(a, int) else lax.rem(a, b)
+
+
 def x_next(v):
     return turn(v, -1, 0)
 
@@ -51,6 +53,24 @@
 def place(shape):
     lane = iota(shape, 1)
     return lane >> 3, lane & 7
+
+
+UNROLL = 8
+
+
+def sweep(count, body, carry, unroll=None):
+    unroll = min(count, unroll or UNROLL)
+    if unroll == count:
+        for i in range(count):
+            carry = body(i, carry)
+        return carry
+
+    def several(i, carry):
+        for u in range(unroll):
+            carry = body(i * unroll + u, carry)
+        return carry
+
+    return lax.fori_loop(0, count // unroll, several, carry)
 
 
 def eights(values):
@@ -58,6 +78,73 @@
     for t in range(1, values.shape[0] // 8):
         out = out + values[8 * t : 8 * t + 8]
     return out
+
+
+def spread_row(acc_ref):
+    count = acc_ref.shape[0]
+    column = jnp.broadcast_to(jnp.sum(acc_ref[...], axis=1, keepdims=True), (count, LANES))
+    match = iota((count, LANES), 0) == (iota((count, LANES), 1) & (count - 1))
+    return jnp.sum(jnp.where(match, column, 0.0), axis=0, keepdims=True)
+
+
+def prep_kernel(zdim, xdim, perm, stor, resid, d, owners, margin, row_ref, up_ref, down_ref, acc, line):
+    for f, field in enumerate((perm, stor, resid)):
+        for pz in range(zdim):
+            at = (f * zdim + pz) * 3
+            up_ref[at : at + 3, :] = field[pz, xdim - 3 : xdim, :]
+            down_ref[at : at + 3, :] = field[pz, 0:3, :]
+    vectors = d.shape[0]
+    acc[...] = jnp.zeros(acc.shape, jnp.float32)
+    for k in range(vectors):
+        total = jnp.zeros((8, LANES), jnp.float32)
+        for pz in range(zdim):
+            at = (9 + k) * zdim + pz
+            up_ref[at : at + 1, :] = d[k, pz, xdim - 1 : xdim, :]
+            down_ref[at : at + 1, :] = d[k, pz, 0:1, :]
+            total = total + eights(d[k, pz] * resid[pz])
+        acc[k : k + 1, :] = jnp.sum(total, axis=0, keepdims=True)
+    line[...] = jnp.zeros(line.shape, jnp.float32)
+    line[0:1, 8 : 8 + vectors] = owners[...].astype(jnp.float32)
+    line[0:1, 16:22] = margin[...].astype(jnp.float32)
+    extra = line[0:1, :]
+    extra = extra + turn(extra, PERIOD, 1)
+    extra = extra + turn(extra, 2 * PERIOD, 1)
+    row = spread_row(acc) + extra
+    for p in range(row_ref.shape[0]):
+        row_ref[p] = row
+
+
+def coarse_kernel(ids, table, whole, select, known_ref, near, hot):
+    order = whole.shape[0]
+    zb = ids[9]
+    place_of = (zb, 1 - zb)
+    lane = iota((1, LANES), 1)
+    lane8, sub8 = iota((8, LANES), 1), iota((8, LANES), 0)
+    number = iota((8, order), 1).astype(jnp.float32)
+    near[...] = jnp.zeros(near.shape, jnp.float32)
+    for col in range(5):
+        for b in range(2):
+            row = table[2 * ids[col] + place_of[b]]
+            near[2 * col + b : 2 * col + b + 1, :] = row
+            owner = jnp.sum(jnp.where(lane8 == sub8 + 8, row, 0.0), axis=1, keepdims=True)
+            at = 8 * (3 * b + col if col < 3 else 2 * col + b)
+            hot[at : at + 8, :] = (number == owner).astype(jnp.float32)
+    rows = jnp.dot(hot[...], whole[...], precision=PRECISE, preferred_element_type=jnp.float32)
+    index = iota((order, LANES), 0).astype(jnp.float32)
+    for t in range(known_ref.shape[0]):
+        known = jnp.zeros((1, LANES), jnp.float32)
+        owner = known - 1.0
+        for i in range(4):
+            for b in range(2):
+                row = table[2 * (4 * t + i) + place_of[b]]
+                mine = (lane >> 3) == 4 * i + b
+                known = jnp.where(mine, turn(row, 8 * b, 1), known)
+                owner = jnp.where(mine, turn(row, 8 * b - 8, 1), owner)
+        known_ref[t : t + 1, :] = known
+        pick = (index == owner).astype(jnp.float32)
+        select[:, LANES * t : LANES * (t + 1)] = jnp.dot(
+            rows, pick, precision=PRECISE, preferred_element_type=jnp.float32
+        )
 
 
 def pack_kernel(zdim, xdim, *refs):
@@ -94,12 +181,12 @@
             def body(pz, carry, k=k, b=b, d_ref=d_ref):
                 one, two = carry
                 at = STRIDE * (b * zdim + pz) + k
-                moved = pltpu.roll(d_ref[k, pz], at + 1, 1)
+                moved = turn(d_ref[k, pz], at + 1, 1)
                 one = jnp.where(lane == at, moved, one)
                 two = jnp.where(lane == ((at + 1) & (LANES - 1)), moved, two)
                 return one, two
 
-            hi_acc, lo_acc = lax.fori_loop(0, zdim, body, (hi_acc, lo_acc))
+            hi_acc, lo_acc = sweep(zdim, body, (hi_acc, lo_acc))
     strip_hi[3 * rows : 3 * rows + xdim, :] = hi_acc
     strip_lo[3 * rows : 3 * rows + xdim, :] = turn(lo_acc, -1, 1)
 
@@ -155,7 +242,8 @@
             acc = 0.0
             for k in range(vectors):
                 at = (3 * b + 1 + side) * vectors + k
-                acc = acc + dx[k * zdim : (k + 1) * zdim, :] * yb[at : at + 1, :]
+                start = (9 + k) * zdim
+                acc = acc + dx[start : start + zdim, :] * yb[at : at + 1, :]
             x_rows.append(acc)
         c["bx"][0] = x_rows[0]
         c["bx"][1] = x_rows[1]
@@ -167,9 +255,9 @@
             tx, ty = c["tx"][p], c["ty"][p]
             acc = tx * mxp * x_next(q) + mxm * x_prev(tx * q)
             acc = acc + ty * y_next(q) + y_prev(ty * q)
-            acc = acc + my * pltpu.roll(edge_q, LANES - 6 - STRIDE * p, 1)
-            acc = acc + c["tzlp"][p] * scaled[lax.rem(p + 1, planes)]
-            acc = acc + c["tzlm"][p] * scaled[lax.rem(p + planes - 1, planes)]
+            acc = acc + my * turn(edge_q, LANES - 6 - STRIDE * p, 1)
+            acc = acc + c["tzlp"][p] * scaled[rem(p + 1, planes)]
+            acc = acc + c["tzlm"][p] * scaled[rem(p + planes - 1, planes)]
             z = (2.0 - RELAXATION) * q + c["s"][p] * acc
             field = 0.0
             for k in range(vectors):
@@ -183,7 +271,7 @@
                 zown_ref[pz] = z[:xdim]
             return carry
 
-        lax.fori_loop(0, zdim, body, 0)
+        sweep(zdim, body, 0)
 
     lane = iota((rows, LANES), 1)
     edge = jnp.where((lane == 0) | (lane == LANES - 1), 1.0, 0.0)
@@ -200,11 +288,11 @@
             p = b * zdim + pz
             z = z_ref[p]
             tx, ty = c["tx"][p], c["ty"][p]
-            before = lax.rem(p + planes - 1, planes)
+            before = rem(p + planes - 1, planes)
             acc = tx * x_next(z) + x_prev(tx * z)
             acc = acc + ty * y_next(z) + y_prev(ty * z)
-            acc = acc + edge * pltpu.roll(edge_z, LANES - 6 - STRIDE * p, 1)
-            acc = acc + c["tz"][p] * z_ref[lax.rem(p + 1, planes)]
+            acc = acc + edge * turn(edge_z, LANES - 6 - STRIDE * p, 1)
+            acc = acc + c["tz"][p] * z_ref[rem(p + 1, planes)]
             acc = acc + c["tz"][before] * z_ref[before]
             w = (c["diag"][p] * z - acc)[:xdim]
             z = z[:xdim]
@@ -215,32 +303,29 @@
             if img_ref is not None:
                 zi = zi + eights(img_ref[p][:xdim] * z)
             sums = tuple(sums[k] + eights(d_ref[k, pz] * w) for k in range(vectors))
-            moved = pltpu.roll(w, lax.rem(STRIDE * p + 2, LANES), 1)
+            moved = turn(w, rem(STRIDE * p + 2, LANES), 1)
             packed = jnp.where((plane64 == p) & (slot64 < 4), moved, packed)
             return (rz, zw, zi), sums, packed
 
-        scal, sums, packed = lax.fori_loop(0, zdim, body, (scal, (zero,) * vectors, packed))
+        scal, sums, packed = sweep(zdim, body, (scal, (zero,) * vectors, packed))
         coeffs.extend(sums)
 
     acc_ref = c["acc"]
     acc_ref[...] = jnp.zeros(acc_ref.shape, jnp.float32)
     for j, value in enumerate(coeffs + list(scal)):
         acc_ref[j : j + 1, :] = jnp.sum(value, axis=0, keepdims=True)
-    column = jnp.sum(acc_ref[...], axis=1, keepdims=True)
-    spread = jnp.broadcast_to(column, (PERIOD, LANES))
-    spread = jnp.where(iota((PERIOD, LANES), 0) == (iota((PERIOD, LANES), 1) & (PERIOD - 1)), spread, 0.0)
-    row = jnp.sum(spread, axis=0, keepdims=True)
+    row = spread_row(acc_ref)
     peers = send_ref.shape[0]
     if last:
         for p in range(peers):
             send_ref[p] = row
         return
     for p in range(peers):
-        send_ref[p, ROW : ROW + 1, :] = row
+        send_ref[p, planes, 0:1, :] = row
     sw_ref[...] = packed
     for p in range(planes):
-        send_ref[ids[1], 2 * p : 2 * p + 2, :] = w_ref[p, xdim - 2 : xdim, :]
-        send_ref[ids[2], 2 * p : 2 * p + 2, :] = w_ref[p, 0:2, :]
+        send_ref[ids[1], p] = w_ref[p, xdim - 2 : xdim, :]
+        send_ref[ids[2], p] = w_ref[p, 0:2, :]
     part = xdim // 4
     pair = (iota((part, LANES), 1) & 7) >> 1
     to_hi = jnp.zeros((part, LANES), jnp.float32)
@@ -249,16 +334,17 @@
         rows_g = packed[g * part : (g + 1) * part]
         to_hi = jnp.where(pair == g, turn(rows_g, 2 * g, 1), to_hi)
         to_lo = jnp.where(pair == g, turn(rows_g, 2 * g - 2, 1), to_lo)
-    send_ref[ids[3], 0:part, :] = to_hi
-    send_ref[ids[4], 0:part, :] = to_lo
+    for i in range(part // 2):
+        send_ref[ids[3], i] = to_hi[2 * i : 2 * i + 2]
+        send_ref[ids[4], i] = to_lo[2 * i : 2 * i + 2]
     for i in (5, 6):
-        send_ref[ids[i], 0:1, :] = packed[xdim - 1 : xdim, :]
+        send_ref[ids[i], 0, 0:1, :] = packed[xdim - 1 : xdim, :]
     for i in (7, 8):
-        send_ref[ids[i], 0:1, :] = packed[0:1, :]
+        send_ref[ids[i], 0, 0:1, :] = packed[0:1, :]
 
 
 def first_kernel(zdim, xdim, *refs):
-    (ids, mt, f, s_own, s_hi, s_lo, d_own, d_other) = refs[0:8]
+    (ids, near, f, s_own, s_hi, s_lo, d_own, d_other) = refs[0:8]
     dx = refs[8:12]
     (select, known_ref) = refs[12:14]
     (send, w_ref, zown, sw, strips, tx, ty, tz, tzlp, tzlm, s_ref, diag_ref, mxp, mxm, my, rs_ref) = refs[14:30]
@@ -271,7 +357,8 @@
     cut = jnp.where(zb == 0, planes - 1, zdim - 1)
 
     def mg(col, b, d):
-        return mt[(col * 2 + b) * 6 + d]
+        at = 2 * col + b
+        return near[at : at + 1, 16 + d : 17 + d]
 
     def by_row(b, d):
         return jnp.where(row < xdim, mg(0, b, d), jnp.where(row < xdim + 4, mg(1, b, d), mg(2, b, d)))
@@ -331,13 +418,13 @@
 
     def transmit(p, carry):
         here = f[0, p]
-        after = f[0, lax.rem(p + 1, planes)]
+        after = f[0, rem(p + 1, planes)]
         tx[p] = conduct(here, x_next(here))
         ty[p] = jnp.where(inside, conduct(here, y_next(here)), 0.0)
         tz[p] = conduct(here, after) * jnp.where(p == cut, 0.0, 1.0)
         return carry
 
-    lax.fori_loop(0, planes, transmit, 0)
+    sweep(planes, transmit, 0)
     edge = (lane == 0) | (lane == LANES - 1)
     inner = jnp.zeros(shape, jnp.float32)
     for b in range(2):
@@ -346,19 +433,19 @@
         def diagonal(pz, inner, b=b, m_hi=m_hi, m_lo=m_lo):
             p = b * zdim + pz
             t_x, t_y, t_z = tx[p], ty[p], tz[p]
-            t_b = tz[lax.rem(p + planes - 1, planes)]
+            t_b = tz[rem(p + planes - 1, planes)]
             total = f[1, p] + t_x + x_prev(t_x) + t_y + y_prev(t_y) + t_z + t_b
-            total = total + jnp.where(edge, pltpu.roll(t_in, LANES - 6 - STRIDE * p, 1), 0.0)
+            total = total + jnp.where(edge, turn(t_in, LANES - 6 - STRIDE * p, 1), 0.0)
             relax = jnp.where(total > 0.0, RELAXATION / jnp.where(total > 0.0, total, 1.0), 0.0)
             diag_ref[p] = total
             s_ref[p] = relax
             tzlp[p] = t_z * jnp.where(pz == zdim - 1, m_hi, 1.0)
             tzlm[p] = t_b * jnp.where(pz == 0, m_lo, 1.0)
             scaled[p] = relax * f[2, p]
-            moved = pltpu.roll(relax, lax.rem(STRIDE * p + 2, LANES), 1)
+            moved = turn(relax, rem(STRIDE * p + 2, LANES), 1)
             return jnp.where((plane_of == p) & ((slot_of == 1) | (slot_of == 2)), moved, inner)
 
-        inner = lax.fori_loop(0, zdim, diagonal, inner)
+        inner = sweep(zdim, diagonal, inner)
     ss = jnp.where((slot_of == 1) | (slot_of == 2), inner, ss)
     strips[7] = ss
 
@@ -423,7 +510,7 @@
     plane_of, slot_of = place((rows, LANES))
 
     peers = got.shape[0]
-    tiles, sums = totals([got[p, ROW : ROW + 1, :] for p in range(peers)])
+    tiles, sums = totals([got[p, planes, 0:1, :] for p in range(peers)])
     inner, ratio, curvature, step = scalars(sums, None if first else scal_ref, first)
     scal_out[0:1, :] = jnp.broadcast_to(inner, (1, LANES))
     scal_out[1:2, :] = jnp.broadcast_to(curvature, (1, LANES))
@@ -438,7 +525,10 @@
     solve_coarse(known, select, yb)
 
     part = xdim // 4
-    from_hi, from_lo = got[ids[3], 0:part, :], got[ids[4], 0:part, :]
+    for i in range(part // 2):
+        tiles_ref[0, 2 * i : 2 * i + 2, :] = got[ids[3], i]
+        tiles_ref[1, 2 * i : 2 * i + 2, :] = got[ids[4], i]
+    from_hi, from_lo = tiles_ref[0], tiles_ref[1]
     own = sw_in[...]
     slot_part = slot_of[:part]
     blocks = []
@@ -452,7 +542,7 @@
     slot8, row8 = slot_of[:8], iota((8, LANES), 0)
     tile = jnp.zeros((8, LANES), jnp.float32)
     for i, at, want, shift in ((5, 0, 5, 3), (6, 0, 6, 5), (7, 7, 5, 3), (8, 7, 6, 5)):
-        value = turn(jnp.broadcast_to(got[ids[i], 0:1, :], (8, LANES)), shift, 1)
+        value = turn(jnp.broadcast_to(got[ids[i], 0, 0:1, :], (8, LANES)), shift, 1)
         tile = jnp.where((row8 == at) & (slot8 == want), value, tile)
     ws = jnp.concatenate(blocks + [tile], axis=0)
     ws = jnp.where((slot_of == 0) | (slot_of == 7), 0.0, ws)
@@ -465,11 +555,11 @@
 
     tiles_ref[...] = jnp.zeros(tiles_ref.shape, jnp.float32)
     for p in range(planes):
-        tiles_ref[p, 0:2, :] = got[ids[1], 2 * p : 2 * p + 2, :]
-        tiles_ref[p, 6:8, :] = got[ids[2], 2 * p : 2 * p + 2, :]
+        tiles_ref[p, 0:2, :] = got[ids[1], p]
+        tiles_ref[p, 6:8, :] = got[ids[2], p]
 
     def update(p, carry):
-        image = jnp.concatenate([w_in[p], tiles_ref[p]], axis=0)
+        image = jnp.concatenate([w_in[p], tiles_ref[p, 0:8, :]], axis=0)
         if not first:
             image = image + ratio * img_in[p]
         img_ref[p] = image
@@ -478,7 +568,7 @@
         scaled[p] = s_ref[p] * r
         return carry
 
-    lax.fori_loop(0, planes, update, 0)
+    sweep(planes, update, 0)
 
     def advance(p, carry):
         d = z_in[p]
@@ -490,7 +580,7 @@
         dir_ref[p] = d
         return carry
 
-    lax.fori_loop(0, zdim, advance, 0)
+    sweep(zdim, advance, 0)
     c = dict(
         tx=tx, ty=ty, tz=tz, tzlp=tzlp, tzlm=tzlm, s=s_ref, diag=diag_ref, mxp=mxp, mxm=mxm, my=my,
         strips=strips, d_own=d_own, d_other=d_other, dx=dx, dy_hi=s_hi.at[3 * rows : 3 * rows + xdim, :],
@@ -502,6 +592,7 @@
 def last_kernel(zdim, xdim, got, w_in, z_in, r_in, img_in, dir_in, sol_in, scal_ref, sol_ref, r_ref):
     peers = got.shape[0]
     _, sums = totals([got[p] for p in range(peers)])
+    sums = [0.5 * value for value in sums]
     _, ratio, _, step = scalars(sums, scal_ref, False)
 
     def body(p, carry):
@@ -510,7 +601,7 @@
         sol_ref[p] = sol_in[p] + step * (z_in[p] + ratio * dir_in[p])
         return carry
 
-    lax.fori_loop(0, zdim, body, 0)
+    sweep(zdim, body, 0)
 
 
 def call(kernel, name, args, outs, scratch=(), smem=0):
@@ -551,64 +642,42 @@
         return lax.ppermute(v, axis, [(i + 1, i) for i in range(count - 1)])
 
     fields = (permeability, storage, right_side)
-
-    def edge_rows(lo, hi, at):
-        parts = [v[:, lo:hi, :].reshape(-1, LANES) for v in fields]
-        return jnp.concatenate(parts + [deflation[:, :, at, :].reshape(-1, LANES)], axis=0)
-
-    x_lo = up(edge_rows(xdim - 3, xdim, xdim - 1), "gx", nx)
-    x_hi = down(edge_rows(0, 3, 0), "gx", nx)
     others = [swap(v) for v in fields]
     d_other = swap(deflation)
-
-    coeffs = jnp.sum(deflation * right_side[None], axis=(1, 2, 3))
-    first_row = jnp.concatenate(
-        [coeffs, owners.reshape(-1).astype(jnp.float32), margin.reshape(-1).astype(jnp.float32)]
-    )
-    first_row = jnp.pad(first_row, (0, LANES - first_row.shape[0]))
-    table = lax.all_to_all(
-        jnp.broadcast_to(first_row[None, None], (peers * nz, 1, LANES)),
-        ("gx", "gy", "gz"), 0, 0, tiled=True,
-    ).reshape(peers, nz, LANES)
-    table = jnp.where(gz == 0, table, table[:, ::-1])
-    hot = (ids[:5, None] == jnp.arange(peers)[None, :]).astype(jnp.float32)
-    near = jnp.dot(hot, table.reshape(peers, nz * LANES), precision=PRECISE).reshape(5, nz, LANES)
-    mt = near[:, :, 16:22].reshape(-1)
-    near_owners = near[:, :, 8:16]
-    wanted = jnp.concatenate(
-        [near_owners[:3].transpose(1, 0, 2).reshape(-1), near_owners[3].reshape(-1), near_owners[4].reshape(-1)]
-    )
-    numbers = jnp.arange(order, dtype=jnp.float32)
-    spare = PERIOD - 2 * vectors
-    owner_all = jnp.pad(table[:, :, 8:16].reshape(peers, -1), ((0, 0), (0, spare)), constant_values=-1.0)
-    known = jnp.pad(table[:, :, 0:8].reshape(peers, -1), ((0, 0), (0, spare))).reshape(-1, LANES)
-
-    x_hi_other, x_lo_other = swap(x_hi), swap(x_lo)
-    split = 3 * zdim * 3
-    sides = [(v[:split], v[split:]) for v in (x_hi, x_lo, x_hi_other, x_lo_other)]
+    edge_rows = ((9 + vectors) * zdim, LANES)
+    first_row, x_up, x_down = call(
+        lambda *refs: prep_kernel(zdim, xdim, *refs), "prep",
+        [*fields, deflation, owners.reshape(1, -1), margin.reshape(1, -1)],
+        [(peers * nz, 1, LANES), edge_rows, edge_rows],
+        [(PERIOD, LANES), (8, LANES)],
+    )
+    x_lo, x_hi = up(x_up, "gx", nx), down(x_down, "gx", nx)
+    table = lax.all_to_all(first_row, ("gx", "gy", "gz"), 0, 0, tiled=True)
+    dx = [x_hi, x_lo, swap(x_hi), swap(x_lo)]
     strip_rows = 3 * rows + xdim
     main, strip_hi, strip_lo = call(
         lambda *refs: pack_kernel(zdim, xdim, *refs), "pack",
-        [*fields, *others, *(v[0] for v in sides), deflation, d_other],
+        [*fields, *others, *dx, deflation, d_other],
         [(3, planes, rows, LANES), (strip_rows, LANES), (strip_rows, LANES)],
     )
-    dx = [v[1] for v in sides]
     s_lo = up(strip_hi, "gy", ny)
     s_hi = down(strip_lo, "gy", ny)
+    coarse_inverse, _ = lax.optimization_barrier((coarse_inverse, strip_hi))
     whole = lax.all_gather(coarse_inverse, "gx", axis=0, tiled=True)
-    select = jnp.dot((wanted[:, None] == numbers[None, :]).astype(jnp.float32), whole, precision=PRECISE)
-    pick = (numbers[:, None] == owner_all.reshape(1, -1)).astype(jnp.float32)
-    select = jnp.dot(select, pick, precision=PRECISE)
-
-    tiles = known.shape[0]
+    tiles = peers * PERIOD // LANES
+    select, known, near = call(
+        coarse_kernel, "coarse", [ids, table, whole],
+        [(10 * vectors, peers * PERIOD), (tiles, LANES), (16, LANES)],
+        [(10 * vectors, order)], smem=1,
+    )
     full, brick, one = (planes, rows, LANES), (planes, xdim, LANES), (rows, LANES)
-    mine, slots = (zdim, xdim, LANES), (peers, SLOT, LANES)
+    mine, slots = (zdim, xdim, LANES), (peers, planes + 1, 2, LANES)
     scratch = [full, full, (10 * vectors, LANES), (PERIOD, LANES), (2, zdim, LANES)]
     (send, w, z, sw, strips, *consts, rs) = call(
         lambda *refs: first_kernel(zdim, xdim, *refs), "first",
-        [ids, mt, main, strip_hi, s_hi, s_lo, deflation, d_other, *dx, select, known],
+        [ids, near, main, strip_hi, s_hi, s_lo, deflation, d_other, *dx, select, known],
         [slots, brick, mine, (xdim, LANES), (8, *one)] + [full] * 7 + [(2, *one)] * 3 + [one],
-        scratch, smem=2,
+        scratch, smem=1,
     )
     state = [main]
     for iteration in range(ITERS - 1):
@@ -617,12 +686,12 @@
         send, w, z, sw, rs, r, img, direct, sol, ist, known, kimg, scal = call(
             lambda *refs: next_kernel(zdim, xdim, first, last, *refs), f"step{iteration}",
             [ids, got, deflation, d_other, *dx, s_hi, s_lo, select, strips, *consts, known, w, z, sw, rs, *state],
-            [(peers, 1, LANES) if last else slots, brick, mine, (xdim, LANES), one, full, full, mine, mine, one,
+            [(peers * nz, 1, LANES) if last else slots, brick, mine, (xdim, LANES), one, full, full, mine, mine, one,
              (tiles, LANES), (tiles, LANES), (8, LANES)],
-            scratch + [(planes, 8, LANES)], smem=1,
+            scratch + [(planes, max(8, xdim // 4), LANES)], smem=1,
         )
         state = [r, img, direct, sol, ist, kimg, scal]
-    got = lax.all_to_all(send, ("gx", "gy"), 0, 0, tiled=True)
+    got = lax.all_to_all(send, ("gx", "gy", "gz"), 0, 0, tiled=True)
     return tuple(call(
         lambda *refs: last_kernel(zdim, xdim, *refs), "last",
         [got, w, z, r, img, direct, sol, scal], [mine, mine],

time: 154 us -> 119 us (0.77)
  Pallas kernels: 45.9 us -> 28.7 us
  blocking collectives: 66 us -> 55.9 us
  waiting for transfers between devices: 0.03 us -> 8.47 us
  other arithmetic: 6.11 us -> 0.01 us
  local copies, waits for them, and re-layouts: 11.6 us -> 5.59 us
  matrix products: 1.72 us -> 0 us
  starting transfers between devices: 20.5 us -> 18.8 us
    all_to_all x4 -> x3, blocking collectives: 55.3 us -> 37.6 us  [local(): got = lax.all_to_all(send, ('gx', 'gy'), 0, 0, tiled=True)]
    pallas_call x6 -> x8, Pallas kernels: 45.9 us -> 28.7 us  [call(): pl.pallas_call(kernel, name=name, in_specs=specs, out_specs=[pl.BlockSpec...]
    all_to_all x0 -> x1, blocking collectives: none -> 8.98 us  [local(): got = lax.all_to_all(send, ('gx', 'gy', 'gz'), 0, 0, tiled=True)]
    slice x18 -> x0, local copies, waits for them, and re-layouts: 8.85 us -> none  [the longest x4 3.1 us: local(): v[:split]]
    ppermute x2, waiting for transfers between devices: 0.01 us -> 5.28 us  [down(): return lax.ppermute(v, axis, [(i + 1, i) for i in range(count - 1)])]
    unnamed x18 -> x20, local copies, waits for them, and re-layouts: 0.81 us -> 5.59 us
    concatenate x4 -> x0, other arithmetic: 2.14 us -> none  [the longest x2 1.98 us: edge_rows(): jnp.concatenate(parts + [deflation[:, :, at, :].reshape(-1, LANES)], axis=0)]
    reduce_sum x1 -> x0, other arithmetic: 1.95 us -> none  [local(): coeffs = jnp.sum(deflation * right_side[None], axis=(1, 2, 3))]
  transfers between devices with their start and end apart: 11 -> 11, of which waited for: 0 -> 3; matrix products, arithmetic and copies ran while one was open for 12% -> 0% of each run, Pallas kernels for 0% -> 6%
where the time goes in v3:
time: 119 us; the launch traced here: 118 us
  blocking collectives  55.9 us (47%)
  Pallas kernels  28.7 us (24%)
  starting transfers between devices  18.8 us (16%)
  waiting for transfers between devices  8.47 us (7%)
  local copies, waits for them, and re-layouts  5.59 us (5%)
    all_to_all x3, blocking collectives, local(): got = lax.all_to_all(send, ('gx', 'gy'), 0, 0, tiled=True)  37.6 us
    pallas_call x8, Pallas kernels, call(): pl.pallas_call(kernel, name=name, in_specs=specs, out_specs=[pl.BlockSpec...  28.7 us
    all_gather x1, blocking collectives, local(): whole = lax.all_gather(coarse_inverse, 'gx', axis=0, tiled=True)  9.24 us
    ppermute x2, starting transfers between devices, up(): return lax.ppermute(v, axis, [(i, i + 1) for i in range(count - 1)])  9.08 us
    all_to_all x1, blocking collectives, local(): got = lax.all_to_all(send, ('gx', 'gy', 'gz'), 0, 0, tiled=True)  8.98 us
    all_to_all x1, starting transfers between devices, local(): table = lax.all_to_all(first_row, ('gx', 'gy', 'gz'), 0, 0, tiled=True)  5.8 us
    unnamed x20, local copies, waits for them, and re-layouts  5.59 us
    ppermute x2, waiting for transfers between devices, down(): return lax.ppermute(v, axis, [(i + 1, i) for i in range(count - 1)])  5.28 us
  transfers between devices with their start and end apart: 11, of which 3 were waited for; matrix products, arithmetic and copies ran while one was open for 0% of the time, Pallas kernels for 6%

profile of v3, /device:TPU:0, one launch (start us, length us, event | category | flops | bytes accessed | tf_op | source)
XLA Modules:
  0.0 118.3 jit_solution(11093291788581323676)
XLA Ops:
  0.6 0.6 collective-permute-start.7
  1.2 1.6 %copy-done = f32[8,8,64,128]{3,2,1,0:T(8,128)S(1)} copy-done((f32[8,8,64,128]{3,2,1,0:T(8,128)S(1)}, f32[8,8,64,128]{3,2,1,0:T(8,128)}, u32[]{:S(2)}) %copy-start) | copy-done | bytes 2097176
  2.8 0.7 copy-done.5
  3.4 0.7 copy-done.6
  4.1 2.1 %prep.1 = (f32[32,1,128]{2,1,0:T(1,128)}, f32[136,128]{1,0:T(8,128)S(1)}, f32[136,128]{1,0:T(8,128)S(1)}) custom-call(f32[8,64,128]{2,1,0:T(8,128)} %refs_0_.3, f32[8,64,128]{2,1,0:T(8,128)} %refs_1_.3, f32[8,64,128]{2,1,0:T(8,128)} %refs_2_.6, f32[8,8,64,128]{3,2,1,0:T(8,128)S(1)} %copy-done, s32[1,8]{1,0:T(1,128)S(1)} %bitcast.2, s32[1,6]{1,0:T(1,128)S(1)} %bitcast.3), custom_call_target="tpu_custom_call" | custom-call | tf_op jit(solution)/shard_map/prep/pallas_call | solution.py:610
  6.2 1.3 %collective-permute-start.3 = (f32[136,128]{1,0:T(8,128)S(1)}, f32[136,128]{1,0:T(8,128)S(1)}, u32[]{:S(2)}, u32[]{:S(2)}) collective-permute-start(f32[136,128]{1,0:T(8,128)S(1)} %get-tuple-element.63), channel_id=1, source_target_pairs={{8,0},{16,8},{24,16},{9,1},{17,9},{25,17},{10,2},{18,10},{26,18},{... | collective-permute-start | bytes 208904 | tf_op jit(solution)/shard_map/ppermute | solution.py:642
  7.5 0.1 collective-permute-start.2
  7.6 0.5 collective-permute-start
  8.1 0.1 collective-permute-start.1
  8.2 5.3 %collective-permute-done.3.refs_6_.refs_8_.refs_4_ = f32[136,128]{1,0:T(8,128)S(1)} collective-permute-done((f32[136,128]{1,0:T(8,128)S(1)}, f32[136,128]{1,0:T(8,128)S(1)}, u32[]{:S(2)}, u32[]{:S(2)}) %collective-permute-start.3) | collective-permute-done | bytes 69664 | tf_op jit(solution)/shard_map/ppermute | solution.py:642
  13.5 4.5 %collective-permute-start.4 = (f32[136,128]{1,0:T(8,128)S(1)}, f32[136,128]{1,0:T(8,128)S(1)}, u32[]{:S(2)}, u32[]{:S(2)}) collective-permute-start(f32[136,128]{1,0:T(8,128)S(1)} %get-tuple-element.64), channel_id=1, source_target_pairs={{0,8},{8,16},{16,24},{1,9},{9,17},{17,25},{2,10},{10,18},{18,26},{... | collective-permute-start | bytes 208904 | tf_op jit(solution)/shard_map/ppermute | solution.py:639
  18.0 1.9 %collective-permute-done.4.refs_7_.refs_9_.refs_5_ = f32[136,128]{1,0:T(8,128)S(1)} collective-permute-done((f32[136,128]{1,0:T(8,128)S(1)}, f32[136,128]{1,0:T(8,128)S(1)}, u32[]{:S(2)}, u32[]{:S(2)}) %collective-permute-start.4) | collective-permute-done | bytes 69664 | tf_op jit(solution)/shard_map/ppermute | solution.py:639
  19.9 1.3 %collective-permute-done.5.refs_8_.refs_10_.refs_6_ = f32[136,128]{1,0:T(8,128)S(1)} collective-permute-done((f32[136,128]{1,0:T(8,128)S(1)}, f32[136,128]{1,0:T(8,128)S(1)}, u32[]{:S(2)}, u32[]{:S(2)}) %collective-permute-start.5) | collective-permute-done | bytes 69664 | tf_op jit(solution)/shard_map/ppermute | solution.py:636
  21.2 0.2 collective-permute-start.6
  21.3 5.8 %all-to-all-start = ((f32[32,1,128]{2,1,0:T(1,128)}), f32[32,1,128]{2,1,0:T(1,128)S(1)}, u32[]{:S(2)}, u32[]{:S(2)}) async-start(f32[32,1,128]{2,1,0:T(1,128)} %get-tuple-element.62), calls=%async_computation | async-start | bytes 32768 | tf_op jit(solution)/shard_map/all_to_all | solution.py:655
  27.2 0.0 copy-start.9
  27.2 3.6 %pack.1 = (f32[3,16,72,128]{3,2,1,0:T(8,128)S(1)}, f32[280,128]{1,0:T(8,128)S(1)}, f32[280,128]{1,0:T(8,128)S(1)}) custom-call(f32[8,64,128]{2,1,0:T(8,128)} %refs_0_.3, f32[8,64,128]{2,1,0:T(8,128)} %refs_1_.3, f32[8,64,128]{2,1,0:T(8,128)} %refs_2_.6, f32[8,64,128]{2,1,0:T(8,128)S(1)} %collective-permute-done.refs_3_, ...), custom_call_target="tpu_custom_call" | custom-call | tf_op jit(solution)/shard_map/pack/pallas_call | solution.py:610
  30.8 1.2 %copy-done.2 = f32[3,16,72,128]{3,2,1,0:T(8,128)} copy-done((f32[3,16,72,128]{3,2,1,0:T(8,128)}, f32[3,16,72,128]{3,2,1,0:T(8,128)S(1)}, u32[]{:S(2)}) %copy-start.2) | copy-done | bytes 1769496
  32.0 1.3 %collective-permute-start.8 = (f32[280,128]{1,0:T(8,128)S(1)}, f32[280,128]{1,0:T(8,128)S(1)}, u32[]{:S(2)}, u32[]{:S(2)}) collective-permute-start(f32[280,128]{1,0:T(8,128)S(1)} %get-tuple-element.69), channel_id=1, source_target_pairs={{2,0},{4,2},{6,4},{3,1},{5,3},{7,5},{10,8},{12,10},{14,12},{11,9},... | collective-permute-start | bytes 430088 | tf_op jit(solution)/shard_map/ppermute | solution.py:642
  33.3 4.6 %collective-permute-start.9 = (f32[280,128]{1,0:T(8,128)S(1)}, f32[280,128]{1,0:T(8,128)S(1)}, u32[]{:S(2)}, u32[]{:S(2)}) collective-permute-start(f32[280,128]{1,0:T(8,128)S(1)} %get-tuple-element.65.refs_3_), channel_id=1, source_target_pairs={{0,2},{2,4},{4,6},{1,3},{3,5},{5,7},{8,10},{10,12},{12,14},{9,11},... | collective-permute-start | bytes 430088 | tf_op jit(solution)/shard_map/ppermute | solution.py:639
  37.9 9.2 %all_gather.3.whole = f32[256,256]{1,0:T(8,128)S(1)} all-gather(f32[64,256]{1,0:T(8,128)S(1)} %copy-done.7), channel_id=1, replica_groups=mesh['gx'=4,'gy'=4,'gz'=2] {'gx'}, dimensions={0}, use_global_device_ids=true | all-gather | bytes 327680 | tf_op jit(solution)/shard_map/all_gather | solution.py:666
  47.2 1.4 %coarse.1 = (f32[80,512]{1,0:T(8,128)S(1)}, f32[4,128]{1,0:T(4,128)S(1)}, f32[16,128]{1,0:T(8,128)S(1)}) custom-call(s32[10]{0:T(128)S(1)} %compare_select_fusion.ids.refs_0_, f32[32,1,128]{2,1,0:T(1,128)S(1)} %all-to-all-done.table, f32[256,256]{1,0:T(8,128)S(1)} %all_gather.3.whole), custom_call_target="tpu_custom_call" | custom-call | tf_op jit(solution)/shard_map/coarse/pallas_call | solution.py:610
  48.6 1.5 %copy-done.3 = f32[3,16,72,128]{3,2,1,0:T(8,128)S(1)} copy-done((f32[3,16,72,128]{3,2,1,0:T(8,128)S(1)}, f32[3,16,72,128]{3,2,1,0:T(8,128)}, u32[]{:S(2)}) %copy-start.3) | copy-done | bytes 1769496
  50.1 6.9 %first.1 = (f32[16,17,2,128]{3,2,1,0:T(2,128)S(1)}, f32[16,64,128]{2,1,0:T(8,128)S(1)}, f32[8,64,128]{2,1,0:T(8,128)S(1)}, f32[64,128]{1,0:T(8,128)S(1)}, f32[8,...) custom-call(s32[10]{0:T(128)S(1)} %compare_select_fusion.ids.refs_0_, ...), custom_call_target="tpu_custom_call" | custom-call | tf_op jit(solution)/shard_map/first/pallas_call | solution.py:610
  57.0 13.6 %all_to_all.25.refs_1_ = f32[16,17,2,128]{3,2,1,0:T(2,128)S(1)} all-to-all(f32[16,17,2,128]{3,2,1,0:T(2,128)S(1)} %get-tuple-element.72), channel_id=1, replica_groups=mesh['gx'=4,'gy'=4,'gz'=2] {'gx','gy'}, dimensions={0} | all-to-all | bytes 557056 | tf_op jit(solution)/shard_map/all_to_all | solution.py:685
  70.6 4.5 %step0.1 = (f32[16,17,2,128]{3,2,1,0:T(2,128)S(1)}, f32[16,64,128]{2,1,0:T(8,128)S(1)}, f32[8,64,128]{2,1,0:T(8,128)S(1)}, f32[64,128]{1,0:T(8,128)S(1)}, f32[72...) custom-call(s32[10]{0:T(128)S(1)} %compare_select_fusion.ids.refs_0_, ...), custom_call_target="tpu_custom_call" | custom-call | tf_op jit(solution)/shard_map/step0/pallas_call | solution.py:610
  75.1 12.0 %all_to_all.26.refs_1_ = f32[16,17,2,128]{3,2,1,0:T(2,128)S(1)} all-to-all(f32[16,17,2,128]{3,2,1,0:T(2,128)S(1)} %get-tuple-element.88), channel_id=1, replica_groups=mesh['gx'=4,'gy'=4,'gz'=2] {'gx','gy'}, dimensions={0} | all-to-all | bytes 557056 | tf_op jit(solution)/shard_map/all_to_all | solution.py:685
  87.1 4.6 %step1.1 = (f32[16,17,2,128]{3,2,1,0:T(2,128)S(1)}, f32[16,64,128]{2,1,0:T(8,128)S(1)}, f32[8,64,128]{2,1,0:T(8,128)S(1)}, f32[64,128]{1,0:T(8,128)S(1)}, f32[72...) custom-call(s32[10]{0:T(128)S(1)} %compare_select_fusion.ids.refs_0_, ...), custom_call_target="tpu_custom_call" | custom-call | tf_op jit(solution)/shard_map/step1/pallas_call | solution.py:610
  91.7 12.0 %all_to_all.27.refs_1_ = f32[16,17,2,128]{3,2,1,0:T(2,128)S(1)} all-to-all(f32[16,17,2,128]{3,2,1,0:T(2,128)S(1)} %get-tuple-element.101), channel_id=1, replica_groups=mesh['gx'=4,'gy'=4,'gz'=2] {'gx','gy'}, dimensions={0} | all-to-all | bytes 557056 | tf_op jit(solution)/shard_map/all_to_all | solution.py:685
  103.7 4.6 %step2.1 = (f32[32,1,128]{2,1,0:T(1,128)S(1)}, f32[16,64,128]{2,1,0:T(8,128)S(1)}, f32[8,64,128]{2,1,0:T(8,128)S(1)}, f32[64,128]{1,0:T(8,128)}, f32[72,128]{1,0...) custom-call(s32[10]{0:T(128)S(1)} %compare_select_fusion.ids.refs_0_, ...), custom_call_target="tpu_custom_call" | custom-call | tf_op jit(solution)/shard_map/step2/pallas_call | solution.py:610
  108.3 9.0 %all_to_all.28.refs_0_ = f32[32,1,128]{2,1,0:T(1,128)S(1)} all-to-all(f32[32,1,128]{2,1,0:T(1,128)S(1)} %get-tuple-element.114), channel_id=1, replica_groups=mesh['gx'=4,'gy'=4,'gz'=2] {'gx','gy','gz'}, dimensions={0} | all-to-all | bytes 32768 | tf_op jit(solution)/shard_map/all_to_all | solution.py:694
  117.3 1.0 last.1
  (24 shorter events, 0.1 us)
Async XLA Ops:
  0.6 26.6 %collective-permute-start.7 = (f32[8,8,64,128]{3,2,1,0:T(8,128)}, f32[8,8,64,128]{3,2,1,0:T(8,128)}, u32[]{:S(2)}, u32[]{:S(2)}) collective-permute-start(f32[8,8,64,128]{3,2,1,0:T(8,128)} %refs_2_.9), channel_id=1, source_target_pairs={{0,1},{1,0},{2,3},{3,2},{4,5},{5,4},{6,7},{7,6},{8,9},{9,8},{10,11... | collective-permute-start | bytes 6291464 | tf_op jit(solution)/shard_map/ppermute | solution.py:636
  1.2 1.6 %copy-start = (f32[8,8,64,128]{3,2,1,0:T(8,128)S(1)}, f32[8,8,64,128]{3,2,1,0:T(8,128)}, u32[]{:S(2)}) copy-start(f32[8,8,64,128]{3,2,1,0:T(8,128)} %refs_2_.9) | copy-start | bytes 6291460
  2.8 0.7 copy-start.5
  3.4 0.7 copy-start.6
  4.1 23.1 %copy-start.1 = (f32[8,8,64,128]{3,2,1,0:T(8,128)S(1)}, f32[8,8,64,128]{3,2,1,0:T(8,128)}, u32[]{:S(2)}) copy-start(f32[8,8,64,128]{3,2,1,0:T(8,128)} %refs_2_.9) | copy-start | bytes 6291460
  6.2 7.2 %collective-permute-start.3 = (f32[136,128]{1,0:T(8,128)S(1)}, f32[136,128]{1,0:T(8,128)S(1)}, u32[]{:S(2)}, u32[]{:S(2)}) collective-permute-start(f32[136,128]{1,0:T(8,128)S(1)} %get-tuple-element.63), channel_id=1, source_target_pairs={{8,0},{16,8},{24,16},{9,1},{17,9},{25,17},{10,2},{18,10},{26,18},{... | collective-permute-start | bytes 208904 | tf_op jit(solution)/shard_map/ppermute | solution.py:642
  7.5 19.7 %collective-permute-start.2 = (f32[8,64,128]{2,1,0:T(8,128)}, f32[8,64,128]{2,1,0:T(8,128)S(1)}, u32[]{:S(2)}, u32[]{:S(2)}) collective-permute-start(f32[8,64,128]{2,1,0:T(8,128)} %refs_2_.6), channel_id=1, source_target_pairs={{0,1},{1,0},{2,3},{3,2},{4,5},{5,4},{6,7},{7,6},{8,9},{9,8},{10,11... | collective-permute-start | bytes 786440 | tf_op jit(solution)/shard_map/ppermute | solution.py:636
  7.6 19.6 %collective-permute-start = (f32[8,64,128]{2,1,0:T(8,128)}, f32[8,64,128]{2,1,0:T(8,128)S(1)}, u32[]{:S(2)}, u32[]{:S(2)}) collective-permute-start(f32[8,64,128]{2,1,0:T(8,128)} %refs_0_.3), channel_id=1, source_target_pairs={{0,1},{1,0},{2,3},{3,2},{4,5},{5,4},{6,7},{7,6},{8,9},{9,8},{10,11... | collective-permute-start | bytes 786440 | tf_op jit(solution)/shard_map/ppermute | solution.py:636
  8.1 19.1 %collective-permute-start.1 = (f32[8,64,128]{2,1,0:T(8,128)}, f32[8,64,128]{2,1,0:T(8,128)S(1)}, u32[]{:S(2)}, u32[]{:S(2)}) collective-permute-start(f32[8,64,128]{2,1,0:T(8,128)} %refs_1_.3), channel_id=1, source_target_pairs={{0,1},{1,0},{2,3},{3,2},{4,5},{5,4},{6,7},{7,6},{8,9},{9,8},{10,11... | collective-permute-start | bytes 786440 | tf_op jit(solution)/shard_map/ppermute | solution.py:636
  13.5 6.5 %collective-permute-start.4 = (f32[136,128]{1,0:T(8,128)S(1)}, f32[136,128]{1,0:T(8,128)S(1)}, u32[]{:S(2)}, u32[]{:S(2)}) collective-permute-start(f32[136,128]{1,0:T(8,128)S(1)} %get-tuple-element.64), channel_id=1, source_target_pairs={{0,8},{8,16},{16,24},{1,9},{9,17},{17,25},{2,10},{10,18},{18,26},{... | collective-permute-start | bytes 208904 | tf_op jit(solution)/shard_map/ppermute | solution.py:639
  19.9 1.3 %collective-permute-start.5 = (f32[136,128]{1,0:T(8,128)S(1)}, f32[136,128]{1,0:T(8,128)S(1)}, u32[]{:S(2)}, u32[]{:S(2)}) collective-permute-start(f32[136,128]{1,0:T(8,128)S(1)} %collective-permute-done.3.refs_6_.refs_8_.refs_4_), channel_id=1, source_target_pairs={{0,1},{1,0},{2,3},{3,2},{4,5},{5,4},{6,7},{7,6},{8,9},{9,8},{10,11... | collective-permute-start | bytes 208904 | tf_op jit(solution)/shard_map/ppermute | solution.py:636
  21.2 6.0 %collective-permute-start.6 = (f32[136,128]{1,0:T(8,128)S(1)}, f32[136,128]{1,0:T(8,128)S(1)}, u32[]{:S(2)}, u32[]{:S(2)}) collective-permute-start(f32[136,128]{1,0:T(8,128)S(1)} %collective-permute-done.4.refs_7_.refs_9_.refs_5_), channel_id=1, source_target_pairs={{0,1},{1,0},{2,3},{3,2},{4,5},{5,4},{6,7},{7,6},{8,9},{9,8},{10,11... | collective-permute-start | bytes 208904 | tf_op jit(solution)/shard_map/ppermute | solution.py:636
  21.3 25.8 %all-to-all-start = ((f32[32,1,128]{2,1,0:T(1,128)}), f32[32,1,128]{2,1,0:T(1,128)S(1)}, u32[]{:S(2)}, u32[]{:S(2)}) async-start(f32[32,1,128]{2,1,0:T(1,128)} %get-tuple-element.62), calls=%async_computation | async-start | bytes 32768 | tf_op jit(solution)/shard_map/all_to_all | solution.py:655
  27.1 10.7 %copy-start.8 = (s32[10]{0:T(128)S(1)}, s32[10]{0:T(128)}, u32[]{:S(2)}) copy-start(s32[10]{0:T(128)} %constant.23.clone) | copy-start | bytes 124
  27.2 10.7 %copy-start.9 = (s32[10]{0:T(128)S(1)}, s32[10]{0:T(128)}, u32[]{:S(2)}) copy-start(s32[10]{0:T(128)} %constant.22.clone) | copy-start | bytes 124
  27.2 10.7 %copy-start.7 = (f32[64,256]{1,0:T(8,128)S(1)}, f32[64,256]{1,0:T(8,128)}, u32[]{:S(2)}) copy-start(f32[64,256]{1,0:T(8,128)} %param.13) | copy-start | bytes 196612
  30.8 1.2 %copy-start.2 = (f32[3,16,72,128]{3,2,1,0:T(8,128)}, f32[3,16,72,128]{3,2,1,0:T(8,128)S(1)}, u32[]{:S(2)}) copy-start(f32[3,16,72,128]{3,2,1,0:T(8,128)S(1)} %get-tuple-element.68.refs_2_.refs_27_) | copy-start | bytes 5308420
  32.0 16.6 %collective-permute-start.8 = (f32[280,128]{1,0:T(8,128)S(1)}, f32[280,128]{1,0:T(8,128)S(1)}, u32[]{:S(2)}, u32[]{:S(2)}) collective-permute-start(f32[280,128]{1,0:T(8,128)S(1)} %get-tuple-element.69), channel_id=1, source_target_pairs={{2,0},{4,2},{6,4},{3,1},{5,3},{7,5},{10,8},{12,10},{14,12},{11,9},... | collective-permute-start | bytes 430088 | tf_op jit(solution)/shard_map/ppermute | solution.py:642
  33.3 15.3 %collective-permute-start.9 = (f32[280,128]{1,0:T(8,128)S(1)}, f32[280,128]{1,0:T(8,128)S(1)}, u32[]{:S(2)}, u32[]{:S(2)}) collective-permute-start(f32[280,128]{1,0:T(8,128)S(1)} %get-tuple-element.65.refs_3_), channel_id=1, source_target_pairs={{0,2},{2,4},{4,6},{1,3},{3,5},{5,7},{8,10},{10,12},{12,14},{9,11},... | collective-permute-start | bytes 430088 | tf_op jit(solution)/shard_map/ppermute | solution.py:639
  48.6 1.5 %copy-start.3 = (f32[3,16,72,128]{3,2,1,0:T(8,128)S(1)}, f32[3,16,72,128]{3,2,1,0:T(8,128)}, u32[]{:S(2)}) copy-start(f32[3,16,72,128]{3,2,1,0:T(8,128)} %copy-done.2) | copy-start | bytes 5308420
  50.1 20.5 %copy-start.4 = (f32[3,16,72,128]{3,2,1,0:T(8,128)S(1)}, f32[3,16,72,128]{3,2,1,0:T(8,128)}, u32[]{:S(2)}) copy-start(f32[3,16,72,128]{3,2,1,0:T(8,128)} %copy-done.2) | copy-start | bytes 5308420

commit v4 on v3

v4 whole, which is shorter than its diff:
```python
import jax
import jax.numpy as jnp
from jax import lax
from jax.experimental import pallas as pl
from jax.experimental.pallas import tpu as pltpu
from jax.sharding import PartitionSpec as P

ITERS = 4
RELAXATION = 0.7
PRECISE = lax.Precision.HIGHEST
LANES = 128
STRIDE = 8
PERIOD = 32


def conduct(first_perm, second_perm):
    return 2.0 * first_perm * second_perm / jnp.maximum(first_perm + second_perm, 0.05)


def turn(values, shift, axis):
    size = values.shape[axis]
    if isinstance(shift, int):
        shift = shift % size
        if shift == 0:
            return values
    return pltpu.roll(values, shift, axis)


def rem(a, b):
    return a % b if isinstance(a, int) else lax.rem(a, b)


def x_next(v):
    return turn(v, -1, 0)


def x_prev(v):
    return turn(v, 1, 0)


def y_next(v):
    return turn(v, -1, 1)


def y_prev(v):
    return turn(v, 1, 1)


def iota(shape, dim):
    return lax.broadcasted_iota(jnp.int32, shape, dim)


def place(shape):
    lane = iota(shape, 1)
    return lane >> 3, lane & 7


def mirror(p, zdim):
    return p + lax.axis_index("gz") * (zdim - 1 - 2 * p)


def by_tiles(mask, values, tiles):
    parts, at = [], 0
    for t in tiles:
        if 8 * t > at:
            parts.append(values[at : 8 * t])
        at = 8 * (t + 1)
        parts.append(mask[8 * t : at] * values[8 * t : at])
    if at < values.shape[0]:
        parts.append(values[at:])
    return jnp.concatenate(parts, axis=0)


def eights(values):
    out = values[0:8]
    for t in range(1, values.shape[0] // 8):
        out = out + values[8 * t : 8 * t + 8]
    return out


def spread_row(acc_ref):
    count = acc_ref.shape[0]
    column = jnp.broadcast_to(jnp.sum(acc_ref[...], axis=1, keepdims=True), (count, LANES))
    match = iota((count, LANES), 0) == (iota((count, LANES), 1) & (count - 1))
    return jnp.sum(jnp.where(match, column, 0.0), axis=0, keepdims=True)


def prep_kernel(zdim, xdim, perm, stor, resid, d, whose, row_ref, up_ref, down_ref, acc, line):
    for f, field in enumerate((perm, stor, resid)):
        for pz in range(zdim):
            at = (f * zdim + pz) * 3
            up_ref[at : at + 3, :] = field[mirror(pz, zdim), xdim - 3 : xdim, :]
            down_ref[at : at + 3, :] = field[mirror(pz, zdim), 0:3, :]
    vectors = d.shape[0]
    acc[...] = jnp.zeros(acc.shape, jnp.float32)
    for k in range(vectors):
        total = jnp.zeros((8, LANES), jnp.float32)
        for pz in range(zdim):
            at = (9 + k) * zdim + pz
            up_ref[at : at + 1, :] = d[k, mirror(pz, zdim), xdim - 1 : xdim, :]
            down_ref[at : at + 1, :] = d[k, mirror(pz, zdim), 0:1, :]
            total = total + eights(d[k, pz] * resid[pz])
        acc[k : k + 1, :] = jnp.sum(total, axis=0, keepdims=True)
    line[...] = jnp.zeros(line.shape, jnp.float32)
    line[0:1, 8 : 8 + vectors] = whose[:, :vectors].astype(jnp.float32)
    line[0:1, 16:22] = whose[:, vectors:].astype(jnp.float32)
    extra = line[0:1, :]
    extra = extra + turn(extra, PERIOD, 1)
    extra = extra + turn(extra, 2 * PERIOD, 1)
    row = spread_row(acc) + extra
    for p in range(row_ref.shape[0]):
        row_ref[p] = row


def coarse_kernel(ids, table, whole, select, known_ref, near, hot):
    order = whole.shape[0]
    zb = ids[9]
    place_of = (zb, 1 - zb)
    lane = iota((1, LANES), 1)
    lane8, sub8 = iota((8, LANES), 1), iota((8, LANES), 0)
    number = iota((8, order), 1).astype(jnp.float32)
    near[...] = jnp.zeros(near.shape, jnp.float32)
    for col in range(5):
        for b in range(2):
            row = table[2 * ids[col] + place_of[b]]
            near[2 * col + b : 2 * col + b + 1, :] = row
            owner = jnp.sum(jnp.where(lane8 == sub8 + 8, row, 0.0), axis=1, keepdims=True)
            at = 8 * (3 * b + col if col < 3 else 2 * col + b)
            hot[at : at + 8, :] = (number == owner).astype(jnp.float32)
    rows = jnp.dot(hot[...], whole[...], precision=PRECISE, preferred_element_type=jnp.float32)
    index = iota((order, LANES), 0).astype(jnp.float32)
    for t in range(known_ref.shape[0]):
        known = jnp.zeros((1, LANES), jnp.float32)
        owner = known - 1.0
        for i in range(4):
            for b in range(2):
                row = table[2 * (4 * t + i) + place_of[b]]
                mine = (lane >> 3) == 4 * i + b
                known = jnp.where(mine, turn(row, 8 * b, 1), known)
                owner = jnp.where(mine, turn(row, 8 * b - 8, 1), owner)
        known_ref[t : t + 1, :] = known
        pick = (index == owner).astype(jnp.float32)
        select[:, LANES * t : LANES * (t + 1)] = jnp.dot(
            rows, pick, precision=PRECISE, preferred_element_type=jnp.float32
        )


def plane_of_field(fields, halos, f, p):
    own, other = fields
    zdim, xdim = own[0].shape[0], own[0].shape[1]
    hi_own, lo_own, hi_other, lo_other = halos
    src, hi, lo = (own, hi_own, lo_own) if p < zdim else (other, hi_other, lo_other)
    at = (f * zdim + (p if p < zdim else 2 * zdim - 1 - p)) * 3
    gap = jnp.zeros((2, LANES), jnp.float32)
    tile = jnp.concatenate([hi[at : at + 3, :], gap, lo[at : at + 3, :]], axis=0)
    return jnp.concatenate([src[f][mirror(p % zdim, zdim)], tile], axis=0)


def pack_kernel(zdim, xdim, *refs):
    fields = (refs[0:3], refs[3:6])
    halos, d_own = refs[6:10], refs[10]
    strip_hi, strip_lo = refs[11:13]
    rows = xdim + 8
    shape = (rows, LANES)
    plane_of, slot_of = place(shape)
    for f in range(3):
        acc = jnp.zeros(shape, jnp.float32)
        for p in range(zdim + 3):
            moved = turn(plane_of_field(fields, halos, f, p), STRIDE * p + 3, 1)
            acc = jnp.where((plane_of == p) & (slot_of < 6), moved, acc)
        strip_hi[f * rows : (f + 1) * rows, :] = acc
        strip_lo[f * rows : (f + 1) * rows, :] = acc
    lane = iota((xdim, LANES), 1)
    vectors = d_own.shape[0]
    hi_acc = jnp.zeros((xdim, LANES), jnp.float32)
    lo_acc = hi_acc
    for k in range(vectors):
        for p in range(zdim):
            at = STRIDE * p + k
            moved = turn(d_own[k, mirror(p, zdim)], at + 1, 1)
            hi_acc = jnp.where(lane == at, moved, hi_acc)
            lo_acc = jnp.where(lane == at + 1, moved, lo_acc)
    strip_hi[3 * rows : 3 * rows + xdim, :] = hi_acc
    strip_lo[3 * rows : 3 * rows + xdim, :] = turn(lo_acc, -1, 1)


def solve_coarse(known, select_ref, yb_ref):
    total = 0.0
    for t, row in enumerate(known):
        total = total + select_ref[:, LANES * t : LANES * (t + 1)] * row
    column = jnp.sum(total, axis=1, keepdims=True)
    yb_ref[...] = jnp.broadcast_to(column, yb_ref.shape)


def finish(c, scaled, strip_q, r_ref, z_ref, send_ref, w_ref, zown_ref, sw_ref, zsend_ref, img_ref, ids, last):
    zdim, xdim = c["d_own"].shape[1], c["d_own"].shape[2]
    rows = xdim + 8
    vectors = c["d_own"].shape[0]
    strips = c["strips"]
    yb = c["yb"]
    plane_of, slot_of = place((rows, LANES))

    te, cxp, cxm, cin, cout, czp, czm, ss = (strips[i] for i in range(8))
    smooth = (
        cxp * x_next(strip_q)
        + cxm * x_prev(strip_q)
        + cin * turn(strip_q, 4, 1)
        + cout * turn(strip_q, 2, 1)
        + czp * turn(strip_q, -STRIDE, 1)
        + czm * turn(strip_q, STRIDE, 1)
    )
    strip_z = (2.0 - RELAXATION) * strip_q + ss * smooth
    lane8, row8 = iota((vectors, LANES), 1), iota((vectors, LANES), 0)
    wanted = row8 == (lane8 & 7)
    for side, d_strip in ((0, c["dy_hi"]), (1, c["dy_lo"])):
        at = 6 * vectors + side * 2 * vectors
        coeff = jnp.sum(jnp.where(wanted, yb[at : at + vectors, :], 0.0), axis=0, keepdims=True)
        t = d_strip[...] * coeff
        t = t + turn(t, -1, 1)
        t = t + turn(t, -2, 1)
        t = t + turn(t, -4, 1)
        t = jnp.where(slot_of[:xdim] == 5 + side, turn(t, 5 + side, 1), 0.0)
        t = jnp.concatenate([t, jnp.zeros((8, LANES), jnp.float32)], axis=0)
        strip_z = strip_z + t
    edge_q = te * strip_q
    edge_z = te * strip_z

    for side in range(2):
        dx = c["dx"][side]
        acc = 0.0
        for k in range(vectors):
            at = (1 + side) * vectors + k
            start = (9 + k) * zdim
            acc = acc + dx[start : start + zdim, :] * yb[at : at + 1, :]
        c["bx"][side] = acc
    row8 = iota((8, LANES), 0)
    nothing = jnp.zeros((8, LANES), jnp.float32)
    for p in range(zdim + 1):
        b = p // zdim
        d_ref = c["d_own"] if b == 0 else c["d_other"]
        mxp, mxm, my = c["mxp"][b], c["mxm"][b], c["my"][b]
        q = scaled[p]
        tx, ty = c["tx"][p], c["ty"][p]
        acc = by_tiles(mxp, tx * x_next(q), (xdim // 8 - 1, xdim // 8))
        acc = acc + by_tiles(mxm, x_prev(tx * q), (0, xdim // 8))
        acc = acc + ty * y_next(q) + y_prev(ty * q)
        acc = acc + my * turn(edge_q, LANES - 6 - STRIDE * p, 1)
        acc = acc + c["tzlp"][p] * scaled[p + 1]
        if p > 0:
            acc = acc + c["tzlm"][p] * scaled[p - 1]
        z = (2.0 - RELAXATION) * q + c["s"][p] * acc
        field = 0.0
        at = 3 * b * vectors
        for k in range(vectors):
            field = field + d_ref[k, mirror(p % zdim, zdim)] * yb[at + k : at + k + 1, :]
        tile = nothing
        if b == 0:
            tile = jnp.where(row8 == 0, c["bx"][0, p : p + 1, :], 0.0)
            tile = jnp.where(row8 == 7, c["bx"][1, p : p + 1, :], tile)
            zown_ref[p] = (z[:xdim] + field)
        z_ref[p] = z + jnp.concatenate([field, tile], axis=0)

    lane = iota((rows, LANES), 1)
    edge = jnp.where((lane == 0) | (lane == LANES - 1), 1.0, 0.0)
    plane64, slot64 = plane_of[:xdim], slot_of[:xdim]
    rz = zw = zi = nothing
    sums = [nothing] * vectors
    packed = jnp.zeros((xdim, LANES), jnp.float32)
    for p in range(zdim):
        z = z_ref[p]
        tx, ty = c["tx"][p], c["ty"][p]
        acc = tx * x_next(z) + x_prev(tx * z)
        acc = acc + ty * y_next(z) + y_prev(ty * z)
        acc = acc + edge * turn(edge_z, LANES - 6 - STRIDE * p, 1)
        acc = acc + c["tz"][p] * z_ref[p + 1]
        if p > 0:
            acc = acc + c["tz"][p - 1] * z_ref[p - 1]
        w = (c["diag"][p] * z - acc)[:xdim]
        z = z[:xdim]
        w_ref[p] = w
        rz = rz + eights(r_ref[p][:xdim] * z)
        zw = zw + eights(w * z)
        if img_ref is not None:
            zi = zi + eights(img_ref[p][:xdim] * z)
        for k in range(vectors):
            sums[k] = sums[k] + eights(c["d_own"][k, mirror(p, zdim)] * w)
        moved = turn(w, STRIDE * p + 2, 1)
        packed = jnp.where((plane64 == p) & (slot64 < 4), moved, packed)

    acc_ref = c["acc"]
    acc_ref[...] = jnp.zeros(acc_ref.shape, jnp.float32)
    for j, value in list(enumerate(sums)) + [(16, rz), (17, zw), (18, zi)]:
        acc_ref[j : j + 1, :] = jnp.sum(value, axis=0, keepdims=True)
    row = spread_row(acc_ref)
    peers = send_ref.shape[0]
    if last:
        for p in range(peers):
            send_ref[p] = row
        return
    for p in range(peers):
        send_ref[p, zdim, 0:1, :] = row
    sw_ref[...] = packed
    zsend_ref[0] = w_ref[zdim - 1]
    zsend_ref[1] = w_ref[zdim - 2]
    for p in range(zdim):
        send_ref[ids[1], p] = w_ref[p, xdim - 2 : xdim, :]
        send_ref[ids[2], p] = w_ref[p, 0:2, :]
    part = xdim // 4
    pair = (iota((part, LANES), 1) & 7) >> 1
    to_hi = jnp.zeros((part, LANES), jnp.float32)
    to_lo = to_hi
    for g in range(4):
        rows_g = packed[g * part : (g + 1) * part]
        to_hi = jnp.where(pair == g, turn(rows_g, 2 * g, 1), to_hi)
        to_lo = jnp.where(pair == g, turn(rows_g, 2 * g - 2, 1), to_lo)
    for i in range(part // 2):
        send_ref[ids[3], i] = to_hi[2 * i : 2 * i + 2]
        send_ref[ids[4], i] = to_lo[2 * i : 2 * i + 2]
    for i in (5, 6):
        send_ref[ids[i], 0, 0:1, :] = packed[xdim - 1 : xdim, :]
    for i in (7, 8):
        send_ref[ids[i], 0, 0:1, :] = packed[0:1, :]


def first_kernel(zdim, xdim, *refs):
    (ids, near, s_own, s_hi, s_lo, d_own, d_other) = refs[0:7]
    dx = refs[7:11]
    (select, known_ref) = refs[11:13]
    fields = (refs[13:16], refs[16:19])
    refs = refs[19:]
    (send, w_ref, zown, sw, strips, tx, ty, tz, tzlp, tzlm, s_ref, diag_ref, mxp, mxm, my, rs_ref, r_full, zsend) = refs[:18]
    (scaled, z_ref, yb, acc, bx) = refs[18:23]
    rows = xdim + 8
    deep = zdim + 3
    shape = (rows, LANES)
    row, lane = iota(shape, 0), iota(shape, 1)
    plane_of, slot_of = place(shape)
    mirrored = ids[9] == 1

    def mg(col, b, d):
        at = 2 * col + b
        return near[at : at + 1, 16 + d : 17 + d]

    def facing(col, b, up):
        return jnp.where(mirrored, mg(col, b, 0 if up else 1), mg(col, b, 1 if up else 0))

    def z_by_row(b, up):
        beyond = jnp.where(row < xdim + 4, facing(1, b, up), facing(2, b, up))
        return jnp.where(row < xdim, facing(0, b, up), beyond)

    def by_row(b, d):
        return jnp.where(row < xdim, mg(0, b, d), jnp.where(row < xdim + 4, mg(1, b, d), mg(2, b, d)))

    for b in range(2):
        mxp[b] = jnp.where(row == xdim - 1, mg(0, b, 3), jnp.where(row == rows - 1, mg(2, b, 3), 1.0))
        mxm[b] = jnp.where(row == 0, mg(0, b, 2), jnp.where(row == xdim, mg(1, b, 2), 1.0))
        my[b] = jnp.where(lane == LANES - 1, by_row(b, 5), jnp.where(lane == 0, by_row(b, 4), 0.0))

    def strip(i):
        at = slice(i * rows, (i + 1) * rows)
        own, hi, lo = s_own[at, :], s_hi[at, :], s_lo[at, :]
        out = jnp.where((slot_of == 1) | (slot_of == 2), turn(own, -1, 1), 0.0)
        out = jnp.where(slot_of == 5, turn(hi, 2, 1), out)
        out = jnp.where(slot_of == 3, turn(hi, -1, 1), out)
        out = jnp.where(slot_of == 0, turn(hi, -5, 1), out)
        out = jnp.where(slot_of == 6, turn(lo, 4, 1), out)
        out = jnp.where(slot_of == 4, turn(lo, 3, 1), out)
        return jnp.where(slot_of == 7, turn(lo, 7, 1), out)

    ps, st, rs = strip(0), strip(1), strip(2)
    rs_ref[...] = rs
    face = (slot_of == 5) | (slot_of == 6)
    t_x = conduct(ps, x_next(ps))
    t_z = jnp.where(plane_of < deep - 1, conduct(ps, turn(ps, -STRIDE, 1)), 0.0)
    t_in = jnp.where(face, conduct(ps, turn(ps, 4, 1)), 0.0)
    t_out = jnp.where(face, conduct(ps, turn(ps, 2, 1)), 0.0)
    t_far = jnp.where(
        slot_of == 3,
        conduct(ps, turn(ps, 3, 1)),
        jnp.where(slot_of == 4, conduct(ps, turn(ps, -3, 1)), 0.0),
    )
    diag_s = st + t_x + x_prev(t_x) + t_z + turn(t_z, STRIDE, 1)
    diag_s = diag_s + t_in + t_out + turn(t_out, -2, 1) + t_far
    ss = jnp.where(diag_s > 0.0, RELAXATION / jnp.where(diag_s > 0.0, diag_s, 1.0), 0.0)

    def by_side(b, d_hi, d_lo):
        return jnp.where(slot_of == 5, mg(3, b, d_hi), mg(4, b, d_lo))

    def by_brick(d_hi, d_lo):
        return jnp.where(plane_of < zdim, by_side(0, d_hi, d_lo), by_side(1, d_hi, d_lo))

    def only(values):
        return jnp.where(face, values, 0.0)

    strips[0] = t_in
    strips[1] = only(t_x * jnp.where(row == xdim - 1, by_brick(3, 3), 1.0))
    strips[2] = only(x_prev(t_x) * jnp.where(row == 0, by_brick(2, 2), 1.0))
    strips[3] = t_in * by_brick(4, 5)
    strips[4] = t_out
    at_side = jnp.where(slot_of == 5, facing(3, 0, True), facing(4, 0, True))
    strips[5] = only(t_z * jnp.where(plane_of == zdim - 1, at_side, 1.0))
    strips[6] = only(jnp.where(plane_of == 0, 0.0, turn(t_z, STRIDE, 1)))

    inside = lane < LANES - 1

    for p in range(deep):
        scaled[p] = plane_of_field(fields, dx, 0, p)
        diag_ref[p] = plane_of_field(fields, dx, 1, p)
        r_full[p] = plane_of_field(fields, dx, 2, p)
    for p in range(deep - 1):
        here = scaled[p]
        tx[p] = conduct(here, x_next(here))
        ty[p] = jnp.where(inside, conduct(here, y_next(here)), 0.0)
        tz[p] = conduct(here, scaled[p + 1])
    edge = (lane == 0) | (lane == LANES - 1)
    inner = jnp.zeros(shape, jnp.float32)
    for p in range(deep - 1):
        t_x, t_y, t_z = tx[p], ty[p], tz[p]
        t_b = tz[p - 1] if p > 0 else jnp.zeros(shape, jnp.float32)
        total = diag_ref[p] + t_x + x_prev(t_x) + t_y + y_prev(t_y) + t_z + t_b
        total = total + jnp.where(edge, turn(t_in, LANES - 6 - STRIDE * p, 1), 0.0)
        relax = jnp.where(total > 0.0, RELAXATION / jnp.where(total > 0.0, total, 1.0), 0.0)
        diag_ref[p] = total
        s_ref[p] = relax
        tzlp[p] = t_z * z_by_row(0, True) if p == zdim - 1 else t_z
        tzlm[p] = t_b * z_by_row(1, False) if p == zdim else t_b
        scaled[p] = relax * r_full[p]
        if p < zdim:
            moved = turn(relax, STRIDE * p + 2, 1)
            inner = jnp.where((plane_of == p) & ((slot_of == 1) | (slot_of == 2)), moved, inner)
    ss = jnp.where((slot_of == 1) | (slot_of == 2), inner, ss)
    strips[7] = ss

    known = [known_ref[t : t + 1, :] for t in range(known_ref.shape[0])]
    solve_coarse(known, select, yb)
    c = dict(
        tx=tx, ty=ty, tz=tz, tzlp=tzlp, tzlm=tzlm, s=s_ref, diag=diag_ref, mxp=mxp, mxm=mxm, my=my,
        strips=strips, d_own=d_own, d_other=d_other, dx=dx, dy_hi=s_hi.at[3 * rows : 3 * rows + xdim, :],
        dy_lo=s_lo.at[3 * rows : 3 * rows + xdim, :], yb=yb, acc=acc, bx=bx,
    )
    finish(c, scaled, ss * rs, r_full, z_ref, send, w_ref, zown, sw, zsend, None, ids, False)


def totals(rows, count):
    lane = iota((1, LANES), 1)
    total = 0.0
    for i in range(count):
        total = total + (rows(i, 0) + rows(i, 1))
    sums = [
        jnp.sum(jnp.where(lane == 16 + j, total, 0.0), axis=1, keepdims=True) for j in range(3)
    ]
    tiles = []
    for t in range(count // 4):
        tile = jnp.zeros((1, LANES), jnp.float32)
        for i in range(4):
            for b in range(2):
                mine = (lane >> 3) == 4 * i + b
                tile = jnp.where(mine, turn(rows(4 * t + i, b), 8 * b, 1), tile)
        tiles.append(tile)
    return tiles, sums


def scalars(sums, scal_ref, first):
    inner = sums[0]
    if first:
        ratio = jnp.zeros_like(inner)
        curvature = sums[1]
    else:
        ratio = inner / scal_ref[0:1, 0:1]
        curvature = sums[1] + ratio * (2.0 * sums[2] + ratio * scal_ref[1:2, 0:1])
    return inner, ratio, curvature, inner / curvature


def next_kernel(zdim, xdim, first, last, *refs):
    refs = list(refs)

    def take(n):
        out, refs[:n] = refs[:n], []
        return out

    ids, got, far, zgot, d_own, d_other, *dx = take(10)
    s_hi, s_lo, select, strips, tx, ty, tz, tzlp, tzlm, s_ref, diag_ref, mxp, mxm, my = take(14)
    known_ref, w_in, z_in, sw_in, rs_in = take(5)
    if first:
        (r_in,) = take(1)
    else:
        r_in, img_in, dir_in, sol_in, is_in, kimg_ref, scal_ref = take(7)
    send, w_ref, zown, sw, rs_ref, r_ref, img_ref, dir_ref, sol_ref, is_ref, known_out, kimg_out, scal_out, zsend = take(14)
    scaled, z_ref, yb, acc, bx, tiles_ref = take(6)
    rows = xdim + 8
    plane_of, slot_of = place((rows, LANES))

    peers = got.shape[0]
    tiles, sums = totals(lambda i, b: (got, far)[b][i, zdim, 0:1, :], peers)
    inner, ratio, curvature, step = scalars(sums, None if first else scal_ref, first)
    scal_out[0:1, :] = jnp.broadcast_to(inner, (1, LANES))
    scal_out[1:2, :] = jnp.broadcast_to(curvature, (1, LANES))
    known = []
    for t, tile in enumerate(tiles):
        if not first:
            tile = tile + ratio * kimg_ref[t : t + 1, :]
        kimg_out[t : t + 1, :] = tile
        value = known_ref[t : t + 1, :] - step * tile
        known_out[t : t + 1, :] = value
        known.append(value)
    solve_coarse(known, select, yb)

    part = xdim // 4
    for i in range(part // 2):
        for j in range(4):
            tiles_ref[j, 2 * i : 2 * i + 2, :] = (got, far)[j // 2][ids[3 + j % 2], i]
    from_hi, from_lo, far_hi, far_lo = (tiles_ref[j] for j in range(4))
    beyond = plane_of[:part] == zdim
    own = sw_in[...]
    slot_part = slot_of[:part]
    blocks = []
    for g in range(4):
        value = own[g * part : (g + 1) * part]
        value = jnp.where(slot_part == 5, turn(from_hi, 5 - 2 * g, 1), value)
        value = jnp.where(slot_part == 3, turn(from_hi, 2 - 2 * g, 1), value)
        value = jnp.where(slot_part == 4, turn(from_lo, 4 - 2 * g, 1), value)
        value = jnp.where(slot_part == 6, turn(from_lo, 5 - 2 * g, 1), value)
        value = jnp.where(beyond & (slot_part == 5), turn(far_hi, STRIDE + 5 - 2 * g, 1), value)
        value = jnp.where(beyond & (slot_part == 6), turn(far_lo, STRIDE + 5 - 2 * g, 1), value)
        blocks.append(value)
    slot8, row8 = slot_of[:8], iota((8, LANES), 0)
    tile = jnp.zeros((8, LANES), jnp.float32)
    for i, at, want, shift in ((5, 0, 5, 3), (6, 0, 6, 5), (7, 7, 5, 3), (8, 7, 6, 5)):
        value = turn(jnp.broadcast_to(got[ids[i], 0, 0:1, :], (8, LANES)), shift, 1)
        tile = jnp.where((row8 == at) & (slot8 == want), value, tile)
    ws = jnp.concatenate(blocks + [tile], axis=0)
    ws = jnp.where((slot_of == 0) | (slot_of == 7), 0.0, ws)
    if not first:
        ws = ws + ratio * is_in[...]
    is_ref[...] = ws
    rs = rs_in[...] - step * ws
    rs_ref[...] = rs
    strip_q = strips[7] * rs

    tiles_ref[...] = jnp.zeros(tiles_ref.shape, jnp.float32)
    for p in range(zdim):
        tiles_ref[p, 0:2, :] = got[ids[1], p]
        tiles_ref[p, 6:8, :] = got[ids[2], p]
    tiles_ref[zdim, 0:1, :] = far[ids[1], zdim - 1, 0:1, :]
    tiles_ref[zdim, 7:8, :] = far[ids[2], zdim - 1, 1:2, :]
    for p in range(zdim + 2):
        inside = w_in[p] if p < zdim else zgot[p - zdim]
        image = jnp.concatenate([inside, tiles_ref[p, 0:8, :]], axis=0)
        if not first:
            image = image + ratio * img_in[p]
        img_ref[p] = image
        r = r_in[p] - step * image
        r_ref[p] = r
        scaled[p] = s_ref[p] * r
    for p in range(zdim):
        d = z_in[p]
        if first:
            sol_ref[p] = step * d
        else:
            d = d + ratio * dir_in[p]
            sol_ref[p] = sol_in[p] + step * d
        dir_ref[p] = d
    c = dict(
        tx=tx, ty=ty, tz=tz, tzlp=tzlp, tzlm=tzlm, s=s_ref, diag=diag_ref, mxp=mxp, mxm=mxm, my=my,
        strips=strips, d_own=d_own, d_other=d_other, dx=dx, dy_hi=s_hi.at[3 * rows : 3 * rows + xdim, :],
        dy_lo=s_lo.at[3 * rows : 3 * rows + xdim, :], yb=yb, acc=acc, bx=bx,
    )
    finish(c, scaled, strip_q, r_ref, z_ref, send, w_ref, zown, sw, zsend, img_ref, ids, last)


def last_kernel(zdim, xdim, got, w_in, z_in, r_in, img_in, dir_in, sol_in, scal_ref, sol_ref, r_ref):
    _, sums = totals(lambda i, b: got[2 * i + b], got.shape[0] // 2)
    _, ratio, _, step = scalars(sums, scal_ref, False)
    for p in range(zdim):
        at = mirror(p, zdim)
        image = w_in[p] + ratio * img_in[p][:xdim]
        r_ref[at] = r_in[p][:xdim] - step * image
        sol_ref[at] = sol_in[p] + step * (z_in[p] + ratio * dir_in[p])


def call(kernel, name, args, outs, scratch=(), smem=0):
    specs = [pl.BlockSpec(memory_space=pltpu.SMEM)] * smem
    specs += [pl.BlockSpec(memory_space=pltpu.VMEM)] * (len(args) - smem)
    return pl.pallas_call(
        kernel,
        name=name,
        in_specs=specs,
        out_specs=[pl.BlockSpec(memory_space=pltpu.VMEM)] * len(outs),
        out_shape=[jax.ShapeDtypeStruct(o, jnp.float32) for o in outs],
        scratch_shapes=[pltpu.VMEM(s, jnp.float32) for s in scratch],
        compiler_params=pltpu.CompilerParams(vmem_limit_bytes=24 * 1024 * 1024),
    )(*args)


def local(right_side, permeability, storage, deflation, coarse_inverse, owners, margin):
    nx, ny, nz = (lax.axis_size(a) for a in ("gx", "gy", "gz"))
    vectors, zdim, xdim, ydim = deflation.shape
    order = coarse_inverse.shape[1]
    assert nz == 2 and ydim == LANES and 2 * zdim * STRIDE == LANES and vectors == 8
    gx, gy, gz = (lax.axis_index(a) for a in ("gx", "gy", "gz"))
    peers, rows = nx * ny, xdim + 8
    me = gx * ny + gy
    off_x = jnp.array([0, 1, -1, 0, 0, 1, 1, -1, -1, 0], jnp.int32) + gx
    off_y = jnp.array([0, 0, 0, 1, -1, 1, -1, 1, -1, 0], jnp.int32) + gy
    there = (off_x >= 0) & (off_x < nx) & (off_y >= 0) & (off_y < ny)
    ids = jnp.where(there, off_x * ny + off_y, me)
    ids = jnp.where(jnp.arange(10) == 9, gz, ids)

    def swap(v):
        return lax.ppermute(v, "gz", [(0, 1), (1, 0)])

    def up(v, axis, count):
        return lax.ppermute(v, axis, [(i, i + 1) for i in range(count - 1)])

    def down(v, axis, count):
        return lax.ppermute(v, axis, [(i + 1, i) for i in range(count - 1)])

    fields = (permeability, storage, right_side)
    others = [swap(v) for v in fields]
    d_other = swap(deflation)
    edge_rows = ((9 + vectors) * zdim, LANES)
    first_row, x_up, x_down = call(
        lambda *refs: prep_kernel(zdim, xdim, *refs), "prep",
        [*fields, deflation, jnp.concatenate([owners.reshape(1, -1), margin.reshape(1, -1)], axis=1)],
        [(peers * nz, 1, LANES), edge_rows, edge_rows],
        [(PERIOD, LANES), (8, LANES)],
    )
    x_lo, x_hi = up(x_up, "gx", nx), down(x_down, "gx", nx)
    table = lax.all_to_all(first_row, ("gx", "gy", "gz"), 0, 0, tiled=True)
    dx = [x_hi, x_lo, swap(x_hi), swap(x_lo)]
    strip_rows = 3 * rows + xdim
    strip_hi, strip_lo = call(
        lambda *refs: pack_kernel(zdim, xdim, *refs), "pack",
        [*fields, *others, *dx, deflation],
        [(strip_rows, LANES), (strip_rows, LANES)],
    )
    s_lo = up(strip_hi, "gy", ny)
    s_hi = down(strip_lo, "gy", ny)
    coarse_inverse, _ = lax.optimization_barrier((coarse_inverse, strip_hi))
    whole = lax.all_gather(coarse_inverse, "gx", axis=0, tiled=True)
    tiles = peers * PERIOD // LANES
    select, known, near = call(
        coarse_kernel, "coarse", [ids, table, whole],
        [(10 * vectors, peers * PERIOD), (tiles, LANES), (16, LANES)],
        [(10 * vectors, order)], smem=1,
    )
    full, brick, one = (zdim + 3, rows, LANES), (zdim, xdim, LANES), (rows, LANES)
    mine, slots = (zdim, xdim, LANES), (peers, zdim + 1, 2, LANES)
    scratch = [full, full, (10 * vectors, LANES), (PERIOD, LANES), (2, zdim, LANES)]
    (send, w, z, sw, strips, *consts, rs, r_full, zsend) = call(
        lambda *refs: first_kernel(zdim, xdim, *refs), "first",
        [ids, near, strip_hi, s_hi, s_lo, deflation, d_other, *dx, select, known, *fields, *others],
        [slots, brick, mine, (xdim, LANES), (8, *one)] + [full] * 7 + [(2, *one)] * 3 + [one, full, (2, xdim, LANES)],
        scratch, smem=1,
    )
    state = [r_full]
    for iteration in range(ITERS - 1):
        first, last = iteration == 0, iteration == ITERS - 2
        got = lax.all_to_all(send, ("gx", "gy"), 0, 0, tiled=True)
        far, (zsend, _) = swap(got), lax.optimization_barrier((zsend, got))
        zgot = swap(zsend)
        send, w, z, sw, rs, r, img, direct, sol, ist, known, kimg, scal, zsend = call(
            lambda *refs: next_kernel(zdim, xdim, first, last, *refs), f"step{iteration}",
            [ids, got, far, zgot, deflation, d_other, *dx, s_hi, s_lo, select, strips, *consts, known, w, z, sw, rs, *state],
            [(peers * nz, 1, LANES) if last else slots, brick, mine, (xdim, LANES), one, full, full, mine, mine, one,
             (tiles, LANES), (tiles, LANES), (8, LANES), (2, xdim, LANES)],
            scratch + [(zdim + 2, max(8, xdim // 4), LANES)], smem=1,
        )
        state = [r, img, direct, sol, ist, kimg, scal]
    got = lax.all_to_all(send, ("gx", "gy", "gz"), 0, 0, tiled=True)
    return tuple(call(
        lambda *refs: last_kernel(zdim, xdim, *refs), "last",
        [got, w, z, r, img, direct, sol, scal], [mine, mine],
    ))


def solution(mesh):
    in_specs = (
        P("gz", "gx", "gy"),
        P("gz", "gx", "gy"),
        P("gz", "gx", "gy"),
        P(None, "gz", "gx", "gy"),
        P("gx", None),
        P("gz", "gx", "gy", None),
        P("gz", "gx", "gy", None),
    )
    out_specs = (P("gz", "gx", "gy"), P("gz", "gx", "gy"))
    return jax.shard_map(local, mesh=mesh, in_specs=in_specs, out_specs=out_specs, check_vma=False)
```

time: 119 us -> 113 us (0.950)
  Pallas kernels: 28.7 us -> 22.9 us
  local copies, waits for them, and re-layouts: 5.59 us -> 2.56 us
  waiting for transfers between devices: 8.47 us -> 11.3 us
  blocking collectives: 55.9 us -> 53.1 us
  starting transfers between devices: 18.8 us -> 20.5 us
    pallas_call x8, Pallas kernels: 28.7 us -> 22.9 us  [call(): pl.pallas_call(kernel, name=name, in_specs=specs, out_specs=[pl.BlockSpec...]
    unnamed x20 -> x14, local copies, waits for them, and re-layouts: 5.59 us -> 2.56 us
    ppermute x6 -> x12, waiting for transfers between devices: 1.27 us -> 4.14 us  [swap(): return lax.ppermute(v, 'gz', [(0, 1), (1, 0)])]
    all_to_all x3, blocking collectives: 37.6 us -> 34.9 us  [local(): got = lax.all_to_all(send, ('gx', 'gy'), 0, 0, tiled=True)]
    ppermute x6 -> x12, starting transfers between devices: 1.37 us -> 2.9 us  [swap(): return lax.ppermute(v, 'gz', [(0, 1), (1, 0)])]
  transfers between devices with their start and end apart: 11 -> 17, of which waited for: 3 -> 6; matrix products, arithmetic and copies ran while one was open for 0% -> 1% of each run, Pallas kernels for 6% -> 6%
where the time goes in v4:
time: 113 us; the launch traced here: 112 us
  blocking collectives  53.1 us (47%)
  Pallas kernels  22.9 us (20%)
  starting transfers between devices  20.5 us (18%)
  waiting for transfers between devices  11.3 us (10%)
  local copies, waits for them, and re-layouts  2.56 us (2%)
    all_to_all x3, blocking collectives, local(): got = lax.all_to_all(send, ('gx', 'gy'), 0, 0, tiled=True)  34.9 us
    pallas_call x8, Pallas kernels, call(): pl.pallas_call(kernel, name=name, in_specs=specs, out_specs=[pl.BlockSpec...  22.9 us
    all_gather x1, blocking collectives, local(): whole = lax.all_gather(coarse_inverse, 'gx', axis=0, tiled=True)  9.24 us
    ppermute x2, starting transfers between devices, up(): return lax.ppermute(v, axis, [(i, i + 1) for i in range(count - 1)])  9.08 us
    all_to_all x1, blocking collectives, local(): got = lax.all_to_all(send, ('gx', 'gy', 'gz'), 0, 0, tiled=True)  8.98 us
    all_to_all x1, starting transfers between devices, local(): table = lax.all_to_all(first_row, ('gx', 'gy', 'gz'), 0, 0, tiled=True)  5.8 us
    ppermute x2, waiting for transfers between devices, down(): return lax.ppermute(v, axis, [(i + 1, i) for i in range(count - 1)])  5.28 us
    ppermute x12, waiting for transfers between devices, swap(): return lax.ppermute(v, 'gz', [(0, 1), (1, 0)])  4.14 us
  transfers between devices with their start and end apart: 17, of which 6 were waited for; matrix products, arithmetic and copies ran while one was open for 1% of the time, Pallas kernels for 6%

profile of v4, /device:TPU:0, one launch (start us, length us, event | category | flops | bytes accessed | tf_op | source)
XLA Modules:
  0.0 112.0 jit_solution(3602015835048909368)
XLA Ops:
  0.6 0.6 collective-permute-start.9
  1.2 0.7 pad_add_fusion.refs_4_
  1.9 1.6 %copy-done = f32[8,8,64,128]{3,2,1,0:T(8,128)S(1)} copy-done((f32[8,8,64,128]{3,2,1,0:T(8,128)S(1)}, f32[8,8,64,128]{3,2,1,0:T(8,128)}, u32[]{:S(2)}) %copy-start) | copy-done | bytes 2097176
  3.5 2.1 %prep.1 = (f32[32,1,128]{2,1,0:T(1,128)}, f32[136,128]{1,0:T(8,128)S(1)}, f32[136,128]{1,0:T(8,128)S(1)}) custom-call(f32[8,64,128]{2,1,0:T(8,128)} %refs_13_.1, f32[8,64,128]{2,1,0:T(8,128)} %refs_14_.1, f32[8,64,128]{2,1,0:T(8,128)} %refs_15_.1, f32[8,8,64,128]{3,2,1,0:T(8,128)S(1)} %copy-done, s32[1,14]{1,0:T(1,128)S(1)} %pad_add_fusion.refs_4_), custom_call_target="tpu_custom_call" | custom-call | tf_op jit(solution)/shard_map/prep/pallas_call | solution.py:584
  5.7 1.4 %collective-permute-start.3 = (f32[136,128]{1,0:T(8,128)S(1)}, f32[136,128]{1,0:T(8,128)S(1)}, u32[]{:S(2)}, u32[]{:S(2)}) collective-permute-start(f32[136,128]{1,0:T(8,128)S(1)} %get-tuple-element.69), channel_id=1, source_target_pairs={{8,0},{16,8},{24,16},{9,1},{17,9},{25,17},{10,2},{18,10},{26,18},{... | collective-permute-start | bytes 208904 | tf_op jit(solution)/shard_map/ppermute | solution.py:616
  7.2 0.5 collective-permute-start
  7.7 5.3 %collective-permute-done.3.refs_6_.refs_7_ = f32[136,128]{1,0:T(8,128)S(1)} collective-permute-done((f32[136,128]{1,0:T(8,128)S(1)}, f32[136,128]{1,0:T(8,128)S(1)}, u32[]{:S(2)}, u32[]{:S(2)}) %collective-permute-start.3) | collective-permute-done | bytes 69664 | tf_op jit(solution)/shard_map/ppermute | solution.py:616
  13.0 4.5 %collective-permute-start.4 = (f32[136,128]{1,0:T(8,128)S(1)}, f32[136,128]{1,0:T(8,128)S(1)}, u32[]{:S(2)}, u32[]{:S(2)}) collective-permute-start(f32[136,128]{1,0:T(8,128)S(1)} %get-tuple-element.70), channel_id=1, source_target_pairs={{0,8},{8,16},{16,24},{1,9},{9,17},{17,25},{2,10},{10,18},{18,26},{... | collective-permute-start | bytes 208904 | tf_op jit(solution)/shard_map/ppermute | solution.py:613
  17.6 1.9 %collective-permute-done.4.refs_7_.refs_8_ = f32[136,128]{1,0:T(8,128)S(1)} collective-permute-done((f32[136,128]{1,0:T(8,128)S(1)}, f32[136,128]{1,0:T(8,128)S(1)}, u32[]{:S(2)}, u32[]{:S(2)}) %collective-permute-start.4) | collective-permute-done | bytes 69664 | tf_op jit(solution)/shard_map/ppermute | solution.py:613
  19.5 1.3 %collective-permute-done.5.refs_8_.refs_9_ = f32[136,128]{1,0:T(8,128)S(1)} collective-permute-done((f32[136,128]{1,0:T(8,128)S(1)}, f32[136,128]{1,0:T(8,128)S(1)}, u32[]{:S(2)}, u32[]{:S(2)}) %collective-permute-start.5) | collective-permute-done | bytes 69664 | tf_op jit(solution)/shard_map/ppermute | solution.py:610
  20.9 5.8 %all-to-all-start = ((f32[32,1,128]{2,1,0:T(1,128)}), f32[32,1,128]{2,1,0:T(1,128)S(1)}, u32[]{:S(2)}, u32[]{:S(2)}) async-start(f32[32,1,128]{2,1,0:T(1,128)} %get-tuple-element.68), calls=%async_computation | async-start | bytes 32768 | tf_op jit(solution)/shard_map/all_to_all | solution.py:629
  26.8 2.9 %pack.1 = (f32[280,128]{1,0:T(8,128)}, f32[280,128]{1,0:T(8,128)}) custom-call(f32[8,64,128]{2,1,0:T(8,128)} %refs_13_.1, f32[8,64,128]{2,1,0:T(8,128)} %refs_14_.1, f32[8,64,128]{2,1,0:T(8,128)} %refs_15_.1, f32[8,64,128]{2,1,0:T(8,128)S(1)} %collective-permute-done.refs_3_.refs_16_, f32[8,64,128]{2,1,0:T(8,128)S(1)} %collective-permute-done.1.refs_4_.refs_17_, ...), custom_call_target="tpu_custom_call" | custom-call | tf_op jit(solution)/shard_map/pack/pallas_call | solution.py:584
  29.6 1.3 %collective-permute-start.7 = (f32[280,128]{1,0:T(8,128)}, f32[280,128]{1,0:T(8,128)S(1)}, u32[]{:S(2)}, u32[]{:S(2)}) collective-permute-start(f32[280,128]{1,0:T(8,128)} %get-tuple-element.74), channel_id=1, source_target_pairs={{2,0},{4,2},{6,4},{3,1},{5,3},{7,5},{10,8},{12,10},{14,12},{11,9},... | collective-permute-start | bytes 430088 | tf_op jit(solution)/shard_map/ppermute | solution.py:616
  30.9 4.6 %collective-permute-start.8 = (f32[280,128]{1,0:T(8,128)}, f32[280,128]{1,0:T(8,128)S(1)}, u32[]{:S(2)}, u32[]{:S(2)}) collective-permute-start(f32[280,128]{1,0:T(8,128)} %get-tuple-element.71.refs_2_), channel_id=1, source_target_pairs={{0,2},{2,4},{4,6},{1,3},{3,5},{5,7},{8,10},{10,12},{12,14},{9,11},... | collective-permute-start | bytes 430088 | tf_op jit(solution)/shard_map/ppermute | solution.py:613
  35.5 9.2 %all_gather.3.whole = f32[256,256]{1,0:T(8,128)S(1)} all-gather(f32[64,256]{1,0:T(8,128)S(1)} %copy-done.4), channel_id=1, replica_groups=mesh['gx'=4,'gy'=4,'gz'=2] {'gx'}, dimensions={0}, use_global_device_ids=true | all-gather | bytes 327680 | tf_op jit(solution)/shard_map/all_gather | solution.py:640
  44.8 1.4 %coarse.1 = (f32[80,512]{1,0:T(8,128)S(1)}, f32[4,128]{1,0:T(4,128)S(1)}, f32[16,128]{1,0:T(8,128)S(1)}) custom-call(s32[10]{0:T(128)S(1)} %compare_select_fusion.ids.refs_0_, f32[32,1,128]{2,1,0:T(1,128)S(1)} %all-to-all-done.table, f32[256,256]{1,0:T(8,128)S(1)} %all_gather.3.whole), custom_call_target="tpu_custom_call" | custom-call | tf_op jit(solution)/shard_map/coarse/pallas_call | solution.py:584
  46.3 0.9 copy-done.3
  47.2 5.3 %first.1 = (f32[16,9,2,128]{3,2,1,0:T(2,128)S(1)}, f32[8,64,128]{2,1,0:T(8,128)S(1)}, f32[8,64,128]{2,1,0:T(8,128)S(1)}, f32[64,128]{1,0:T(8,128)S(1)}, f32[8,72...) custom-call(s32[10]{0:T(128)S(1)} %compare_select_fusion.ids.refs_0_, ...), custom_call_target="tpu_custom_call" | custom-call | tf_op jit(solution)/shard_map/first/pallas_call | solution.py:584
  52.5 12.1 %all_to_all.25.refs_1_ = f32[16,9,2,128]{3,2,1,0:T(2,128)S(1)} all-to-all(f32[16,9,2,128]{3,2,1,0:T(2,128)S(1)} %get-tuple-element.77), channel_id=1, replica_groups=mesh['gx'=4,'gy'=4,'gz'=2] {'gx','gy'}, dimensions={0} | all-to-all | bytes 294912 | tf_op jit(solution)/shard_map/all_to_all | solution.py:659
  64.7 0.5 collective-permute-start.11
  65.2 1.0 collective-permute-done.11.refs_3_
  66.1 3.2 %step0.1 = (f32[16,9,2,128]{3,2,1,0:T(2,128)S(1)}, f32[8,64,128]{2,1,0:T(8,128)S(1)}, f32[8,64,128]{2,1,0:T(8,128)S(1)}, f32[64,128]{1,0:T(8,128)S(1)}, f32[72,1...) custom-call(s32[10]{0:T(128)S(1)} %compare_select_fusion.ids.refs_0_, ...), custom_call_target="tpu_custom_call" | custom-call | tf_op jit(solution)/shard_map/step0/pallas_call | solution.py:584
  69.4 11.5 %all_to_all.26.refs_1_ = f32[16,9,2,128]{3,2,1,0:T(2,128)S(1)} all-to-all(f32[16,9,2,128]{3,2,1,0:T(2,128)S(1)} %get-tuple-element.96), channel_id=1, replica_groups=mesh['gx'=4,'gy'=4,'gz'=2] {'gx','gy'}, dimensions={0} | all-to-all | bytes 294912 | tf_op jit(solution)/shard_map/all_to_all | solution.py:659
  80.9 0.5 collective-permute-start.13
  81.4 1.0 collective-permute-done.13.refs_3_
  82.4 3.2 %step1.1 = (f32[16,9,2,128]{3,2,1,0:T(2,128)S(1)}, f32[8,64,128]{2,1,0:T(8,128)S(1)}, f32[8,64,128]{2,1,0:T(8,128)S(1)}, f32[64,128]{1,0:T(8,128)S(1)}, f32[72,1...) custom-call(s32[10]{0:T(128)S(1)} %compare_select_fusion.ids.refs_0_, ...), custom_call_target="tpu_custom_call" | custom-call | tf_op jit(solution)/shard_map/step1/pallas_call | solution.py:584
  85.6 11.3 %all_to_all.27.refs_1_ = f32[16,9,2,128]{3,2,1,0:T(2,128)S(1)} all-to-all(f32[16,9,2,128]{3,2,1,0:T(2,128)S(1)} %get-tuple-element.111), channel_id=1, replica_groups=mesh['gx'=4,'gy'=4,'gz'=2] {'gx','gy'}, dimensions={0} | all-to-all | bytes 294912 | tf_op jit(solution)/shard_map/all_to_all | solution.py:659
  96.9 0.5 collective-permute-start.15
  97.4 1.0 collective-permute-done.15.refs_3_
  98.4 3.7 %step2.1 = (f32[32,1,128]{2,1,0:T(1,128)S(1)}, f32[8,64,128]{2,1,0:T(8,128)S(1)}, f32[8,64,128]{2,1,0:T(8,128)S(1)}, f32[64,128]{1,0:T(8,128)}, f32[72,128]{1,0:...) custom-call(s32[10]{0:T(128)S(1)} %compare_select_fusion.ids.refs_0_, ...), custom_call_target="tpu_custom_call" | custom-call | tf_op jit(solution)/shard_map/step2/pallas_call | solution.py:584
  102.1 9.0 %all_to_all.28.refs_0_ = f32[32,1,128]{2,1,0:T(1,128)S(1)} all-to-all(f32[32,1,128]{2,1,0:T(1,128)S(1)} %get-tuple-element.126), channel_id=1, replica_groups=mesh['gx'=4,'gy'=4,'gz'=2] {'gx','gy','gz'}, dimensions={0} | all-to-all | bytes 32768 | tf_op jit(solution)/shard_map/all_to_all | solution.py:670
  111.0 1.0 last.1
  (31 shorter events, 0.4 us)
Async XLA Ops:
  0.6 45.6 %collective-permute-start.9 = (f32[8,8,64,128]{3,2,1,0:T(8,128)}, f32[8,8,64,128]{3,2,1,0:T(8,128)}, u32[]{:S(2)}, u32[]{:S(2)}) collective-permute-start(f32[8,8,64,128]{3,2,1,0:T(8,128)} %refs_4_.5), channel_id=1, source_target_pairs={{0,1},{1,0},{2,3},{3,2},{4,5},{5,4},{6,7},{7,6},{8,9},{9,8},{10,11... | collective-permute-start | bytes 6291464 | tf_op jit(solution)/shard_map/ppermute | solution.py:610
  1.9 1.6 %copy-start = (f32[8,8,64,128]{3,2,1,0:T(8,128)S(1)}, f32[8,8,64,128]{3,2,1,0:T(8,128)}, u32[]{:S(2)}) copy-start(f32[8,8,64,128]{3,2,1,0:T(8,128)} %refs_4_.5) | copy-start | bytes 6291460
  3.5 23.2 %copy-start.1 = (f32[8,8,64,128]{3,2,1,0:T(8,128)S(1)}, f32[8,8,64,128]{3,2,1,0:T(8,128)}, u32[]{:S(2)}) copy-start(f32[8,8,64,128]{3,2,1,0:T(8,128)} %refs_4_.5) | copy-start | bytes 6291460
  5.7 29.8 %copy-start.5 = (s32[10]{0:T(128)S(1)}, s32[10]{0:T(128)}, u32[]{:S(2)}) copy-start(s32[10]{0:T(128)} %constant.23.clone) | copy-start | bytes 124
  5.7 29.8 %copy-start.6 = (s32[10]{0:T(128)S(1)}, s32[10]{0:T(128)}, u32[]{:S(2)}) copy-start(s32[10]{0:T(128)} %constant.22.clone) | copy-start | bytes 124
  5.7 29.9 %copy-start.4 = (f32[64,256]{1,0:T(8,128)S(1)}, f32[64,256]{1,0:T(8,128)}, u32[]{:S(2)}) copy-start(f32[64,256]{1,0:T(8,128)} %param.13) | copy-start | bytes 196612
  5.7 7.3 %collective-permute-start.3 = (f32[136,128]{1,0:T(8,128)S(1)}, f32[136,128]{1,0:T(8,128)S(1)}, u32[]{:S(2)}, u32[]{:S(2)}) collective-permute-start(f32[136,128]{1,0:T(8,128)S(1)} %get-tuple-element.69), channel_id=1, source_target_pairs={{8,0},{16,8},{24,16},{9,1},{17,9},{25,17},{10,2},{18,10},{26,18},{... | collective-permute-start | bytes 208904 | tf_op jit(solution)/shard_map/ppermute | solution.py:616
  7.1 19.6 %collective-permute-start.2 = (f32[8,64,128]{2,1,0:T(8,128)}, f32[8,64,128]{2,1,0:T(8,128)S(1)}, u32[]{:S(2)}, u32[]{:S(2)}) collective-permute-start(f32[8,64,128]{2,1,0:T(8,128)} %refs_15_.1), channel_id=1, source_target_pairs={{0,1},{1,0},{2,3},{3,2},{4,5},{5,4},{6,7},{7,6},{8,9},{9,8},{10,11... | collective-permute-start | bytes 786440 | tf_op jit(solution)/shard_map/ppermute | solution.py:610
  7.2 19.6 %collective-permute-start = (f32[8,64,128]{2,1,0:T(8,128)}, f32[8,64,128]{2,1,0:T(8,128)S(1)}, u32[]{:S(2)}, u32[]{:S(2)}) collective-permute-start(f32[8,64,128]{2,1,0:T(8,128)} %refs_13_.1), channel_id=1, source_target_pairs={{0,1},{1,0},{2,3},{3,2},{4,5},{5,4},{6,7},{7,6},{8,9},{9,8},{10,11... | collective-permute-start | bytes 786440 | tf_op jit(solution)/shard_map/ppermute | solution.py:610
  7.7 19.1 %collective-permute-start.1 = (f32[8,64,128]{2,1,0:T(8,128)}, f32[8,64,128]{2,1,0:T(8,128)S(1)}, u32[]{:S(2)}, u32[]{:S(2)}) collective-permute-start(f32[8,64,128]{2,1,0:T(8,128)} %refs_14_.1), channel_id=1, source_target_pairs={{0,1},{1,0},{2,3},{3,2},{4,5},{5,4},{6,7},{7,6},{8,9},{9,8},{10,11... | collective-permute-start | bytes 786440 | tf_op jit(solution)/shard_map/ppermute | solution.py:610
  13.0 6.5 %collective-permute-start.4 = (f32[136,128]{1,0:T(8,128)S(1)}, f32[136,128]{1,0:T(8,128)S(1)}, u32[]{:S(2)}, u32[]{:S(2)}) collective-permute-start(f32[136,128]{1,0:T(8,128)S(1)} %get-tuple-element.70), channel_id=1, source_target_pairs={{0,8},{8,16},{16,24},{1,9},{9,17},{17,25},{2,10},{10,18},{18,26},{... | collective-permute-start | bytes 208904 | tf_op jit(solution)/shard_map/ppermute | solution.py:613
  19.5 1.3 %collective-permute-start.5 = (f32[136,128]{1,0:T(8,128)S(1)}, f32[136,128]{1,0:T(8,128)S(1)}, u32[]{:S(2)}, u32[]{:S(2)}) collective-permute-start(f32[136,128]{1,0:T(8,128)S(1)} %collective-permute-done.3.refs_6_.refs_7_), channel_id=1, source_target_pairs={{0,1},{1,0},{2,3},{3,2},{4,5},{5,4},{6,7},{7,6},{8,9},{9,8},{10,11... | collective-permute-start | bytes 208904 | tf_op jit(solution)/shard_map/ppermute | solution.py:610
  20.7 6.0 %collective-permute-start.6 = (f32[136,128]{1,0:T(8,128)S(1)}, f32[136,128]{1,0:T(8,128)S(1)}, u32[]{:S(2)}, u32[]{:S(2)}) collective-permute-start(f32[136,128]{1,0:T(8,128)S(1)} %collective-permute-done.4.refs_7_.refs_8_), channel_id=1, source_target_pairs={{0,1},{1,0},{2,3},{3,2},{4,5},{5,4},{6,7},{7,6},{8,9},{9,8},{10,11... | collective-permute-start | bytes 208904 | tf_op jit(solution)/shard_map/ppermute | solution.py:610
  20.9 23.9 %all-to-all-start = ((f32[32,1,128]{2,1,0:T(1,128)}), f32[32,1,128]{2,1,0:T(1,128)S(1)}, u32[]{:S(2)}, u32[]{:S(2)}) async-start(f32[32,1,128]{2,1,0:T(1,128)} %get-tuple-element.68), calls=%async_computation | async-start | bytes 32768 | tf_op jit(solution)/shard_map/all_to_all | solution.py:629
  26.8 8.7 %copy-start.2 = (f32[8,64,128]{2,1,0:T(8,128)}, f32[8,64,128]{2,1,0:T(8,128)S(1)}, u32[]{:S(2)}) copy-start(f32[8,64,128]{2,1,0:T(8,128)S(1)} %collective-permute-done.1.refs_4_.refs_17_) | copy-start | bytes 786436
  29.6 16.6 %collective-permute-start.7 = (f32[280,128]{1,0:T(8,128)}, f32[280,128]{1,0:T(8,128)S(1)}, u32[]{:S(2)}, u32[]{:S(2)}) collective-permute-start(f32[280,128]{1,0:T(8,128)} %get-tuple-element.74), channel_id=1, source_target_pairs={{2,0},{4,2},{6,4},{3,1},{5,3},{7,5},{10,8},{12,10},{14,12},{11,9},... | collective-permute-start | bytes 430088 | tf_op jit(solution)/shard_map/ppermute | solution.py:616
  30.9 15.3 %collective-permute-start.8 = (f32[280,128]{1,0:T(8,128)}, f32[280,128]{1,0:T(8,128)S(1)}, u32[]{:S(2)}, u32[]{:S(2)}) collective-permute-start(f32[280,128]{1,0:T(8,128)} %get-tuple-element.71.refs_2_), channel_id=1, source_target_pairs={{0,2},{2,4},{4,6},{1,3},{3,5},{5,7},{8,10},{10,12},{12,14},{9,11},... | collective-permute-start | bytes 430088 | tf_op jit(solution)/shard_map/ppermute | solution.py:613
  46.2 1.0 copy-start.3
  64.7 1.5 %collective-permute-start.10 = (f32[16,9,2,128]{3,2,1,0:T(2,128)S(1)}, f32[16,9,2,128]{3,2,1,0:T(2,128)S(1)}, u32[]{:S(2)}, u32[]{:S(2)}) collective-permute-start(f32[16,9,2,128]{3,2,1,0:T(2,128)S(1)} %all_to_all.25.refs_1_), channel_id=1, source_target_pairs={{0,1},{1,0},{2,3},{3,2},{4,5},{5,4},{6,7},{7,6},{8,9},{9,8},{10,11... | collective-permute-start | bytes 442376 | tf_op jit(solution)/shard_map/ppermute | solution.py:610
  64.7 1.5 %collective-permute-start.11 = (f32[2,64,128]{2,1,0:T(8,128)S(1)}, f32[2,64,128]{2,1,0:T(8,128)S(1)}, u32[]{:S(2)}, u32[]{:S(2)}) collective-permute-start(f32[2,64,128]{2,1,0:T(8,128)S(1)} %get-tuple-element.79), channel_id=1, source_target_pairs={{0,1},{1,0},{2,3},{3,2},{4,5},{5,4},{6,7},{7,6},{8,9},{9,8},{10,11... | collective-permute-start | bytes 196616 | tf_op jit(solution)/shard_map/ppermute | solution.py:610
  80.9 1.5 %collective-permute-start.12 = (f32[16,9,2,128]{3,2,1,0:T(2,128)S(1)}, f32[16,9,2,128]{3,2,1,0:T(2,128)S(1)}, u32[]{:S(2)}, u32[]{:S(2)}) collective-permute-start(f32[16,9,2,128]{3,2,1,0:T(2,128)S(1)} %all_to_all.26.refs_1_), channel_id=1, source_target_pairs={{0,1},{1,0},{2,3},{3,2},{4,5},{5,4},{6,7},{7,6},{8,9},{9,8},{10,11... | collective-permute-start | bytes 442376 | tf_op jit(solution)/shard_map/ppermute | solution.py:610
  80.9 1.5 %collective-permute-start.13 = (f32[2,64,128]{2,1,0:T(8,128)S(1)}, f32[2,64,128]{2,1,0:T(8,128)S(1)}, u32[]{:S(2)}, u32[]{:S(2)}) collective-permute-start(f32[2,64,128]{2,1,0:T(8,128)S(1)} %get-tuple-element.98), channel_id=1, source_target_pairs={{0,1},{1,0},{2,3},{3,2},{4,5},{5,4},{6,7},{7,6},{8,9},{9,8},{10,11... | collective-permute-start | bytes 196616 | tf_op jit(solution)/shard_map/ppermute | solution.py:610
  96.9 1.5 %collective-permute-start.14 = (f32[16,9,2,128]{3,2,1,0:T(2,128)S(1)}, f32[16,9,2,128]{3,2,1,0:T(2,128)S(1)}, u32[]{:S(2)}, u32[]{:S(2)}) collective-permute-start(f32[16,9,2,128]{3,2,1,0:T(2,128)S(1)} %all_to_all.27.refs_1_), channel_id=1, source_target_pairs={{0,1},{1,0},{2,3},{3,2},{4,5},{5,4},{6,7},{7,6},{8,9},{9,8},{10,11... | collective-permute-start | bytes 442376 | tf_op jit(solution)/shard_map/ppermute | solution.py:610
  96.9 1.5 %collective-permute-start.15 = (f32[2,64,128]{2,1,0:T(8,128)S(1)}, f32[2,64,128]{2,1,0:T(8,128)S(1)}, u32[]{:S(2)}, u32[]{:S(2)}) collective-permute-start(f32[2,64,128]{2,1,0:T(8,128)S(1)} %get-tuple-element.113), channel_id=1, source_target_pairs={{0,1},{1,0},{2,3},{3,2},{4,5},{5,4},{6,7},{7,6},{8,9},{9,8},{10,11... | collective-permute-start | bytes 196616 | tf_op jit(solution)/shard_map/ppermute | solution.py:610

commit v5 on v4

--- a/solution.py
+++ b/solution.py
@@ -85,7 +85,7 @@
     return jnp.sum(jnp.where(match, column, 0.0), axis=0, keepdims=True)
 
 
-def prep_kernel(zdim, xdim, perm, stor, resid, d, whose, row_ref, up_ref, down_ref, acc, line):
+def prep_kernel(zdim, xdim, perm, stor, resid, d, owners, margin, whole, row_ref, up_ref, down_ref, acc, line):
     for f, field in enumerate((perm, stor, resid)):
         for pz in range(zdim):
             at = (f * zdim + pz) * 3
@@ -102,18 +102,27 @@
             total = total + eights(d[k, pz] * resid[pz])
         acc[k : k + 1, :] = jnp.sum(total, axis=0, keepdims=True)
     line[...] = jnp.zeros(line.shape, jnp.float32)
-    line[0:1, 8 : 8 + vectors] = whose[:, :vectors].astype(jnp.float32)
-    line[0:1, 16:22] = whose[:, vectors:].astype(jnp.float32)
+    line[0:1, 8 : 8 + vectors] = owners[...].astype(jnp.float32)
+    line[0:1, 16:22] = margin[...].astype(jnp.float32)
     extra = line[0:1, :]
     extra = extra + turn(extra, PERIOD, 1)
     extra = extra + turn(extra, 2 * PERIOD, 1)
     row = spread_row(acc) + extra
+    share, halves = row_ref.shape[1] - 1, row_ref.shape[2]
+    block = lax.axis_index("gy") * lax.axis_size("gz") + lax.axis_index("gz")
+    piece = whole[pl.ds(pl.multiple_of(block * share, 8), share), :]
     for p in range(row_ref.shape[0]):
-        row_ref[p] = row
-
-
-def coarse_kernel(ids, table, whole, select, known_ref, near, hot):
+        row_ref[p, share, 0:1, :] = row
+        for h in range(halves):
+            row_ref[p, 0:share, h, :] = piece[:, LANES * h : LANES * (h + 1)]
+
+
+def coarse_kernel(ids, table, select, known_ref, near, hot, whole):
     order = whole.shape[0]
+    share = table.shape[1] - 1
+    for p in range(table.shape[0]):
+        for h in range(table.shape[2]):
+            whole[share * p : share * (p + 1), LANES * h : LANES * (h + 1)] = table[p, 0:share, h, :]
     zb = ids[9]
     place_of = (zb, 1 - zb)
     lane = iota((1, LANES), 1)
@@ -122,7 +131,7 @@
     near[...] = jnp.zeros(near.shape, jnp.float32)
     for col in range(5):
         for b in range(2):
-            row = table[2 * ids[col] + place_of[b]]
+            row = table[2 * ids[col] + place_of[b], share, 0:1, :]
             near[2 * col + b : 2 * col + b + 1, :] = row
             owner = jnp.sum(jnp.where(lane8 == sub8 + 8, row, 0.0), axis=1, keepdims=True)
             at = 8 * (3 * b + col if col < 3 else 2 * col + b)
@@ -134,7 +143,7 @@
         owner = known - 1.0
         for i in range(4):
             for b in range(2):
-                row = table[2 * (4 * t + i) + place_of[b]]
+                row = table[2 * (4 * t + i) + place_of[b], share, 0:1, :]
                 mine = (lane >> 3) == 4 * i + b
                 known = jnp.where(mine, turn(row, 8 * b, 1), known)
                 owner = jnp.where(mine, turn(row, 8 * b - 8, 1), owner)
@@ -578,7 +587,7 @@
         sol_ref[at] = sol_in[p] + step * (z_in[p] + ratio * dir_in[p])
 
 
-def call(kernel, name, args, outs, scratch=(), smem=0):
+def call(kernel, name, args, outs, scratch=(), smem=0, limit=24):
     specs = [pl.BlockSpec(memory_space=pltpu.SMEM)] * smem
     specs += [pl.BlockSpec(memory_space=pltpu.VMEM)] * (len(args) - smem)
     return pl.pallas_call(
@@ -588,7 +597,7 @@
         out_specs=[pl.BlockSpec(memory_space=pltpu.VMEM)] * len(outs),
         out_shape=[jax.ShapeDtypeStruct(o, jnp.float32) for o in outs],
         scratch_shapes=[pltpu.VMEM(s, jnp.float32) for s in scratch],
-        compiler_params=pltpu.CompilerParams(vmem_limit_bytes=24 * 1024 * 1024),
+        compiler_params=pltpu.CompilerParams(vmem_limit_bytes=limit * 1024 * 1024),
     )(*args)
 
 
@@ -619,11 +628,14 @@
     others = [swap(v) for v in fields]
     d_other = swap(deflation)
     edge_rows = ((9 + vectors) * zdim, LANES)
+    share = coarse_inverse.shape[0] // (ny * nz)
+    assert share % 8 == 0
     first_row, x_up, x_down = call(
         lambda *refs: prep_kernel(zdim, xdim, *refs), "prep",
-        [*fields, deflation, jnp.concatenate([owners.reshape(1, -1), margin.reshape(1, -1)], axis=1)],
-        [(peers * nz, 1, LANES), edge_rows, edge_rows],
+        [*fields, deflation, owners.reshape(1, -1), margin.reshape(1, -1), coarse_inverse],
+        [(peers * nz, share + 1, order // LANES, LANES), edge_rows, edge_rows],
         [(PERIOD, LANES), (8, LANES)],
+        limit=60,
     )
     x_lo, x_hi = up(x_up, "gx", nx), down(x_down, "gx", nx)
     table = lax.all_to_all(first_row, ("gx", "gy", "gz"), 0, 0, tiled=True)
@@ -636,13 +648,11 @@
     )
     s_lo = up(strip_hi, "gy", ny)
     s_hi = down(strip_lo, "gy", ny)
-    coarse_inverse, _ = lax.optimization_barrier((coarse_inverse, strip_hi))
-    whole = lax.all_gather(coarse_inverse, "gx", axis=0, tiled=True)
     tiles = peers * PERIOD // LANES
     select, known, near = call(
-        coarse_kernel, "coarse", [ids, table, whole],
+        coarse_kernel, "coarse", [ids, table],
         [(10 * vectors, peers * PERIOD), (tiles, LANES), (16, LANES)],
-        [(10 * vectors, order)], smem=1,
+        [(10 * vectors, order), (order, order)], smem=1,
     )
     full, brick, one = (zdim + 3, rows, LANES), (zdim, xdim, LANES), (rows, LANES)
     mine, slots = (zdim, xdim, LANES), (peers, zdim + 1, 2, LANES)

time: 113 us -> 109 us (0.965)
  blocking collectives: 53.1 us -> 47 us
  waiting for transfers between devices: 11.3 us -> 13.9 us
  local copies, waits for them, and re-layouts: 2.56 us -> 0.98 us
  Pallas kernels: 22.9 us -> 24.1 us
    all_gather x1 -> x0, blocking collectives: 9.24 us -> none  [local(): whole = lax.all_gather(coarse_inverse, 'gx', axis=0, tiled=True)]
    all_to_all x3, blocking collectives: 34.9 us -> 38 us  [local(): got = lax.all_to_all(send, ('gx', 'gy'), 0, 0, tiled=True)]
    ppermute x2, waiting for transfers between devices: 1.93 us -> 3.52 us  [up(): return lax.ppermute(v, axis, [(i, i + 1) for i in range(count - 1)])]
    unnamed x14 -> x16, local copies, waits for them, and re-layouts: 2.56 us -> 0.98 us
    all_to_all x1, starting transfers between devices: 5.8 us -> 7.03 us  [local(): table = lax.all_to_all(first_row, ('gx', 'gy', 'gz'), 0, 0, tiled=True)]
    pallas_call x8, Pallas kernels: 22.9 us -> 24.1 us  [call(): pl.pallas_call(kernel, name=name, in_specs=specs, out_specs=[pl.BlockSpec...]
  transfers between devices with their start and end apart: 17 -> 17, of which waited for: 6 -> 9; matrix products, arithmetic and copies ran while one was open for 1% -> 0% of each run, Pallas kernels for 6% -> 7%
where the time goes in v5:
time: 109 us; the launch traced here: 108 us
  blocking collectives  47 us (43%)
  Pallas kernels  24.1 us (22%)
  starting transfers between devices  21.5 us (20%)
  waiting for transfers between devices  13.9 us (13%)
    all_to_all x3, blocking collectives, local(): got = lax.all_to_all(send, ('gx', 'gy'), 0, 0, tiled=True)  38 us
    pallas_call x8, Pallas kernels, call(): pl.pallas_call(kernel, name=name, in_specs=specs, out_specs=[pl.BlockSpec...  24.1 us
    all_to_all x1, blocking collectives, local(): got = lax.all_to_all(send, ('gx', 'gy', 'gz'), 0, 0, tiled=True)  8.98 us
    ppermute x2, starting transfers between devices, up(): return lax.ppermute(v, axis, [(i, i + 1) for i in range(count - 1)])  8.86 us
    all_to_all x1, starting transfers between devices, local(): table = lax.all_to_all(first_row, ('gx', 'gy', 'gz'), 0, 0, tiled=True)  7.03 us
    ppermute x12, waiting for transfers between devices, swap(): return lax.ppermute(v, 'gz', [(0, 1), (1, 0)])  5.24 us
    ppermute x2, waiting for transfers between devices, down(): return lax.ppermute(v, axis, [(i + 1, i) for i in range(count - 1)])  5.18 us
    ppermute x2, waiting for transfers between devices, up(): return lax.ppermute(v, axis, [(i, i + 1) for i in range(count - 1)])  3.52 us
  transfers between devices with their start and end apart: 17, of which 9 were waited for; matrix products, arithmetic and copies ran while one was open for 0% of the time, Pallas kernels for 7%

profile of v5, /device:TPU:0, one launch (start us, length us, event | category | flops | bytes accessed | tf_op | source)
XLA Modules:
  0.0 108.4 jit_solution(16404946616188138957)
XLA Ops:
  0.7 0.6 collective-permute-start.9
  1.2 3.0 %prep.1 = (f32[32,9,2,128]{3,2,1,0:T(2,128)}, f32[136,128]{1,0:T(8,128)}, f32[136,128]{1,0:T(8,128)}) custom-call(f32[8,64,128]{2,1,0:T(8,128)} %refs_13_.1, f32[8,64,128]{2,1,0:T(8,128)} %refs_14_.1, f32[8,64,128]{2,1,0:T(8,128)} %refs_15_.1, f32[8,8,64,128]{3,2,1,0:T(8,128)} %refs_4_.5, s32[1,8]{1,0:T(1,128)} %bitcast.2, s32[1,6]{1,0:T(1,128)} %bitcast.3, ...), custom_call_target="tpu_custom_call" | custom-call | tf_op jit(solution)/shard_map/prep/pallas_call | solution.py:593
  4.2 7.0 %all-to-all-start = ((f32[32,9,2,128]{3,2,1,0:T(2,128)}), f32[32,9,2,128]{3,2,1,0:T(2,128)}, u32[]{:S(2)}, u32[]{:S(2)}) async-start(f32[32,9,2,128]{3,2,1,0:T(2,128)} %get-tuple-element.67), calls=%async_computation | async-start | bytes 589824 | tf_op jit(solution)/shard_map/all_to_all | solution.py:641
  11.3 1.3 %collective-permute-start.3 = (f32[136,128]{1,0:T(8,128)}, f32[136,128]{1,0:T(8,128)S(1)}, u32[]{:S(2)}, u32[]{:S(2)}) collective-permute-start(f32[136,128]{1,0:T(8,128)} %get-tuple-element.69), channel_id=1, source_target_pairs={{8,0},{16,8},{24,16},{9,1},{17,9},{25,17},{10,2},{18,10},{26,18},{... | collective-permute-start | bytes 208904 | tf_op jit(solution)/shard_map/ppermute | solution.py:625
  12.6 0.3 collective-permute-start.2
  12.9 0.3 collective-permute-start
  13.4 5.1 %collective-permute-done.3.refs_6_.refs_7_ = f32[136,128]{1,0:T(8,128)S(1)} collective-permute-done((f32[136,128]{1,0:T(8,128)}, f32[136,128]{1,0:T(8,128)S(1)}, u32[]{:S(2)}, u32[]{:S(2)}) %collective-permute-start.3) | collective-permute-done | bytes 69664 | tf_op jit(solution)/shard_map/ppermute | solution.py:625
  18.5 4.3 %collective-permute-start.4 = (f32[136,128]{1,0:T(8,128)}, f32[136,128]{1,0:T(8,128)S(1)}, u32[]{:S(2)}, u32[]{:S(2)}) collective-permute-start(f32[136,128]{1,0:T(8,128)} %get-tuple-element.70), channel_id=1, source_target_pairs={{0,8},{8,16},{16,24},{1,9},{9,17},{17,25},{2,10},{10,18},{18,26},{... | collective-permute-start | bytes 208904 | tf_op jit(solution)/shard_map/ppermute | solution.py:622
  22.8 2.2 %collective-permute-done.4.refs_7_.refs_8_ = f32[136,128]{1,0:T(8,128)S(1)} collective-permute-done((f32[136,128]{1,0:T(8,128)}, f32[136,128]{1,0:T(8,128)S(1)}, u32[]{:S(2)}, u32[]{:S(2)}) %collective-permute-start.4) | collective-permute-done | bytes 69664 | tf_op jit(solution)/shard_map/ppermute | solution.py:622
  25.0 1.3 %collective-permute-done.5.refs_8_.refs_9_ = f32[136,128]{1,0:T(8,128)S(1)} collective-permute-done((f32[136,128]{1,0:T(8,128)S(1)}, f32[136,128]{1,0:T(8,128)S(1)}, u32[]{:S(2)}, u32[]{:S(2)}) %collective-permute-start.5) | collective-permute-done | bytes 69664 | tf_op jit(solution)/shard_map/ppermute | solution.py:619
  26.4 1.1 %collective-permute-done.6.refs_9_.refs_10_ = f32[136,128]{1,0:T(8,128)S(1)} collective-permute-done((f32[136,128]{1,0:T(8,128)S(1)}, f32[136,128]{1,0:T(8,128)S(1)}, u32[]{:S(2)}, u32[]{:S(2)}) %collective-permute-start.6) | collective-permute-done | bytes 69664 | tf_op jit(solution)/shard_map/ppermute | solution.py:619
  27.6 2.8 %pack.1 = (f32[280,128]{1,0:T(8,128)}, f32[280,128]{1,0:T(8,128)}) custom-call(f32[8,64,128]{2,1,0:T(8,128)S(1)} %copy-done.1, f32[8,64,128]{2,1,0:T(8,128)S(1)} %copy-done.2, f32[8,64,128]{2,1,0:T(8,128)S(1)} %copy-done.3, f32[8,64,128]{2,1,0:T(8,128)} %collective-permute-done.refs_3_.refs_16_, f32[8,64,128]{2,1,0:T(8,128)} %collective-permute-done.1.refs_4_.refs_17_, ...), custom_call_target="tpu_custom_call" | custom-call | tf_op jit(solution)/shard_map/pack/pallas_call | solution.py:593
  30.4 1.3 %collective-permute-start.7 = (f32[280,128]{1,0:T(8,128)}, f32[280,128]{1,0:T(8,128)S(1)}, u32[]{:S(2)}, u32[]{:S(2)}) collective-permute-start(f32[280,128]{1,0:T(8,128)} %get-tuple-element.72), channel_id=1, source_target_pairs={{2,0},{4,2},{6,4},{3,1},{5,3},{7,5},{10,8},{12,10},{14,12},{11,9},... | collective-permute-start | bytes 430088 | tf_op jit(solution)/shard_map/ppermute | solution.py:625
  31.7 4.6 %collective-permute-start.8 = (f32[280,128]{1,0:T(8,128)}, f32[280,128]{1,0:T(8,128)S(1)}, u32[]{:S(2)}, u32[]{:S(2)}) collective-permute-start(f32[280,128]{1,0:T(8,128)} %get-tuple-element.71.refs_2_), channel_id=1, source_target_pairs={{0,2},{2,4},{4,6},{1,3},{3,5},{5,7},{8,10},{10,12},{12,14},{9,11},... | collective-permute-start | bytes 430088 | tf_op jit(solution)/shard_map/ppermute | solution.py:622
  36.3 1.9 %coarse.1 = (f32[80,512]{1,0:T(8,128)S(1)}, f32[4,128]{1,0:T(4,128)S(1)}, f32[16,128]{1,0:T(8,128)S(1)}) custom-call(s32[10]{0:T(128)S(1)} %compare_select_fusion.ids.refs_0_, f32[32,9,2,128]{3,2,1,0:T(2,128)} %all-to-all-done.table), custom_call_target="tpu_custom_call" | custom-call | tf_op jit(solution)/shard_map/coarse/pallas_call | solution.py:593
  38.3 1.3 %collective-permute-done.8.refs_4_.refs_11_ = f32[280,128]{1,0:T(8,128)S(1)} collective-permute-done((f32[280,128]{1,0:T(8,128)}, f32[280,128]{1,0:T(8,128)S(1)}, u32[]{:S(2)}, u32[]{:S(2)}) %collective-permute-start.8) | collective-permute-done | bytes 143392 | tf_op jit(solution)/shard_map/ppermute | solution.py:622
  39.6 0.9 copy-done.5
  40.5 5.2 %first.1 = (f32[16,9,2,128]{3,2,1,0:T(2,128)S(1)}, f32[8,64,128]{2,1,0:T(8,128)S(1)}, f32[8,64,128]{2,1,0:T(8,128)S(1)}, f32[64,128]{1,0:T(8,128)S(1)}, f32[8,72...) custom-call(s32[10]{0:T(128)S(1)} %compare_select_fusion.ids.refs_0_, ...), custom_call_target="tpu_custom_call" | custom-call | tf_op jit(solution)/shard_map/first/pallas_call | solution.py:593
  45.8 15.2 %all_to_all.25.refs_1_ = f32[16,9,2,128]{3,2,1,0:T(2,128)S(1)} all-to-all(f32[16,9,2,128]{3,2,1,0:T(2,128)S(1)} %get-tuple-element.75), channel_id=1, replica_groups=mesh['gx'=4,'gy'=4,'gz'=2] {'gx','gy'}, dimensions={0} | all-to-all | bytes 294912 | tf_op jit(solution)/shard_map/all_to_all | solution.py:669
  61.0 0.5 collective-permute-start.11
  61.5 1.0 collective-permute-done.11.refs_3_
  62.5 3.2 %step0.1 = (f32[16,9,2,128]{3,2,1,0:T(2,128)S(1)}, f32[8,64,128]{2,1,0:T(8,128)S(1)}, f32[8,64,128]{2,1,0:T(8,128)S(1)}, f32[64,128]{1,0:T(8,128)S(1)}, f32[72,1...) custom-call(s32[10]{0:T(128)S(1)} %compare_select_fusion.ids.refs_0_, ...), custom_call_target="tpu_custom_call" | custom-call | tf_op jit(solution)/shard_map/step0/pallas_call | solution.py:593
  65.7 11.5 %all_to_all.26.refs_1_ = f32[16,9,2,128]{3,2,1,0:T(2,128)S(1)} all-to-all(f32[16,9,2,128]{3,2,1,0:T(2,128)S(1)} %get-tuple-element.94), channel_id=1, replica_groups=mesh['gx'=4,'gy'=4,'gz'=2] {'gx','gy'}, dimensions={0} | all-to-all | bytes 294912 | tf_op jit(solution)/shard_map/all_to_all | solution.py:669
  77.2 0.5 collective-permute-start.13
  77.7 1.0 collective-permute-done.13.refs_3_
  78.7 3.2 %step1.1 = (f32[16,9,2,128]{3,2,1,0:T(2,128)S(1)}, f32[8,64,128]{2,1,0:T(8,128)S(1)}, f32[8,64,128]{2,1,0:T(8,128)S(1)}, f32[64,128]{1,0:T(8,128)S(1)}, f32[72,1...) custom-call(s32[10]{0:T(128)S(1)} %compare_select_fusion.ids.refs_0_, ...), custom_call_target="tpu_custom_call" | custom-call | tf_op jit(solution)/shard_map/step1/pallas_call | solution.py:593
  81.9 11.3 %all_to_all.27.refs_1_ = f32[16,9,2,128]{3,2,1,0:T(2,128)S(1)} all-to-all(f32[16,9,2,128]{3,2,1,0:T(2,128)S(1)} %get-tuple-element.109), channel_id=1, replica_groups=mesh['gx'=4,'gy'=4,'gz'=2] {'gx','gy'}, dimensions={0} | all-to-all | bytes 294912 | tf_op jit(solution)/shard_map/all_to_all | solution.py:669
  93.2 0.5 collective-permute-start.15
  93.7 1.0 collective-permute-done.15.refs_3_
  94.7 3.7 %step2.1 = (f32[32,1,128]{2,1,0:T(1,128)S(1)}, f32[8,64,128]{2,1,0:T(8,128)S(1)}, f32[8,64,128]{2,1,0:T(8,128)S(1)}, f32[64,128]{1,0:T(8,128)}, f32[72,128]{1,0:...) custom-call(s32[10]{0:T(128)S(1)} %compare_select_fusion.ids.refs_0_, ...), custom_call_target="tpu_custom_call" | custom-call | tf_op jit(solution)/shard_map/step2/pallas_call | solution.py:593
  98.4 9.0 %all_to_all.28.refs_0_ = f32[32,1,128]{2,1,0:T(1,128)S(1)} all-to-all(f32[32,1,128]{2,1,0:T(1,128)S(1)} %get-tuple-element.124), channel_id=1, replica_groups=mesh['gx'=4,'gy'=4,'gz'=2] {'gx','gy','gz'}, dimensions={0} | all-to-all | bytes 32768 | tf_op jit(solution)/shard_map/all_to_all | solution.py:680
  107.3 1.0 last.1
  (31 shorter events, 0.5 us)
Async XLA Ops:
  0.6 26.9 %copy-start = (f32[8,8,64,128]{3,2,1,0:T(8,128)S(1)}, f32[8,8,64,128]{3,2,1,0:T(8,128)}, u32[]{:S(2)}) copy-start(f32[8,8,64,128]{3,2,1,0:T(8,128)} %refs_4_.5) | copy-start | bytes 6291460
  0.6 12.5 %copy-start.2 = (f32[8,64,128]{2,1,0:T(8,128)S(1)}, f32[8,64,128]{2,1,0:T(8,128)}, u32[]{:S(2)}) copy-start(f32[8,64,128]{2,1,0:T(8,128)} %refs_14_.1) | copy-start | bytes 786436
  0.7 12.2 %copy-start.1 = (f32[8,64,128]{2,1,0:T(8,128)S(1)}, f32[8,64,128]{2,1,0:T(8,128)}, u32[]{:S(2)}) copy-start(f32[8,64,128]{2,1,0:T(8,128)} %refs_13_.1) | copy-start | bytes 786436
  0.7 11.9 %copy-start.3 = (f32[8,64,128]{2,1,0:T(8,128)S(1)}, f32[8,64,128]{2,1,0:T(8,128)}, u32[]{:S(2)}) copy-start(f32[8,64,128]{2,1,0:T(8,128)} %refs_15_.1) | copy-start | bytes 786436
  0.7 38.9 %collective-permute-start.9 = (f32[8,8,64,128]{3,2,1,0:T(8,128)}, f32[8,8,64,128]{3,2,1,0:T(8,128)}, u32[]{:S(2)}, u32[]{:S(2)}) collective-permute-start(f32[8,8,64,128]{3,2,1,0:T(8,128)} %refs_4_.5), channel_id=1, source_target_pairs={{0,1},{1,0},{2,3},{3,2},{4,5},{5,4},{6,7},{7,6},{8,9},{9,8},{10,11... | collective-permute-start | bytes 6291464 | tf_op jit(solution)/shard_map/ppermute | solution.py:619
  4.2 32.0 %all-to-all-start = ((f32[32,9,2,128]{3,2,1,0:T(2,128)}), f32[32,9,2,128]{3,2,1,0:T(2,128)}, u32[]{:S(2)}, u32[]{:S(2)}) async-start(f32[32,9,2,128]{3,2,1,0:T(2,128)} %get-tuple-element.67), calls=%async_computation | async-start | bytes 589824 | tf_op jit(solution)/shard_map/all_to_all | solution.py:641
  11.3 24.9 %copy-start.6 = (s32[10]{0:T(128)S(1)}, s32[10]{0:T(128)}, u32[]{:S(2)}) copy-start(s32[10]{0:T(128)} %constant.23.clone) | copy-start | bytes 124
  11.3 24.9 %copy-start.7 = (s32[10]{0:T(128)S(1)}, s32[10]{0:T(128)}, u32[]{:S(2)}) copy-start(s32[10]{0:T(128)} %constant.22.clone) | copy-start | bytes 124
  11.3 7.2 %collective-permute-start.3 = (f32[136,128]{1,0:T(8,128)}, f32[136,128]{1,0:T(8,128)S(1)}, u32[]{:S(2)}, u32[]{:S(2)}) collective-permute-start(f32[136,128]{1,0:T(8,128)} %get-tuple-element.69), channel_id=1, source_target_pairs={{8,0},{16,8},{24,16},{9,1},{17,9},{25,17},{10,2},{18,10},{26,18},{... | collective-permute-start | bytes 208904 | tf_op jit(solution)/shard_map/ppermute | solution.py:625
  12.6 14.9 %collective-permute-start.2 = (f32[8,64,128]{2,1,0:T(8,128)S(1)}, f32[8,64,128]{2,1,0:T(8,128)S(1)}, u32[]{:S(2)}, u32[]{:S(2)}) collective-permute-start(f32[8,64,128]{2,1,0:T(8,128)S(1)} %copy-done.3), channel_id=1, source_target_pairs={{0,1},{1,0},{2,3},{3,2},{4,5},{5,4},{6,7},{7,6},{8,9},{9,8},{10,11... | collective-permute-start | bytes 786440 | tf_op jit(solution)/shard_map/ppermute | solution.py:619
  12.9 14.7 %collective-permute-start = (f32[8,64,128]{2,1,0:T(8,128)S(1)}, f32[8,64,128]{2,1,0:T(8,128)}, u32[]{:S(2)}, u32[]{:S(2)}) collective-permute-start(f32[8,64,128]{2,1,0:T(8,128)S(1)} %copy-done.1), channel_id=1, source_target_pairs={{0,1},{1,0},{2,3},{3,2},{4,5},{5,4},{6,7},{7,6},{8,9},{9,8},{10,11... | collective-permute-start | bytes 786440 | tf_op jit(solution)/shard_map/ppermute | solution.py:619
  13.2 14.4 %collective-permute-start.1 = (f32[8,64,128]{2,1,0:T(8,128)S(1)}, f32[8,64,128]{2,1,0:T(8,128)}, u32[]{:S(2)}, u32[]{:S(2)}) collective-permute-start(f32[8,64,128]{2,1,0:T(8,128)S(1)} %copy-done.2), channel_id=1, source_target_pairs={{0,1},{1,0},{2,3},{3,2},{4,5},{5,4},{6,7},{7,6},{8,9},{9,8},{10,11... | collective-permute-start | bytes 786440 | tf_op jit(solution)/shard_map/ppermute | solution.py:619
  18.5 6.6 %collective-permute-start.4 = (f32[136,128]{1,0:T(8,128)}, f32[136,128]{1,0:T(8,128)S(1)}, u32[]{:S(2)}, u32[]{:S(2)}) collective-permute-start(f32[136,128]{1,0:T(8,128)} %get-tuple-element.70), channel_id=1, source_target_pairs={{0,8},{8,16},{16,24},{1,9},{9,17},{17,25},{2,10},{10,18},{18,26},{... | collective-permute-start | bytes 208904 | tf_op jit(solution)/shard_map/ppermute | solution.py:622
  25.0 1.3 %collective-permute-start.5 = (f32[136,128]{1,0:T(8,128)S(1)}, f32[136,128]{1,0:T(8,128)S(1)}, u32[]{:S(2)}, u32[]{:S(2)}) collective-permute-start(f32[136,128]{1,0:T(8,128)S(1)} %collective-permute-done.3.refs_6_.refs_7_), channel_id=1, source_target_pairs={{0,1},{1,0},{2,3},{3,2},{4,5},{5,4},{6,7},{7,6},{8,9},{9,8},{10,11... | collective-permute-start | bytes 208904 | tf_op jit(solution)/shard_map/ppermute | solution.py:619
  26.3 1.3 %collective-permute-start.6 = (f32[136,128]{1,0:T(8,128)S(1)}, f32[136,128]{1,0:T(8,128)S(1)}, u32[]{:S(2)}, u32[]{:S(2)}) collective-permute-start(f32[136,128]{1,0:T(8,128)S(1)} %collective-permute-done.4.refs_7_.refs_8_), channel_id=1, source_target_pairs={{0,1},{1,0},{2,3},{3,2},{4,5},{5,4},{6,7},{7,6},{8,9},{9,8},{10,11... | collective-permute-start | bytes 208904 | tf_op jit(solution)/shard_map/ppermute | solution.py:619
  27.6 2.8 %copy-start.4 = (f32[8,64,128]{2,1,0:T(8,128)}, f32[8,64,128]{2,1,0:T(8,128)S(1)}, u32[]{:S(2)}) copy-start(f32[8,64,128]{2,1,0:T(8,128)S(1)} %collective-permute-done.2.refs_5_.refs_18_) | copy-start | bytes 786436
  30.4 7.9 %collective-permute-start.7 = (f32[280,128]{1,0:T(8,128)}, f32[280,128]{1,0:T(8,128)S(1)}, u32[]{:S(2)}, u32[]{:S(2)}) collective-permute-start(f32[280,128]{1,0:T(8,128)} %get-tuple-element.72), channel_id=1, source_target_pairs={{2,0},{4,2},{6,4},{3,1},{5,3},{7,5},{10,8},{12,10},{14,12},{11,9},... | collective-permute-start | bytes 430088 | tf_op jit(solution)/shard_map/ppermute | solution.py:625
  31.7 7.9 %collective-permute-start.8 = (f32[280,128]{1,0:T(8,128)}, f32[280,128]{1,0:T(8,128)S(1)}, u32[]{:S(2)}, u32[]{:S(2)}) collective-permute-start(f32[280,128]{1,0:T(8,128)} %get-tuple-element.71.refs_2_), channel_id=1, source_target_pairs={{0,2},{2,4},{4,6},{1,3},{3,5},{5,7},{8,10},{10,12},{12,14},{9,11},... | collective-permute-start | bytes 430088 | tf_op jit(solution)/shard_map/ppermute | solution.py:622
  39.6 1.0 copy-start.5
  61.0 1.5 %collective-permute-start.10 = (f32[16,9,2,128]{3,2,1,0:T(2,128)S(1)}, f32[16,9,2,128]{3,2,1,0:T(2,128)S(1)}, u32[]{:S(2)}, u32[]{:S(2)}) collective-permute-start(f32[16,9,2,128]{3,2,1,0:T(2,128)S(1)} %all_to_all.25.refs_1_), channel_id=1, source_target_pairs={{0,1},{1,0},{2,3},{3,2},{4,5},{5,4},{6,7},{7,6},{8,9},{9,8},{10,11... | collective-permute-start | bytes 442376 | tf_op jit(solution)/shard_map/ppermute | solution.py:619
  61.0 1.5 %collective-permute-start.11 = (f32[2,64,128]{2,1,0:T(8,128)S(1)}, f32[2,64,128]{2,1,0:T(8,128)S(1)}, u32[]{:S(2)}, u32[]{:S(2)}) collective-permute-start(f32[2,64,128]{2,1,0:T(8,128)S(1)} %get-tuple-element.77), channel_id=1, source_target_pairs={{0,1},{1,0},{2,3},{3,2},{4,5},{5,4},{6,7},{7,6},{8,9},{9,8},{10,11... | collective-permute-start | bytes 196616 | tf_op jit(solution)/shard_map/ppermute | solution.py:619
  77.2 1.5 %collective-permute-start.12 = (f32[16,9,2,128]{3,2,1,0:T(2,128)S(1)}, f32[16,9,2,128]{3,2,1,0:T(2,128)S(1)}, u32[]{:S(2)}, u32[]{:S(2)}) collective-permute-start(f32[16,9,2,128]{3,2,1,0:T(2,128)S(1)} %all_to_all.26.refs_1_), channel_id=1, source_target_pairs={{0,1},{1,0},{2,3},{3,2},{4,5},{5,4},{6,7},{7,6},{8,9},{9,8},{10,11... | collective-permute-start | bytes 442376 | tf_op jit(solution)/shard_map/ppermute | solution.py:619
  77.2 1.5 %collective-permute-start.13 = (f32[2,64,128]{2,1,0:T(8,128)S(1)}, f32[2,64,128]{2,1,0:T(8,128)S(1)}, u32[]{:S(2)}, u32[]{:S(2)}) collective-permute-start(f32[2,64,128]{2,1,0:T(8,128)S(1)} %get-tuple-element.96), channel_id=1, source_target_pairs={{0,1},{1,0},{2,3},{3,2},{4,5},{5,4},{6,7},{7,6},{8,9},{9,8},{10,11... | collective-permute-start | bytes 196616 | tf_op jit(solution)/shard_map/ppermute | solution.py:619
  93.2 1.5 %collective-permute-start.14 = (f32[16,9,2,128]{3,2,1,0:T(2,128)S(1)}, f32[16,9,2,128]{3,2,1,0:T(2,128)S(1)}, u32[]{:S(2)}, u32[]{:S(2)}) collective-permute-start(f32[16,9,2,128]{3,2,1,0:T(2,128)S(1)} %all_to_all.27.refs_1_), channel_id=1, source_target_pairs={{0,1},{1,0},{2,3},{3,2},{4,5},{5,4},{6,7},{7,6},{8,9},{9,8},{10,11... | collective-permute-start | bytes 442376 | tf_op jit(solution)/shard_map/ppermute | solution.py:619
  93.2 1.5 %collective-permute-start.15 = (f32[2,64,128]{2,1,0:T(8,128)S(1)}, f32[2,64,128]{2,1,0:T(8,128)S(1)}, u32[]{:S(2)}, u32[]{:S(2)}) collective-permute-start(f32[2,64,128]{2,1,0:T(8,128)S(1)} %get-tuple-element.111), channel_id=1, source_target_pairs={{0,1},{1,0},{2,3},{3,2},{4,5},{5,4},{6,7},{7,6},{8,9},{9,8},{10,11... | collective-permute-start | bytes 196616 | tf_op jit(solution)/shard_map/ppermute | solution.py:619
